TPU v7x, 32 devices: a whole 2x2x4 slice. The times are simulated.
32 devices in a mesh: dp: 8 (over z, core), fsdp: 4 (over y, x).
Axes of the slice: x: 2, y: 2, z: 4, core: 2. Of those that a mesh axis runs over, the one named last changes fastest.
Arguments:
- act: bfloat16 [8, 16, 512, 768], P('dp', None, 'fsdp'), may hold values from -6 to 6
- single: float32 [8, 512, 384], P('dp', 'fsdp'), may hold values from -6 to 6
- pair: bfloat16 [8, 512, 512, 128], P('dp', 'fsdp'), may hold values from -6 to 6
- segment: int32 [8, 512], P('dp', 'fsdp'), may hold values from 0 to 64, as said below
- padding: int32 [8, 512], P('dp', 'fsdp'), may hold values from 0 to 1, as said below
- cotangent: bfloat16 [8, 16, 512, 768], P('dp', None, 'fsdp'), may hold values from -6 to 6
- gain_s1: bfloat16 [384], P('fsdp'), may hold values from 0.099609375 to 1.8984375
- w_cond1: bfloat16 [384, 2304], P('fsdp'), may hold values from -0.3125 to 0.3125
- b_cond1: bfloat16 [2304], P('fsdp'), may hold values from -4 to 4
- query_key_value_gate_weight: bfloat16 [768, 3072], P('fsdp'), may hold values from -0.21875 to 0.21875
- b_q: bfloat16 [768], P('fsdp'), may hold values from -3 to 3
- gain_z: bfloat16 [128], P('fsdp'), may hold values from 0.099609375 to 1.8984375
- w_pair: bfloat16 [128, 16], P('fsdp'), may hold values from -0.5 to 0.5
- attention_output_weight: bfloat16 [768, 768], P('fsdp'), may hold values from -2.5 to 2.5
- gain_s2: bfloat16 [384], P('fsdp'), may hold values from 0.099609375 to 1.8984375
- w_cond2: bfloat16 [384, 2304], P('fsdp'), may hold values from -0.3125 to 0.3125
- b_cond2: bfloat16 [2304], P('fsdp'), may hold values from -4 to 4
- gate_up_weight: bfloat16 [768, 3072], P('fsdp'), may hold values from -0.21875 to 0.21875
- down_weight: bfloat16 [1536, 768], P('fsdp'), may hold values from -0.21875 to 0.21875
Outputs:
- block_out: bfloat16 [8, 16, 512, 768], P('dp', None, 'fsdp')
- act_grad: bfloat16 [8, 16, 512, 768], P('dp', None, 'fsdp')
- single_grad: float32 [8, 512, 384], P('dp', 'fsdp')
- pair_grad: bfloat16 [8, 512, 512, 128], P('dp', 'fsdp')
- grad_gain_s1: float32 [384], P('fsdp')
- grad_w_cond1: float32 [384, 2304], P('fsdp')
- grad_b_cond1: float32 [2304], P('fsdp')
- grad_w_qkvg: float32 [768, 3072], P('fsdp')
- grad_b_q: float32 [768], P('fsdp')
- grad_gain_z: float32 [128], P('fsdp')
- grad_w_pair: float32 [128, 16], P('fsdp')
- grad_w_o: float32 [768, 768], P('fsdp')
- grad_gain_s2: float32 [384], P('fsdp')
- grad_w_cond2: float32 [384, 2304], P('fsdp')
- grad_b_cond2: float32 [2304], P('fsdp')
- grad_w_ab: float32 [768, 3072], P('fsdp')
- grad_w_out: float32 [1536, 768], P('fsdp')
Inputs may be any that keep to these rules, and one draw needn't show every extreme that they name: Numbers start at 0 in each crop, never fall, and rise by one where a new segment begins; new segments begin only among tokens 5 * 64 to 383 of a crop, so the first 320 tokens lie in segment 0; padded tokens carry the number of the crop's last unpadded token. `padding`: 1 on a tail of 1 to 128 tokens at the end of each crop, 0 elsewhere.
All inputs are finite; a program needn't handle non-finite values.
Results may differ from a plain program's by a relative error of at most 0.02.
The roundings to bfloat16 on the way count: a program that leaves them out, or rounds other values in their place, can miss the bound.
Values may be sent and summed in bfloat16 or wider, within the bound.
No kernel may reach another device: no remote copies, remote signals or barrier semaphores. Data moves between devices by JAX's collectives and lax.ppermute only.
A program may use at most 512 MiB of HBM per device.

v0:
```python
import jax
import jax.numpy as jnp
from jax import lax
from jax.sharding import PartitionSpec as P

HEADS = 16
HEAD = 48
FF = 1536


EPS = 1e-05


def norm_stats(values):
    average = jnp.mean(values, axis=-1, keepdims=True)
    centred = values - average
    inverse = lax.rsqrt(jnp.mean(centred * centred, axis=-1, keepdims=True) + EPS)
    return (centred * inverse, inverse)


def norm_back(normed, inverse, incoming):
    return inverse * (
        incoming
        - jnp.mean(incoming, axis=-1, keepdims=True)
        - normed * jnp.mean(incoming * normed, axis=-1, keepdims=True)
    )


def sig_slope(values):
    sigma_val = jax.nn.sigmoid(values)
    return sigma_val * (1.0 - sigma_val)


def body(
    act,
    single,
    pair,
    segment,
    padding,
    cotangent,
    gain_s1,
    w_cond1,
    b_cond1,
    query_key_value_gate_weight,
    b_q,
    gain_z,
    w_pair,
    attention_output_weight,
    gain_s2,
    w_cond2,
    b_cond2,
    gate_up_weight,
    down_weight,
):
    crop_count, sample_count, row_count, model_width = act.shape
    head_count = HEADS
    head_width = HEAD
    hidden_width = FF
    inv_root = float(head_width) ** (-0.5)
    full_gs1, complete_condition_weight1, full_bc1, full_wq, full_bq, full_gz, full_wp, full_wo = (
        lax.all_gather(gain_s1, "fsdp", axis=0, tiled=True),
        lax.all_gather(w_cond1, "fsdp", axis=0, tiled=True),
        lax.all_gather(b_cond1, "fsdp", axis=0, tiled=True),
        lax.all_gather(query_key_value_gate_weight, "fsdp", axis=0, tiled=True),
        lax.all_gather(b_q, "fsdp", axis=0, tiled=True),
        lax.all_gather(gain_z, "fsdp", axis=0, tiled=True),
        lax.all_gather(w_pair, "fsdp", axis=0, tiled=True),
        lax.all_gather(attention_output_weight, "fsdp", axis=0, tiled=True),
    )
    single_n, single_inv = norm_stats(single)
    single_first = (single_n * full_gs1.astype(jnp.float32)).astype(jnp.bfloat16)
    cond_one = jnp.einsum(
        "qxw,wp->qxp", single_first, complete_condition_weight1, preferred_element_type=jnp.float32
    ) + full_bc1.astype(jnp.float32)
    scale_one = cond_one[..., :model_width]
    shift_one = cond_one[..., model_width : 2 * model_width]
    gate_one = cond_one[..., 2 * model_width :]
    act_in = act.astype(jnp.float32)
    act_n, act_inv = norm_stats(act_in)
    scale_sig1 = jax.nn.sigmoid(scale_one)[:, None]
    input_first = (scale_sig1 * act_n + shift_one[:, None]).astype(jnp.bfloat16)
    apply_projection = jnp.einsum(
        "csld,de->csle", input_first, full_wq, preferred_element_type=jnp.float32
    )
    query_low = (apply_projection[..., :model_width] + full_bq.astype(jnp.float32)).astype(
        jnp.bfloat16
    )
    keys_local = apply_projection[..., model_width : 2 * model_width].astype(jnp.bfloat16)
    values_local = apply_projection[..., 2 * model_width : 3 * model_width].astype(jnp.bfloat16)
    gate_attn = jax.nn.sigmoid(apply_projection[..., 3 * model_width :])
    tag_local = jnp.where(padding == 1, -1, segment).astype(jnp.bfloat16)
    keys_all, values_all, tag_all = (
        lax.all_gather(keys_local, "fsdp", axis=2, tiled=True),
        lax.all_gather(values_local, "fsdp", axis=2, tiled=True),
        lax.all_gather(tag_local, "fsdp", axis=1, tiled=True),
    )
    key_count = keys_all.shape[2]
    allowed = segment.astype(jnp.float32)[:, :, None] == tag_all.astype(jnp.float32)[:, None, :]
    pair_n, pair_inv = norm_stats(pair.astype(jnp.float32))
    pair_low = (pair_n * full_gz.astype(jnp.float32)).astype(jnp.bfloat16)
    pair_bias = jnp.einsum("cijp,ph->chij", pair_low, full_wp, preferred_element_type=jnp.float32)
    query_heads = query_low.reshape(crop_count, sample_count, row_count, head_count, head_width)
    keys_heads = keys_all.reshape(crop_count, sample_count, key_count, head_count, head_width)
    values_heads = values_all.reshape(crop_count, sample_count, key_count, head_count, head_width)

    def make_scores():
        raw_scores = (
            jnp.einsum(
                "csihe,csjhe->cshij", query_heads, keys_heads, preferred_element_type=jnp.float32
            )
            * inv_root
            + pair_bias[:, None]
        )
        return jnp.where(allowed[:, None, None], raw_scores, -1000000000.0)

    scores = make_scores()
    row_peak = jnp.max(scores, axis=-1, keepdims=True)
    expsum = jnp.sum(jnp.exp(scores - row_peak), axis=-1, keepdims=True)
    log_total = row_peak + jnp.log(expsum)
    attn_probs = jnp.exp(scores - log_total)
    attn_mix = jnp.einsum(
        "cshij,csjhe->csihe",
        attn_probs.astype(jnp.bfloat16),
        values_heads,
        preferred_element_type=jnp.float32,
    ).reshape(crop_count, sample_count, row_count, model_width)
    branch_input = (gate_attn * attn_mix).astype(jnp.bfloat16)
    attention_result = jnp.einsum(
        "csld,de->csle", branch_input, full_wo, preferred_element_type=jnp.float32
    )
    gate_sig1 = jax.nn.sigmoid(gate_one)[:, None]
    middle = act_in + gate_sig1 * attention_result
    full_gs2, complete_condition_weight2, full_bc2, full_wab, full_wout = (
        lax.all_gather(gain_s2, "fsdp", axis=0, tiled=True),
        lax.all_gather(w_cond2, "fsdp", axis=0, tiled=True),
        lax.all_gather(b_cond2, "fsdp", axis=0, tiled=True),
        lax.all_gather(gate_up_weight, "fsdp", axis=0, tiled=True),
        lax.all_gather(down_weight, "fsdp", axis=0, tiled=True),
    )
    single_second = (single_n * full_gs2.astype(jnp.float32)).astype(jnp.bfloat16)
    cond_two = jnp.einsum(
        "qxw,wp->qxp", single_second, complete_condition_weight2, preferred_element_type=jnp.float32
    ) + full_bc2.astype(jnp.float32)
    scale_two = cond_two[..., :model_width]
    shift_two = cond_two[..., model_width : 2 * model_width]
    gate_two = cond_two[..., 2 * model_width :]
    middle_n, middle_inv = norm_stats(middle)
    scale_sig2 = jax.nn.sigmoid(scale_two)[:, None]
    input_second = (scale_sig2 * middle_n + shift_two[:, None]).astype(jnp.bfloat16)
    gate_and_up = jnp.einsum(
        "csld,de->csle", input_second, full_wab, preferred_element_type=jnp.float32
    )
    gate_part = gate_and_up[..., :hidden_width]
    up_part = gate_and_up[..., hidden_width:]
    gate_sigma = jax.nn.sigmoid(gate_part)
    silu_val = gate_part * gate_sigma
    hidden_units = (silu_val * up_part).astype(jnp.bfloat16)
    feedforward_result = jnp.einsum(
        "cslf,fd->csld", hidden_units, full_wout, preferred_element_type=jnp.float32
    )
    gate_sig2 = jax.nn.sigmoid(gate_two)[:, None]
    result = middle + gate_sig2 * feedforward_result
    block_out = result.astype(jnp.bfloat16)
    full_gs2, complete_condition_weight2, full_bc2, full_wab, full_wout = (
        lax.all_gather(gain_s2, "fsdp", axis=0, tiled=True),
        lax.all_gather(w_cond2, "fsdp", axis=0, tiled=True),
        lax.all_gather(b_cond2, "fsdp", axis=0, tiled=True),
        lax.all_gather(gate_up_weight, "fsdp", axis=0, tiled=True),
        lax.all_gather(down_weight, "fsdp", axis=0, tiled=True),
    )
    upstream = cotangent.astype(jnp.float32)
    ffn_grad = (upstream * gate_sig2).astype(jnp.bfloat16)
    gate_two_grad = jnp.sum(upstream * feedforward_result, axis=1) * sig_slope(gate_two)
    grad_w_out = jnp.einsum(
        "cslf,csld->fd", hidden_units, ffn_grad, preferred_element_type=jnp.float32
    )
    hidden_grad = jnp.einsum(
        "csld,fd->cslf", ffn_grad, full_wout, preferred_element_type=jnp.float32
    )
    gate_up_grad = jnp.concatenate(
        [
            hidden_grad * up_part * gate_sigma * (1.0 + gate_part * (1.0 - gate_sigma)),
            hidden_grad * silu_val,
        ],
        axis=-1,
    ).astype(jnp.bfloat16)
    grad_w_ab = jnp.einsum(
        "csld,csle->de", input_second, gate_up_grad, preferred_element_type=jnp.float32
    )
    x_two_grad = jnp.einsum(
        "csle,de->csld", gate_up_grad, full_wab, preferred_element_type=jnp.float32
    )
    scale_two_grad = jnp.sum(x_two_grad * middle_n, axis=1) * sig_slope(scale_two)
    shift_two_grad = jnp.sum(x_two_grad, axis=1)
    middle_grad = upstream + norm_back(middle_n, middle_inv, x_two_grad * scale_sig2)
    cond_two_grad = jnp.concatenate([scale_two_grad, shift_two_grad, gate_two_grad], axis=-1)
    grad_b_cond2 = jnp.sum(cond_two_grad, axis=(0, 1))
    condition_second_reduced = cond_two_grad.astype(jnp.bfloat16)
    grad_w_cond2 = jnp.einsum(
        "dxm,dxp->mp", single_second, condition_second_reduced, preferred_element_type=jnp.float32
    )
    s_two_grad = jnp.einsum(
        "huq,fq->huf",
        condition_second_reduced,
        complete_condition_weight2,
        preferred_element_type=jnp.float32,
    )
    grad_gain_s2 = jnp.sum(s_two_grad * single_n, axis=(0, 1))
    single_from_two = s_two_grad * full_gs2.astype(jnp.float32)
    full_gs1, complete_condition_weight1, full_bc1, full_wq, full_bq, full_gz, full_wp, full_wo = (
        lax.all_gather(gain_s1, "fsdp", axis=0, tiled=True),
        lax.all_gather(w_cond1, "fsdp", axis=0, tiled=True),
        lax.all_gather(b_cond1, "fsdp", axis=0, tiled=True),
        lax.all_gather(query_key_value_gate_weight, "fsdp", axis=0, tiled=True),
        lax.all_gather(b_q, "fsdp", axis=0, tiled=True),
        lax.all_gather(gain_z, "fsdp", axis=0, tiled=True),
        lax.all_gather(w_pair, "fsdp", axis=0, tiled=True),
        lax.all_gather(attention_output_weight, "fsdp", axis=0, tiled=True),
    )
    out_grad = (middle_grad * gate_sig1).astype(jnp.bfloat16)
    gate_one_grad = jnp.sum(middle_grad * attention_result, axis=1) * sig_slope(gate_one)
    grad_w_o = jnp.einsum(
        "csld,csle->de", branch_input, out_grad, preferred_element_type=jnp.float32
    )
    branch_grad = jnp.einsum("csle,de->csld", out_grad, full_wo, preferred_element_type=jnp.float32)
    attn_grad = (branch_grad * gate_attn).astype(jnp.bfloat16)
    gate_proj_grad = branch_grad * attn_mix * gate_attn * (1.0 - gate_attn)
    attn_probs = jnp.exp(make_scores() - log_total)
    attn_grad_heads = attn_grad.reshape(crop_count, sample_count, row_count, head_count, head_width)
    probs_grad = jnp.einsum(
        "csihe,csjhe->cshij", attn_grad_heads, values_heads, preferred_element_type=jnp.float32
    )
    row_dot = jnp.sum(probs_grad * attn_probs, axis=-1, keepdims=True)
    score_grad = (attn_probs * (probs_grad - row_dot)).astype(jnp.bfloat16)
    query_grad = (
        jnp.einsum("cshij,csjhe->csihe", score_grad, keys_heads, preferred_element_type=jnp.float32)
        * inv_root
    )
    values_part = jnp.einsum(
        "cshij,csihe->csjhe",
        attn_probs.astype(jnp.bfloat16),
        attn_grad_heads,
        preferred_element_type=jnp.float32,
    )
    keys_part = (
        jnp.einsum(
            "cshij,csihe->csjhe", score_grad, query_heads, preferred_element_type=jnp.float32
        )
        * inv_root
    )
    keys_grad, values_grad = (
        lax.psum_scatter(
            keys_part.reshape(crop_count, sample_count, key_count, model_width).astype(
                jnp.bfloat16
            ),
            "fsdp",
            scatter_dimension=2,
            tiled=True,
        ).astype(jnp.float32),
        lax.psum_scatter(
            values_part.reshape(crop_count, sample_count, key_count, model_width).astype(
                jnp.bfloat16
            ),
            "fsdp",
            scatter_dimension=2,
            tiled=True,
        ).astype(jnp.float32),
    )
    bias_grad = jnp.sum(score_grad.astype(jnp.float32), axis=1).astype(jnp.bfloat16)
    grad_w_pair = jnp.einsum(
        "cijp,chij->ph", pair_low, bias_grad, preferred_element_type=jnp.float32
    )
    pair_low_grad = jnp.einsum(
        "chij,ph->cijp", bias_grad, full_wp, preferred_element_type=jnp.float32
    )
    grad_gain_z = jnp.sum(pair_low_grad * pair_n, axis=(0, 1, 2))
    pair_grad = norm_back(pair_n, pair_inv, pair_low_grad * full_gz.astype(jnp.float32)).astype(
        jnp.bfloat16
    )
    query_grad = query_grad.reshape(crop_count, sample_count, row_count, model_width)
    grad_b_q = jnp.sum(query_grad, axis=(0, 1, 2))
    project_grad = jnp.concatenate(
        [query_grad, keys_grad, values_grad, gate_proj_grad], axis=-1
    ).astype(jnp.bfloat16)
    grad_w_qkvg = jnp.einsum(
        "csld,csle->de", input_first, project_grad, preferred_element_type=jnp.float32
    )
    x_one_grad = jnp.einsum(
        "csle,de->csld", project_grad, full_wq, preferred_element_type=jnp.float32
    )
    scale_one_grad = jnp.sum(x_one_grad * act_n, axis=1) * sig_slope(scale_one)
    shift_one_grad = jnp.sum(x_one_grad, axis=1)
    act_grad = (middle_grad + norm_back(act_n, act_inv, x_one_grad * scale_sig1)).astype(
        jnp.bfloat16
    )
    cond_one_grad = jnp.concatenate([scale_one_grad, shift_one_grad, gate_one_grad], axis=-1)
    grad_b_cond1 = jnp.sum(cond_one_grad, axis=(0, 1))
    condition_first_reduced = cond_one_grad.astype(jnp.bfloat16)
    grad_w_cond1 = jnp.einsum(
        "dxm,dxp->mp", single_first, condition_first_reduced, preferred_element_type=jnp.float32
    )
    s_one_grad = jnp.einsum(
        "huq,fq->huf",
        condition_first_reduced,
        complete_condition_weight1,
        preferred_element_type=jnp.float32,
    )
    grad_gain_s1 = jnp.sum(s_one_grad * single_n, axis=(0, 1))
    single_grad = norm_back(
        single_n, single_inv, s_one_grad * full_gs1.astype(jnp.float32) + single_from_two
    )
    (
        shard_gs1,
        shard_wc1,
        shard_bc1,
        shard_wq,
        shard_bq,
        shard_gz,
        shard_wp,
        shard_wo,
        shard_gs2,
        shard_wc2,
        shard_bc2,
        shard_wab,
        shard_wout,
    ) = (
        lax.psum_scatter(
            grad_gain_s1.astype(jnp.bfloat16), "fsdp", scatter_dimension=0, tiled=True
        ).astype(jnp.float32),
        lax.psum_scatter(
            grad_w_cond1.astype(jnp.bfloat16), "fsdp", scatter_dimension=0, tiled=True
        ).astype(jnp.float32),
        lax.psum_scatter(
            grad_b_cond1.astype(jnp.bfloat16), "fsdp", scatter_dimension=0, tiled=True
        ).astype(jnp.float32),
        lax.psum_scatter(
            grad_w_qkvg.astype(jnp.bfloat16), "fsdp", scatter_dimension=0, tiled=True
        ).astype(jnp.float32),
        lax.psum_scatter(
            grad_b_q.astype(jnp.bfloat16), "fsdp", scatter_dimension=0, tiled=True
        ).astype(jnp.float32),
        lax.psum_scatter(
            grad_gain_z.astype(jnp.bfloat16), "fsdp", scatter_dimension=0, tiled=True
        ).astype(jnp.float32),
        lax.psum_scatter(
            grad_w_pair.astype(jnp.bfloat16), "fsdp", scatter_dimension=0, tiled=True
        ).astype(jnp.float32),
        lax.psum_scatter(
            grad_w_o.astype(jnp.bfloat16), "fsdp", scatter_dimension=0, tiled=True
        ).astype(jnp.float32),
        lax.psum_scatter(
            grad_gain_s2.astype(jnp.bfloat16), "fsdp", scatter_dimension=0, tiled=True
        ).astype(jnp.float32),
        lax.psum_scatter(
            grad_w_cond2.astype(jnp.bfloat16), "fsdp", scatter_dimension=0, tiled=True
        ).astype(jnp.float32),
        lax.psum_scatter(
            grad_b_cond2.astype(jnp.bfloat16), "fsdp", scatter_dimension=0, tiled=True
        ).astype(jnp.float32),
        lax.psum_scatter(
            grad_w_ab.astype(jnp.bfloat16), "fsdp", scatter_dimension=0, tiled=True
        ).astype(jnp.float32),
        lax.psum_scatter(
            grad_w_out.astype(jnp.bfloat16), "fsdp", scatter_dimension=0, tiled=True
        ).astype(jnp.float32),
    )
    (
        total_gs1,
        total_wc1,
        total_bc1,
        total_wq,
        total_bq,
        total_gz,
        total_wp,
        total_wo,
        total_gs2,
        total_wc2,
        total_bc2,
        total_wab,
        total_wout,
    ) = (
        lax.psum(shard_gs1.astype(jnp.bfloat16), "dp").astype(jnp.float32),
        lax.psum(shard_wc1.astype(jnp.bfloat16), "dp").astype(jnp.float32),
        lax.psum(shard_bc1.astype(jnp.bfloat16), "dp").astype(jnp.float32),
        lax.psum(shard_wq.astype(jnp.bfloat16), "dp").astype(jnp.float32),
        lax.psum(shard_bq.astype(jnp.bfloat16), "dp").astype(jnp.float32),
        lax.psum(shard_gz.astype(jnp.bfloat16), "dp").astype(jnp.float32),
        lax.psum(shard_wp.astype(jnp.bfloat16), "dp").astype(jnp.float32),
        lax.psum(shard_wo.astype(jnp.bfloat16), "dp").astype(jnp.float32),
        lax.psum(shard_gs2.astype(jnp.bfloat16), "dp").astype(jnp.float32),
        lax.psum(shard_wc2.astype(jnp.bfloat16), "dp").astype(jnp.float32),
        lax.psum(shard_bc2.astype(jnp.bfloat16), "dp").astype(jnp.float32),
        lax.psum(shard_wab.astype(jnp.bfloat16), "dp").astype(jnp.float32),
        lax.psum(shard_wout.astype(jnp.bfloat16), "dp").astype(jnp.float32),
    )
    return (
        block_out,
        act_grad,
        single_grad,
        pair_grad,
        total_gs1,
        total_wc1,
        total_bc1,
        total_wq,
        total_bq,
        total_gz,
        total_wp,
        total_wo,
        total_gs2,
        total_wc2,
        total_bc2,
        total_wab,
        total_wout,
    )


def solution(mesh):
    return jax.shard_map(
        body,
        mesh=mesh,
        in_specs=(
            P("dp", None, "fsdp", None),
            P("dp", "fsdp", None),
            P("dp", "fsdp", None, None),
            P("dp", "fsdp"),
            P("dp", "fsdp"),
            P("dp", None, "fsdp", None),
            P("fsdp"),
            P("fsdp", None),
            P("fsdp"),
            P("fsdp", None),
            P("fsdp"),
            P("fsdp"),
            P("fsdp", None),
            P("fsdp", None),
            P("fsdp"),
            P("fsdp", None),
            P("fsdp"),
            P("fsdp", None),
            P("fsdp", None),
        ),
        out_specs=(
            P("dp", None, "fsdp", None),
            P("dp", None, "fsdp", None),
            P("dp", "fsdp", None),
            P("dp", "fsdp", None, None),
            P("fsdp"),
            P("fsdp", None),
            P("fsdp"),
            P("fsdp", None),
            P("fsdp"),
            P("fsdp"),
            P("fsdp", None),
            P("fsdp", None),
            P("fsdp"),
            P("fsdp", None),
            P("fsdp"),
            P("fsdp", None),
            P("fsdp", None),
        ),
        check_vma=False,
    )
```

profile of v0, /device:TPU:0, one launch (start us, length us, event | category | flops | bytes accessed | tf_op | source)
XLA Modules:
  0.0 1310.7 jit_solution(1548851830142876294)
XLA Ops:
  20.7 17.8 %all-reduce.15 = (bf16[2304]{0:T(1024)(128)(2,1)S(1)}, bf16[384]{0:T(512)(128)(2,1)S(1)}, bf16[128]{0:T(256)(128)(2,1)S(1)}, bf16[768]{0:T(1024)(128)(2,1)S(1)},...) all-reduce(bf16[2304]{0:T(1024)(128)(2,1)S(1)} %dynamic-update-slic, ...), channel_id=1, replica_groups=mesh['dp'=8,'fsdp'=4] {'fsdp'}, use_global_device_ids=true, to_apply=%add.1 | all-reduce | flops 6272 | bytes 25088
  49.7 54.8 %all-gather.12.cloned.1.call-done = bf16[768,3072]{1,0:T(8,128)(2,1)} async-done(((bf16[192,3072]{1,0:T(8,128)(2,1)}), bf16[768,3072]{1,0:T(8,128)(2,1)}) %all-gather.12.cloned.1.call-update) | async-done | bytes 4718608 | tf_op jit(solution)/shard_map/all_gather | solution.py:64
  104.5 18.0 %fusion.162 = (bf16[1,16,128,3072]{3,2,1,0:T(8,128)(2,1)}, f32[1,16,128,3072]{3,2,1,0:T(8,128)}) fusion(bf16[768,3072]{1,0:T(8,128)(2,1)} %all-gather.12.cloned.1.call-done, bf16[1,16,128,768]{3,2,1,0:T(8,128)(2,1)S(1)} %copy-done.1, f32[128,768]{1,0:T(8,128)} %get-tuple-element.141, f32[16,128]{1,0:T(8,128)S(1)} %add_rsqrt_fusion.2, ...), kind=kOutput, calls=%fused_computation.226 | convolution fusion | flops 9679405056 | bytes 46415872 | tf_op jit(solution)/shard_map/csld,de->csle/dot_general | solution.py:82
  147.0 22.7 %copy.81 = bf16[1,128,512,128]{2,3,1,0:T(8,128)(2,1)} copy(bf16[1,128,512,128]{3,2,1,0:T(8,128)(2,1)} %param.21) | data formatting | bytes 33554432 | tf_op args[2]
  208.7 55.2 %all-gather.16.cloned.1.call-done = bf16[1,16,512,768]{3,2,1,0:T(8,128)(2,1)} async-done(((bf16[1,16,128,768]{3,2,1,0:T(8,128)(2,1)}), bf16[1,16,512,768]{3,2,1,0:T(8,128)(2,1)}) %all-gather.16.cloned.1.call-update) | async-done | bytes 12582928 | tf_op jit(solution)/shard_map/all_gather | solution.py:93
  263.8 17.2 %copy.80 = bf16[1,16,512,768]{2,3,1,0:T(8,128)(2,1)} copy(bf16[1,16,512,768]{3,2,1,0:T(8,128)(2,1)} %all-gather.16.cloned.1.call-done) | data formatting | bytes 25165824 | tf_op jit(solution)/shard_map/all_gather | solution.py:93
  281.0 31.5 %fusion.163 = (f32[16,16,128]{2,1,0:T(8,128)S(1)}, f32[16,16,128,512]{3,2,1,0:T(8,128)}) fusion(f32[16,128,512]{2,1,0:T(8,128)} %copy.84, bf16[16,128,16,48]{1,3,2,0:T(8,128)(2,1)S(1)} %bitcast.293, bf16[16,512,16,48]{1,3,2,0:T(8,128)(2,1)} %bitcast.285, pred[128,512]{1,0:T(8,128)(4,1)S(1)} %broadcast_compare_fusion), kind=kOutput, calls=%fused_computation.227 | convolution fusion | flops 1677688832 | bytes 87228416 | tf_op jit(solution)/shard_map/csihe,csjhe->cshij/dot_general | solution.py:108
  312.5 23.5 %exponential_reduce_fusion = f32[16,16,128]{2,1,0:T(8,128)S(1)} fusion(f32[16,16,128,512]{3,2,1,0:T(8,128)} %get-tuple-element.150, f32[16,16,128]{2,1,0:T(8,128)S(1)} %get-tuple-element.149), kind=kLoop, calls=%fused_computation.3 | loop fusion | flops 33521664 | bytes 67371008 | tf_op jit(solution)/shard_map/reduce_sum | solution.py:118
  336.0 52.6 %all-gather.14.cloned.1.call-done = bf16[1,16,512,768]{3,2,1,0:T(8,128)(2,1)} async-done(((bf16[1,16,128,768]{3,2,1,0:T(8,128)(2,1)}), bf16[1,16,512,768]{3,2,1,0:T(8,128)(2,1)}) %all-gather.14.cloned.1.call-update) | async-done | bytes 12582928 | tf_op jit(solution)/shard_map/all_gather | solution.py:94
  388.6 16.7 %copy.78 = bf16[1,16,512,768]{2,3,1,0:T(8,128)(2,1)} copy(bf16[1,16,512,768]{3,2,1,0:T(8,128)(2,1)} %all-gather.14.cloned.1.call-done) | data formatting | bytes 25165824 | tf_op jit(solution)/shard_map/all_gather | solution.py:94
  405.3 31.2 %fusion.22 = f32[16,16,48,128]{3,2,1,0:T(8,128)} fusion(bf16[16,512,16,48]{1,3,2,0:T(8,128)(2,1)} %bitcast.287, f32[16,16,128,512]{3,2,1,0:T(8,128)} %get-tuple-element.150, f32[16,16,128]{2,1,0:T(8,128)S(1)} %log_add_fusion), kind=kOutput, calls=%fused_computation.46 | convolution fusion | flops 1644167168 | bytes 86114304 | tf_op jit(solution)/shard_map/cshij,csjhe->csihe/dot_general | solution.py:121
  477.0 18.3 %convolution_bitcast_fusion = f32[1,16,128,3072]{3,2,1,0:T(8,128)} fusion(bf16[768,3072]{1,0:T(8,128)(2,1)} %all-gather.22.cloned.1.call-done, f32[1,16,128,768]{3,2,1,0:T(8,128)} %copy-done.6, f32[128,768]{1,0:T(8,128)S(1)} %copy-done.31, f32[16,128]{1,0:T(8,128)S(1)} %add_rsqrt_fusion.1, f32[16,128]{1,0:T(8,128)S(1)} %broadcast_multiply_fusion.7, ...), kind=kOutput, calls=%fused_computation.35 | convolution fusion | flops 9671540736 | bytes 36978688 | tf_op jit(solution)/shard_map/csld,de->csle/dot_general | solution.py:150
  495.3 21.0 %all-gather.24.cloned.1.call-done = bf16[1536,768]{1,0:T(8,128)(2,1)} async-done(((bf16[384,768]{1,0:T(8,128)(2,1)}), bf16[1536,768]{1,0:T(8,128)(2,1)}) %all-gather.24.cloned.1.call-update) | async-done | bytes 2359312 | tf_op jit(solution)/shard_map/all_gather | solution.py:138
  516.4 19.3 %fusion.60 = (bf16[16,128,1536]{2,1,0:T(8,128)(2,1)}, bf16[16,128,1536]{2,1,0:T(8,128)(2,1)}, bf16[16,128,1536]{2,1,0:T(8,128)(2,1)}) fusion(f32[1,16,128,3072]{3,2,1,0:T(8,128)} %convolution_bitcast_fusion, bf16[1536,768]{1,0:T(8,128)(2,1)} %all-gather.24.cloned.1.call-done, bf16[1,16,128,768]{3,2,1,0:T(8,128)(2,1)} %param.24, f32[128,768]{1,0:T(8,128)S(1)} %copy-done.33), kind=kOutput, calls=%fused_computation.96 | convolution fusion | flops 4883742720 | bytes 49938432 | tf_op jit(solution)/shard_map/csld,fd->cslf/dot_general | solution.py:177
  535.7 18.6 %fusion.52 = (f32[128,768]{1,0:T(8,128)}, f32[16,128]{1,0:T(8,128)S(1)}, f32[16,128,768]{2,1,0:T(8,128)}) fusion(f32[1,16,128,768]{3,2,1,0:T(8,128)} %copy-done.6, f32[16,128]{1,0:T(8,128)S(1)} %add_rsqrt_fusion.1, f32[16,128]{1,0:T(8,128)S(1)} %broadcast_multiply_fusion.7, f32[128,768]{1,0:T(8,128)S(1)} %copy-done.20, ...), kind=kOutput, calls=%fused_computation.78 | convolution fusion | flops 9699751936 | bytes 30695424 | tf_op jit(solution)/shard_map/csle,de->csld/dot_general | solution.py:190
  558.9 16.9 %fusion.45 = (f32[128,768]{1,0:T(8,128)}, bf16[1,16,128,768]{3,2,1,0:T(8,128)(2,1)}, f32[128,768]{1,0:T(8,128)}, f32[1,16,128,768]{3,2,1,0:T(8,128)}) fusion(bf16[1,16,128,768]{3,2,1,0:T(8,128)(2,1)} %param.24, f32[1,16,128,768]{3,2,1,0:T(8,128)} %copy-done.6, f32[128,768]{1,0:T(8,128)S(1)} %copy-done.33, f32[16,128,768]{2,1,0:T(8,128)} %get-tuple-element.151, ...), kind=kOutput, calls=%fused_computation.66 | convolution fusion | flops 4856807424 | bytes 41713664 | tf_op jit(solution)/shard_map/cslf,fd->csld/dot_general | solution.py:158
  590.6 28.4 %fusion.32 = bf16[16,16,48,512]{3,2,1,0:T(8,128)(2,1)} fusion(bf16[16,128,16,48]{1,3,2,0:T(8,128)(2,1)S(1)} %bitcast.295, f32[16,16,128,512]{3,2,1,0:T(8,128)} %get-tuple-element.150, f32[16,16,128]{2,1,0:T(8,128)S(1)} %log_add_fusion), kind=kOutput, calls=%fused_computation.55 | convolution fusion | flops 1650458624 | bytes 82968576 | tf_op jit(solution)/shard_map/cshij,csihe->csjhe/dot_general | solution.py:239
  635.7 50.7 %multiply_reduce_fusion = (f32[16,16,128]{2,1,0:T(8,128)S(1)}, f32[16,16,128,512]{3,2,1,0:T(8,128)}) fusion(f32[16,16,128,512]{3,2,1,0:T(8,128)} %get-tuple-element.150, f32[16,16,128]{2,1,0:T(8,128)S(1)} %log_add_fusion, bf16[16,128,16,48]{1,3,2,0:T(8,128)(2,1)S(1)} %bitcast.296, bf16[16,512,16,48]{1,3,2,0:T(8,128)(2,1)} %bitcast.288), kind=kOutput, calls=%fused_computation.1 | convolution fusion | flops 1660911616 | bytes 150208512 | tf_op jit(solution)/shard_map/csihe,csjhe->cshij/dot_general | solution.py:230
  686.4 57.8 %fusion.153 = (bf16[16,128,512]{2,1,0:T(8,128)(2,1)}, bf16[16,16,128,512]{3,2,1,0:T(8,128)(2,1)}) fusion(f32[16,16,128,512]{3,2,1,0:T(8,128)} %get-tuple-element.154, f32[16,16,128]{2,1,0:T(8,128)S(1)} %get-tuple-element.153, f32[16,16,128,512]{3,2,1,0:T(8,128)} %get-tuple-element.150, f32[16,16,128]{2,1,0:T(8,128)S(1)} %log_add_fusion), kind=kLoop, calls=%fused_computation.221 | loop fusion | flops 82837504 | bytes 170131456 | tf_op jit(solution)/shard_map/reduce_sum | solution.py:269
  760.4 16.7 %copy.87 = bf16[1,16,512,768]{3,2,1,0:T(8,128)(2,1)} copy(bf16[1,16,512,768]{2,3,1,0:T(8,128)(2,1)} %bitcast.292) | data formatting | bytes 25165824 | tf_op jit(solution)/shard_map/convert_element_type | solution.py:253
  813.3 20.0 %bitcast_convert_fusion = bf16[768,3072]{1,0:T(8,128)(2,1)} fusion(bf16[16,128,1536]{2,1,0:T(8,128)(2,1)} %get-tuple-element.123, bf16[16,128,1536]{2,1,0:T(8,128)(2,1)} %get-tuple-element.122, f32[1,16,128,768]{3,2,1,0:T(8,128)} %copy-done.6, f32[128,768]{1,0:T(8,128)S(1)} %copy-done.32, f32[16,128]{1,0:T(8,128)S(1)} %copy-done.54, ...), kind=kOutput, calls=%fused_computation.43 | convolution fusion | flops 9699065856 | bytes 24395776 | tf_op jit(solution)/shard_map/csld,csle->de/dot_general | solution.py:187
  833.6 23.5 %bitcast_convert_fusion.2 = (bf16[1,16,128,16,48]{2,4,3,1,0:T(8,128)(2,1)}, f32[16,16,48,128]{3,2,1,0:T(8,128)}) fusion(bf16[16,512,16,48]{1,3,2,0:T(8,128)(2,1)} %bitcast.286, bf16[16,16,128,512]{3,2,1,0:T(8,128)(2,1)} %get-tuple-element.107), kind=kOutput, calls=%fused_computation.76 | convolution fusion | flops 1613758464 | bytes 55574528 | tf_op jit(solution)/shard_map/cshij,csjhe->csihe/dot_general | solution.py:236
  861.9 36.6 %reduce-scatter.12.cloned.1.call-done = bf16[1,16,128,768]{3,2,1,0:T(8,128)(2,1)} async-done(((bf16[1,16,512,768]{3,2,1,0:T(8,128)(2,1)}), bf16[1,16,128,768]{3,2,1,0:T(8,128)(2,1)}) %reduce-scatter.12.cloned.1.call-update) | async-done | bytes 3145744 | tf_op jit(solution)/shard_map/reduce_scatter | solution.py:252
  923.0 19.5 %bitcast_convert_fusion.1 = bf16[768,3072]{1,0:T(8,128)(2,1)} fusion(bf16[16,128,768]{2,1,0:T(8,128)(2,1)} %get-tuple-element.125, bf16[16,128,768]{2,1,0:T(8,128)(2,1)} %bitcast.305, bf16[16,128,768]{2,1,0:T(8,128)(2,1)} %bitcast.307, bf16[16,128,768]{2,1,0:T(8,128)(2,1)} %copy.90, bf16[1,16,128,768]{3,2,1,0:T(8,128)(2,1)S(1)} %copy-done.3, ...), kind=kOutput, calls=%fused_computation.44 | convolution fusion | flops 9725804544 | bytes 21250048 | tf_op jit(solution)/shard_map/csld,csle->de/dot_general | solution.py:285
  950.7 24.7 %fusion.12 = (bf16[128]{0:T(256)(128)(2,1)}, f32[128,512]{1,0:T(8,128)}, f32[128,512,128]{1,2,0:T(8,128)}) fusion(bf16[1,128,512,128]{2,3,1,0:T(8,128)(2,1)} %copy.81, f32[128,512]{1,0:T(8,128)} %copy-done.24, f32[128,512]{1,0:T(8,128)} %copy-done.16, f32[128]{0:T(128)} %copy-done.57, bf16[128,16,1]{0,1,2:T(8,128)(2,1)} %copy-done.56, ...), kind=kOutput, calls=%fused_computation.19 | convolution fusion | flops 335478656 | bytes 53220096 | tf_op jit(solution)/shard_map/chij,ph->cijp/dot_general | solution.py:273
  991.9 25.2 %fusion.11 = bf16[1,128,512,128]{2,3,1,0:T(8,128)(2,1)} fusion(bf16[1,128,512,128]{2,3,1,0:T(8,128)(2,1)} %copy.81, f32[128,512,128]{1,2,0:T(8,128)} %get-tuple-element.159, f32[128,512]{1,0:T(8,128)S(1)} %broadcast_multiply_fusion, f32[128,512]{1,0:T(8,128)S(1)} %broadcast_multiply_fusion.1, f32[128]{0:T(128)S(1)} %copy-done.59, ...), kind=kLoop, calls=%fused_computation.18 | loop fusion | flops 75497472 | bytes 68157952 | tf_op jit(solution)/shard_map/convert_element_type | solution.py:277
  1017.0 21.0 %copy.98 = bf16[1,128,512,128]{3,2,1,0:T(8,128)(2,1)} copy(bf16[1,128,512,128]{2,3,1,0:T(8,128)(2,1)} %fusion.11) | data formatting | bytes 33554432
  1048.0 45.6 %reduce-scatter.24.cloned.1.call-done = bf16[192,3072]{1,0:T(8,128)(2,1)} async-done(((bf16[768,3072]{1,0:T(8,128)(2,1)}), bf16[192,3072]{1,0:T(8,128)(2,1)}) %reduce-scatter.24.cloned.1.call-update) | async-done | bytes 1179664 | tf_op jit(solution)/shard_map/reduce_scatter | solution.py:360
  1093.6 36.2 %reduce-scatter.16.cloned.1.call-done = bf16[96,2304]{1,0:T(8,128)(2,1)} async-done(((bf16[384,2304]{1,0:T(8,128)(2,1)}), bf16[96,2304]{1,0:T(8,128)(2,1)}) %reduce-scatter.16.cloned.1.call-update) | async-done | bytes 442384 | tf_op jit(solution)/shard_map/reduce_scatter | solution.py:330
  1129.9 60.2 %reduce-scatter.18.cloned.1.call-done = bf16[192,3072]{1,0:T(8,128)(2,1)} async-done(((bf16[768,3072]{1,0:T(8,128)(2,1)}), bf16[192,3072]{1,0:T(8,128)(2,1)}) %reduce-scatter.18.cloned.1.call-update) | async-done | bytes 1179664 | tf_op jit(solution)/shard_map/reduce_scatter | solution.py:336
  1218.0 27.6 %all-reduce.12 = (bf16[96]{0:T(256)(128)(2,1)}, bf16[576]{0:T(1024)(128)(2,1)}, bf16[192]{0:T(256)(128)(2,1)}, bf16[32]{0:T(256)(128)(2,1)}, bf16[32,16]{0,1:T(8...) all-reduce(bf16[96]{0:T(256)(128)(2,1)} %dynamic-slice.7, ...), channel_id=1, replica_groups=mesh['dp'=8,'fsdp'=4] {'dp'}, use_global_device_ids=true, to_apply=%region_30.31 | all-reduce | flops 2080 | bytes 8320 | tf_op jit(solution)/shard_map/psum | solution.py:382
  1265.4 25.3 %all-reduce.18.cloned.1.call-done = (bf16[96,2304]{1,0:T(8,128)(2,1)}, bf16[192,3072]{1,0:T(8,128)(2,1)}, bf16[192,768]{1,0:T(8,128)(2,1)}, bf16[96,2304]{1,0:T(...) async-done(((bf16[96,2304]{1,0:T(8,128)(2,1)}, bf16[192,3072]{1,0:T(8,128)(2,1)}, bf16[192,768]{1,0:T(8,128)(2,1)}, bf16[96,2304]{1,0:T(8,128)(2,1)}, ...) | async-done | bytes 4128784 | tf_op jit(solution)/shard_map/psum | solution.py:383
  (285 shorter events, 335.5 us)
Async XLA Ops:
  7.2 38.3 %all-gather.10.cloned.1.call-start = ((), (), s32[]{:S(2)}) async-start(), calls=%async_computation.9 | async-start | bytes 2211840 | tf_op jit(solution)/shard_map/all_gather | solution.py:62
  7.9 96.5 %all-gather.12.cloned.1.call-start = ((), (), s32[]{:S(2)}) async-start(), calls=%async_computation.10 | async-start | bytes 5898240 | tf_op jit(solution)/shard_map/all_gather | solution.py:64
  8.7 186.7 %all-gather.20.cloned.1.call-start = ((), (), s32[]{:S(2)}) async-start(), calls=%async_computation.14 | async-start | bytes 2211840 | tf_op jit(solution)/shard_map/all_gather | solution.py:135
  9.4 254.4 %all-gather.16.cloned.1.call-start = ((), (), s32[]{:S(2)}) async-start(), calls=%async_computation.12 | async-start | bytes 15728640 | tf_op jit(solution)/shard_map/all_gather | solution.py:93
  14.4 181.0 %copy-start.43 = (f32[128]{0:T(128)}, f32[128]{0:T(128)S(1)}, u32[]{:S(2)}) copy-start(f32[128]{0:T(128)S(1)} %broadcast_multiply_fusion.11) | copy-start | bytes 1540
  15.6 179.9 %copy-start.50 = (f32[128]{0:T(128)}, f32[128]{0:T(128)S(1)}, u32[]{:S(2)}) copy-start(f32[128]{0:T(128)S(1)} %add_rsqrt_fusion.3) | copy-start | bytes 1540
  38.6 84.0 %copy-start.46 = (f32[384]{0:T(512)}, f32[384]{0:T(512)S(1)}, u32[]{:S(2)}) copy-start(f32[384]{0:T(512)S(1)} %convert_element_type.266) | copy-start | bytes 4612
  41.0 81.6 %copy-start.37 = (f32[16,128]{1,0:T(8,128)}, f32[16,128]{1,0:T(8,128)S(1)}, u32[]{:S(2)}) copy-start(f32[16,128]{1,0:T(8,128)S(1)} %broadcast_multiply_fusion.8) | copy-start | bytes 24580
  42.1 80.5 %copy-start.39 = (f32[16,128]{1,0:T(8,128)}, f32[16,128]{1,0:T(8,128)S(1)}, u32[]{:S(2)}) copy-start(f32[16,128]{1,0:T(8,128)S(1)} %add_rsqrt_fusion.2) | copy-start | bytes 24580
  128.8 259.8 %all-gather.14.cloned.1.call-start = ((), (), s32[]{:S(2)}) async-start(), calls=%async_computation.11 | async-start | bytes 15728640 | tf_op jit(solution)/shard_map/all_gather | solution.py:94
  129.4 327.7 %all-gather.18.cloned.1.call-start = ((), (), s32[]{:S(2)}) async-start(), calls=%async_computation.13 | async-start | bytes 1474560 | tf_op jit(solution)/shard_map/all_gather | solution.py:68
  130.0 347.1 %all-gather.22.cloned.1.call-start = ((), (), s32[]{:S(2)}) async-start(), calls=%async_computation.15 | async-start | bytes 5898240 | tf_op jit(solution)/shard_map/all_gather | solution.py:137
  130.7 385.7 %all-gather.24.cloned.1.call-start = ((), (), s32[]{:S(2)}) async-start(), calls=%async_computation.16 | async-start | bytes 2949120 | tf_op jit(solution)/shard_map/all_gather | solution.py:138
  131.5 730.4 %reduce-scatter.14.cloned.1.call-start = ((), (), s32[]{:S(2)}) async-start(), calls=%async_computation.18 | async-start | bytes 15728640 | tf_op jit(solution)/shard_map/reduce_scatter | solution.py:260
  139.4 46.0 %copy-start.57 = (f32[128]{0:T(128)}, f32[128]{0:T(128)S(1)}, u32[]{:S(2)}) copy-start(f32[128]{0:T(128)S(1)} %convert_element_type.277) | copy-start | bytes 1540
  139.5 56.0 %copy-start.48 = (f32[384]{0:T(512)}, f32[384]{0:T(512)S(1)}, u32[]{:S(2)}) copy-start(f32[384]{0:T(512)S(1)} %convert_element_type.281) | copy-start | bytes 4612
  208.6 72.3 %copy-start.4 = (bf16[1,16,128,768]{2,3,1,0:T(8,128)(2,1)}, bf16[1,16,128,768]{2,3,1,0:T(8,128)(2,1)S(1)}, u32[]{:S(2)}) copy-start(bf16[1,16,128,768]{2,3,1,0:T(8,128)(2,1)S(1)} %copy.79) | copy-start | bytes 9437188
  465.2 93.7 %copy-start.41 = (f32[16,128]{1,0:T(8,128)}, f32[16,128]{1,0:T(8,128)S(1)}, u32[]{:S(2)}) copy-start(f32[16,128]{1,0:T(8,128)S(1)} %broadcast_multiply_fusion.7) | copy-start | bytes 24580
  468.6 90.3 %copy-start.53 = (f32[16,128]{1,0:T(8,128)}, f32[16,128]{1,0:T(8,128)S(1)}, u32[]{:S(2)}) copy-start(f32[16,128]{1,0:T(8,128)S(1)} %add_rsqrt_fusion.1) | copy-start | bytes 24580
  635.7 262.8 %reduce-scatter.12.cloned.1.call-start = ((), (), s32[]{:S(2)}) async-start(), calls=%async_computation.17 | async-start | bytes 15728640 | tf_op jit(solution)/shard_map/reduce_scatter | solution.py:252
  686.4 57.8 %copy-start.5 = (bf16[1,16,128,768]{2,3,1,0:T(8,128)(2,1)S(1)}, bf16[1,16,128,768]{2,3,1,0:T(8,128)(2,1)}, u32[]{:S(2)}) copy-start(bf16[1,16,128,768]{2,3,1,0:T(8,128)(2,1)} %copy-done.4) | copy-start | bytes 9437188
  777.1 262.8 %reduce-scatter.28.cloned.1.call-start = ((), (), s32[]{:S(2)}) async-start(), calls=%async_computation.25 | async-start | bytes 40960
  789.5 258.5 %reduce-scatter.20.cloned.1.call-start = ((), (), s32[]{:S(2)}) async-start(), calls=%async_computation.21 | async-start | bytes 1474560 | tf_op jit(solution)/shard_map/reduce_scatter | solution.py:348
  796.8 251.2 %reduce-scatter.22.cloned.1.call-start = ((), (), s32[]{:S(2)}) async-start(), calls=%async_computation.22 | async-start | bytes 2211840 | tf_op jit(solution)/shard_map/reduce_scatter | solution.py:354
  803.3 244.7 %reduce-scatter.26.cloned.1.call-start = ((), (), s32[]{:S(2)}) async-start(), calls=%async_computation.24 | async-start | bytes 2949120 | tf_op jit(solution)/shard_map/reduce_scatter | solution.py:363
  813.0 280.6 %reduce-scatter.24.cloned.1.call-start = ((), (), s32[]{:S(2)}) async-start(), calls=%async_computation.23 | async-start | bytes 5898240 | tf_op jit(solution)/shard_map/reduce_scatter | solution.py:360
  833.3 296.6 %reduce-scatter.16.cloned.1.call-start = ((), (), s32[]{:S(2)}) async-start(), calls=%async_computation.19 | async-start | bytes 2211840 | tf_op jit(solution)/shard_map/reduce_scatter | solution.py:330
  857.1 41.4 %copy-start.3 = (bf16[1,16,128,768]{3,2,1,0:T(8,128)(2,1)S(1)}, bf16[1,16,128,768]{3,2,1,0:T(8,128)(2,1)}, u32[]{:S(2)}) copy-start(bf16[1,16,128,768]{3,2,1,0:T(8,128)(2,1)} %param.19) | copy-start | bytes 9437188
  857.1 41.4 %copy-start.38 = (f32[16,128]{1,0:T(8,128)S(1)}, f32[16,128]{1,0:T(8,128)}, u32[]{:S(2)}) copy-start(f32[16,128]{1,0:T(8,128)} %copy-done.37) | copy-start | bytes 24580
  857.1 41.4 %copy-start.40 = (f32[16,128]{1,0:T(8,128)S(1)}, f32[16,128]{1,0:T(8,128)}, u32[]{:S(2)}) copy-start(f32[16,128]{1,0:T(8,128)} %copy-done.39) | copy-start | bytes 24580
  922.9 267.2 %reduce-scatter.18.cloned.1.call-start = ((), (), s32[]{:S(2)}) async-start(), calls=%async_computation.20 | async-start | bytes 5898240 | tf_op jit(solution)/shard_map/reduce_scatter | solution.py:336
  942.5 348.3 %all-reduce.18.cloned.1.call-start = ((), (), s32[]{:S(2)}) async-start(), calls=%async_computation.26 | async-start | bytes 8257536 | tf_op jit(solution)/shard_map/psum | solution.py:383
  (50 other events, 515.6 us)
Sparse Core Ops, SparseCore 0:
  9.9 35.6 all-gather.9
  47.4 57.0 all-gather.11
  106.3 32.6 all-gather.19
  141.3 122.5 all-gather.15
  266.1 122.5 all-gather.13
  390.3 27.7 all-gather.17
  419.9 57.0 all-gather.21
  478.9 37.4 all-gather.23
  635.8 120.7 reduce-scatter.13
  777.2 121.1 reduce-scatter.11
  901.2 23.5 reduce-scatter.27
  927.8 28.5 reduce-scatter.19
  959.8 32.4 reduce-scatter.21
  996.0 37.3 reduce-scatter.25
  1036.5 57.0 reduce-scatter.23
  1097.4 32.4 reduce-scatter.15
  1133.0 57.0 reduce-scatter.17
  1193.1 97.6 all-reduce.17
where the time goes:
time: 1320 us; the launch traced here: 1310 us
  matrix products  419 us (32%)
  waiting for transfers between devices  404 us (31%)
  other arithmetic  209 us (16%)
  local copies, waits for them, and re-layouts  179 us (14%)
  blocking collectives  77.2 us (6%)
  between operations  20.7 us (2%)
    unnamed x152, local copies, waits for them, and re-layouts  74.2 us
    reduce_scatter x1, waiting for transfers between devices, body(): lax.psum_scatter(grad_w_qkvg.astype(jnp.bfloat16), 'fsdp', scatter_dimens...  60.2 us
    reduce_sum x1, other arithmetic, body(): jnp.sum(score_grad.astype(jnp.float32), axis=1).astype(jnp.bfloat16)  57.8 us
    all_gather x1, waiting for transfers between devices, body(): lax.all_gather(keys_local, 'fsdp', axis=2, tiled=True)  55.2 us
    all_gather x1, waiting for transfers between devices, body(): lax.all_gather(query_key_value_gate_weight, 'fsdp', axis=0, tiled=True)  54.8 us
    all_gather x1, waiting for transfers between devices, body(): lax.all_gather(values_local, 'fsdp', axis=2, tiled=True)  52.6 us
    dot_general x1, matrix products, body(): jnp.einsum('csihe,csjhe->cshij', attn_grad_heads, values_heads, preferred...  50.7 us
    reduce_scatter x1, waiting for transfers between devices, body(): lax.psum_scatter(grad_w_ab.astype(jnp.bfloat16), 'fsdp', scatter_dimensio...  45.6 us
  transfers between devices with their start and end apart: 18, of which 11 were waited for; matrix products, arithmetic and copies ran while one was open for 50% of the time, Pallas kernels for 0%

commit v1 on v0

v1 whole, which is shorter than its diff:
```python
import functools

import jax
import jax.numpy as jnp
from jax import lax
from jax.experimental import pallas as pl
from jax.experimental.pallas import tpu as pltpu
from jax.sharding import PartitionSpec as P

HEADS = 16
HEAD = 48
FF = 1536
EPS = 1e-05
LOG2E = 1.4426950408889634
NEG = -1000000000.0
f32 = jnp.float32
bf16 = jnp.bfloat16
NT = (((1,), (1,)), ((), ()))
NN = (((1,), (0,)), ((), ()))
TN = (((0,), (0,)), ((), ()))


def norm_stats(values):
    average = jnp.mean(values, axis=-1, keepdims=True)
    centred = values - average
    inverse = lax.rsqrt(jnp.mean(centred * centred, axis=-1, keepdims=True) + EPS)
    return (centred * inverse, inverse)


def norm_back(normed, inverse, incoming):
    return inverse * (
        incoming
        - jnp.mean(incoming, axis=-1, keepdims=True)
        - normed * jnp.mean(incoming * normed, axis=-1, keepdims=True)
    )


def sig_slope(values):
    sigma_val = jax.nn.sigmoid(values)
    return sigma_val * (1.0 - sigma_val)


def dg(a, b, dims):
    return lax.dot_general(a, b, dims, preferred_element_type=f32)


def head_window(h, D):
    tile = jnp.minimum((h * HEAD) // 128, D // 128 - 2)
    return pl.multiple_of(tile * 128, 128), h * HEAD - tile * 128


def masked_bias(F, ids, seg_ref, tag_ref, parts, bm):
    for p in range(F):
        R = parts[p].shape[1]
        row = pl.multiple_of(ids[F + 2 + p] * R, 16)
        bm[pl.ds(row, R), :] = jnp.where(
            seg_ref[pl.ds(row, R), :] == tag_ref[...], parts[p][0].astype(f32) * LOG2E, -jnp.inf
        )


def head_scores(q, k, bm):
    s = dg(q, k, NT)
    return jnp.where(bm > -jnp.inf, s * (HEAD**-0.5 * LOG2E) + bm, NEG * LOG2E)


def attn_fwd_kernel(F, RB, ids, seg_ref, tag_ref, q_ref, k_ref, v_ref, *refs):
    parts = refs[:F]
    o_ref, lse_ref, bm = refs[F:]
    Sl, T, D = q_ref.shape
    h = pl.program_id(0)

    @pl.when(h == 0)
    def _():
        o_ref[...] = jnp.zeros_like(o_ref)
        lse_ref[...] = jnp.zeros_like(lse_ref)

    start, off = head_window(h, D)
    masked_bias(F, ids, seg_ref, tag_ref, parts, bm)
    lane = lax.broadcasted_iota(jnp.int32, (1, 256), 1)
    mine = (lane >= off) & (lane < off + HEAD)
    column = lax.broadcasted_iota(jnp.int32, (1, 128), 1) == h
    win = pl.ds(start, 256)

    def sample(s, _):
        kw = k_ref[s, :, win]
        vw = v_ref[s, :, win]
        vw = jnp.where(mine, vw, jnp.zeros_like(vw))
        for r in range(0, T, RB):
            rows = pl.ds(r, RB)
            qw = q_ref[s, rows, win]
            sc = head_scores(jnp.where(mine, qw, jnp.zeros_like(qw)), kw, bm[rows, :])
            m = jnp.max(sc, axis=-1, keepdims=True)
            p = jnp.exp2(sc - m)
            l = jnp.sum(p, axis=-1, keepdims=True)
            o_ref[s, rows, win] += dg(p.astype(bf16), vw, NN) * (1.0 / l)
            lse_ref[s, rows, :] = jnp.where(column, m + jnp.log2(l), lse_ref[s, rows, :])
        return 0

    lax.fori_loop(0, Sl, sample, 0)


def resident(a, single=True):
    return pl.BlockSpec(
        a.shape, lambda h, s: (0,) * len(a.shape), pipeline_mode=pl.Buffered(1) if single else None
    )


def attn_fwd(ids, seg, tag, q, k, v, parts):
    Sl, T, D = q.shape
    F = len(parts)
    H, R = parts[0].shape[:2]
    part = pl.BlockSpec((1, R, T), lambda h, s: (h, 0, 0))
    outs = [jax.ShapeDtypeStruct((Sl, T, D), f32), jax.ShapeDtypeStruct((Sl, T, 128), f32)]
    return pl.pallas_call(
        functools.partial(attn_fwd_kernel, F, min(T, 256)),
        grid_spec=pltpu.PrefetchScalarGridSpec(
            num_scalar_prefetch=1,
            grid=(H,),
            in_specs=[resident(x) for x in (seg, tag, q, k, v)] + [part] * F,
            out_specs=[resident(x) for x in outs],
            scratch_shapes=[pltpu.VMEM((T, T), f32)],
        ),
        out_shape=outs,
        compiler_params=pltpu.CompilerParams(
            dimension_semantics=("arbitrary",), vmem_limit_bytes=60 << 20
        ),
        cost_estimate=cost(Sl * H * T * T * 1024, Sl * T * D * 10 + H * T * T * 2, Sl * H * T * T),
        name="attn_fwd",
    )(ids, seg, tag, q, k, v, *parts)


def attn_bwd_kernel(F, RB, ids, seg_ref, tag_ref, q_ref, k_ref, v_ref, do_ref, lse_ref, *refs):
    parts = refs[:F]
    dq_ref, dk_ref, dv_ref = refs[F : F + 3]
    db_refs = refs[F + 3 : F + 3 + F]
    bm, dbacc, pb, dsb, qt, dot, dkt, dvt = refs[F + 3 + F :]
    Sl, T, D = q_ref.shape
    h = pl.program_id(0)

    @pl.when(h == 0)
    def _():
        dq_ref[...] = jnp.zeros_like(dq_ref)

        def turn(s, _):
            qt[s] = q_ref[s].T
            dot[s] = do_ref[s].T
            return 0

        lax.fori_loop(0, Sl, turn, 0)

    start, off = head_window(h, D)
    masked_bias(F, ids, seg_ref, tag_ref, parts, bm)
    lane = lax.broadcasted_iota(jnp.int32, (1, 256), 1)
    mine = (lane >= off) & (lane < off + HEAD)
    column = lax.broadcasted_iota(jnp.int32, (1, 128), 1) == h
    win = pl.ds(start, 256)
    here = pl.ds(pl.multiple_of(h * HEAD, 16), HEAD)
    root = HEAD**-0.5
    dbacc[...] = jnp.zeros_like(dbacc)

    def sample(s, _):
        kw = k_ref[s, :, win]
        vw = v_ref[s, :, win]
        km = jnp.where(mine, kw, jnp.zeros_like(kw))
        for r in range(0, T, RB):
            rows = pl.ds(r, RB)
            qw = q_ref[s, rows, win]
            gw = do_ref[s, rows, win]
            sc = head_scores(jnp.where(mine, qw, jnp.zeros_like(qw)), kw, bm[rows, :])
            lse = jnp.sum(
                jnp.where(column, lse_ref[s, rows, :], 0.0), axis=-1, keepdims=True
            )
            p = jnp.exp2(sc - lse)
            dp = dg(jnp.where(mine, gw, jnp.zeros_like(gw)), vw, NT)
            delta = jnp.sum(p * dp, axis=-1, keepdims=True)
            ds = (p * (dp - delta)).astype(bf16)
            pb[rows, :] = p.astype(bf16)
            dsb[rows, :] = ds
            dbacc[rows, :] += ds.astype(f32)
            dq_ref[s, rows, win] += dg(ds, km, NN) * root
        dvt[s, here, :] = dg(dot[s, here, :], pb[...], NN).astype(bf16)
        dkt[s, here, :] = (dg(qt[s, here, :], dsb[...], NN) * root).astype(bf16)
        return 0

    lax.fori_loop(0, Sl, sample, 0)
    for p in range(F):
        R = db_refs[p].shape[1]
        row = pl.multiple_of(ids[F + 2 + p] * R, 16)
        db_refs[p][0] = dbacc[pl.ds(row, R), :].astype(bf16)

    @pl.when(h == pl.num_programs(0) - 1)
    def _():
        def turn(s, _):
            dk_ref[s] = dkt[s].T
            dv_ref[s] = dvt[s].T
            return 0

        lax.fori_loop(0, Sl, turn, 0)


def attn_bwd(ids, seg, tag, q, k, v, do, lse, parts):
    Sl, T, D = q.shape
    F = len(parts)
    H, R = parts[0].shape[:2]
    part = pl.BlockSpec((1, R, T), lambda h, s: (h, 0, 0))
    outs = [
        jax.ShapeDtypeStruct((Sl, T, D), f32),
        jax.ShapeDtypeStruct((Sl, T, D), bf16),
        jax.ShapeDtypeStruct((Sl, T, D), bf16),
    ]
    res = pl.pallas_call(
        functools.partial(attn_bwd_kernel, F, min(T, 512)),
        grid_spec=pltpu.PrefetchScalarGridSpec(
            num_scalar_prefetch=1,
            grid=(H,),
            in_specs=[resident(x) for x in (seg, tag, q, k, v, do, lse)] + [part] * F,
            out_specs=[resident(x) for x in outs] + [part] * F,
            scratch_shapes=[
                pltpu.VMEM((T, T), f32),
                pltpu.VMEM((T, T), f32),
                pltpu.VMEM((T, T), bf16),
                pltpu.VMEM((T, T), bf16),
                pltpu.VMEM((Sl, D, T), bf16),
                pltpu.VMEM((Sl, D, T), bf16),
                pltpu.VMEM((Sl, D, T), bf16),
                pltpu.VMEM((Sl, D, T), bf16),
            ],
        ),
        out_shape=outs + [jax.ShapeDtypeStruct((H, R, T), bf16)] * F,
        compiler_params=pltpu.CompilerParams(
            dimension_semantics=("arbitrary",), vmem_limit_bytes=63 << 20
        ),
        cost_estimate=cost(Sl * H * T * T * 1536, Sl * T * D * 16 + H * T * T * 4, Sl * H * T * T),
        name="attn_bwd",
    )(ids, seg, tag, q, k, v, do, lse, *parts)
    return res[0], res[1], res[2], list(res[3:])


def pair_norm(x, ones):
    cen = x.astype(f32) - dg(x, ones, NN)
    inv = lax.rsqrt(dg((cen * cen).astype(bf16), ones, NN) + EPS)
    return cen * inv, inv


def pair_fwd_kernel(pair_ref, gain_ref, w_ref, out_ref, low):
    G, T, C = pair_ref.shape
    ones = jnp.full((C, C), 1.0 / C, bf16)

    def row(i, _):
        n, _ = pair_norm(pair_ref[i], ones)
        low[:, pl.ds(pl.multiple_of(i * C, 128), C)] = (n * gain_ref[...]).astype(bf16)
        return 0

    lax.fori_loop(0, G, row, 0)
    res = dg(w_ref[...], low[...], NT)
    out_ref[...] = res.reshape(res.shape[0] // G, G, T).astype(bf16)


def pair_fwd(pair, gain, w_rows):
    R, T, C = pair.shape
    G = 8
    H = w_rows.shape[0] // G
    return pl.pallas_call(
        pair_fwd_kernel,
        grid=(R // G,),
        in_specs=[
            pl.BlockSpec((G, T, C), lambda i: (i, 0, 0)),
            pl.BlockSpec((1, C), lambda i: (0, 0)),
            pl.BlockSpec((H * G, G * C), lambda i: (0, 0)),
        ],
        out_specs=pl.BlockSpec((H, G, T), lambda i: (0, i, 0)),
        out_shape=jax.ShapeDtypeStruct((H, R, T), bf16),
        scratch_shapes=[pltpu.VMEM((T, G * C), bf16)],
        compiler_params=pltpu.CompilerParams(
            dimension_semantics=("arbitrary",), vmem_limit_bytes=40 << 20
        ),
        cost_estimate=cost(R * T * C * 256, R * T * C * 3, R * T * C),
        name="pair_fwd",
    )(pair, gain, w_rows)


def pair_bwd_kernel(P, pair_ref, gain_ref, wc_ref, *refs):
    parts = refs[:P]
    out_ref, gw_ref, acc, turned = refs[P:]
    G, T, C = pair_ref.shape
    H = parts[0].shape[0]
    ones = jnp.full((C, C), 1.0 / C, bf16)

    @pl.when(pl.program_id(0) == 0)
    def _():
        acc[...] = jnp.zeros_like(acc)

    total = parts[0][...].astype(f32)
    for p in range(1, P):
        total = total + parts[p][...].astype(f32)
    flat = total.reshape(H * G, T)
    low8 = flat.astype(bf16)
    cols = low8.T
    turned[:, : H * G] = cols
    turned[:, H * G :] = cols

    def row(i, _):
        n, inv = pair_norm(pair_ref[i], ones)
        low = (n * gain_ref[...]).astype(bf16)
        acc[i] += dg(low8, low, NN)
        g = dg(turned[...], wc_ref[i], NN)
        mean = dg((g * n).astype(bf16), ones, NN)
        out_ref[i] = (inv * (g - n * mean)).astype(bf16)
        return 0

    lax.fori_loop(0, G, row, 0)

    @pl.when(pl.program_id(0) == pl.num_programs(0) - 1)
    def _():
        at = lax.broadcasted_iota(jnp.int32, (H * G, 1), 0) % G
        picked = jnp.zeros((H * G, C), f32)
        for i in range(G):
            picked = picked + jnp.where(at == i, acc[i], 0.0)
        gw_ref[...] = picked


def pair_bwd(pair, gain, wc, parts):
    R, T, C = pair.shape
    G = 8
    H = parts[0].shape[0]
    P = len(parts)
    return pl.pallas_call(
        functools.partial(pair_bwd_kernel, P),
        grid=(R // G,),
        in_specs=[
            pl.BlockSpec((G, T, C), lambda i: (i, 0, 0)),
            pl.BlockSpec((1, C), lambda i: (0, 0)),
            pl.BlockSpec((G, 2 * H * G, C), lambda i: (0, 0, 0)),
        ]
        + [pl.BlockSpec((H, G, T), lambda i: (0, i, 0))] * P,
        out_specs=[
            pl.BlockSpec((G, T, C), lambda i: (i, 0, 0)),
            pl.BlockSpec((H * G, C), lambda i: (0, 0)),
        ],
        out_shape=[
            jax.ShapeDtypeStruct((R, T, C), bf16),
            jax.ShapeDtypeStruct((H * G, C), f32),
        ],
        scratch_shapes=[
            pltpu.VMEM((G, H * G, C), f32),
            pltpu.VMEM((T, 2 * H * G), bf16),
        ],
        compiler_params=pltpu.CompilerParams(
            dimension_semantics=("arbitrary",), vmem_limit_bytes=40 << 20
        ),
        cost_estimate=cost(R * T * C * 512, R * T * C * 5, R * T * C),
        name="pair_bwd",
    )(pair, gain, wc, *parts)


def stats_of(x):
    mean = jnp.mean(x, axis=-1, keepdims=True)
    cen = x - mean
    inv = lax.rsqrt(jnp.mean(cen * cen, axis=-1, keepdims=True) + EPS)
    return cen * inv, inv


def sigmoid(x):
    return 1.0 / (1.0 + jnp.exp(-x))


def flat_rows(x):
    return x.reshape(x.shape[0] * x.shape[1], x.shape[2])


def over_samples(x, sb):
    R = x.shape[0] // sb
    total = x[:R]
    for i in range(1, sb):
        total = total + x[i * R : (i + 1) * R]
    return total


def tile_samples(x, sb):
    return x if sb == 1 else jnp.concatenate([x] * sb, axis=0)


def weight_copies(shapes, F, c, f, own, got, swapped, dst, sems):
    copies = []

    def add(src, to):
        copies.append(pltpu.make_async_copy(src, to, sems.at[len(copies)]))

    for i, (r, n) in enumerate(shapes):
        add(own[i], dst[i].at[pl.ds(pl.multiple_of(f * r, 16), r), :])
    for k in range(1, F):
        for packed, half in ((got[k - 1], c), (swapped[k - 1], 1 - c)):
            at = 0
            for i, (r, n) in enumerate(shapes):
                row = pl.multiple_of((f ^ k) * r, 16)
                for b in range(n // 2 // 384):
                    col = pl.multiple_of(half * (n // 2) + b * 384, 128)
                    add(
                        packed.at[pl.ds(at, r), :],
                        dst[i].at[pl.ds(row, r), pl.ds(col, 384)],
                    )
                    at += r
    return copies


def copies_in_group(shapes, F):
    return len(shapes) + (F - 1) * 2 * sum(n // 2 // 384 for _, n in shapes)


def pack_grads(shapes, F, c, accs, keep_ref, give_ref):
    for g in range(F):
        at = 0
        for (r, n), acc in zip(shapes, accs):
            for b in range(n // 2 // 384):
                for ref, half in ((keep_ref, c), (give_ref, 1 - c)):
                    col = pl.multiple_of(half * (n // 2) + b * 384, 128)
                    ref[g, at : at + r, :] = acc[g * r : (g + 1) * r, pl.ds(col, 384)].astype(bf16)
                at += r


def qkvg_kernel(F, shapes, ids, *refs):
    nin = 2 * (F - 1)
    act_ref, cond_ref, bq_ref, wq_hbm = refs[:4]
    got, swapped = refs[4 : 4 + F - 1], refs[4 + F - 1 : 4 + nin]
    q_ref, k_ref, v_ref, g_ref, w, sems = refs[4 + nin :]
    c, f = ids[F], ids[F + 1]

    @pl.when((pl.program_id(0) == 0) & (pl.program_id(1) == 0))
    def _():
        copies = weight_copies(shapes, F, c, f, (wq_hbm,), got, swapped, (w,), sems)
        for x in copies:
            x.start()
        for x in copies:
            x.wait()

    _, sb, R, D = act_ref.shape
    n, _ = stats_of(flat_rows(act_ref[0].astype(f32)))
    scale = tile_samples(sigmoid(cond_ref[:, :D]), sb)
    shift = tile_samples(cond_ref[:, D : 2 * D], sb)
    x = (scale * n + shift).astype(bf16)
    q_ref[...] = (dg(x, w[:, :D], NN) + bq_ref[...]).astype(bf16).reshape(sb, R, D)
    k_ref[...] = dg(x, w[:, D : 2 * D], NN).astype(bf16).reshape(sb, R, D)
    v_ref[...] = dg(x, w[:, 2 * D : 3 * D], NN).astype(bf16).reshape(sb, R, D)
    g_ref[0] = sigmoid(dg(x, w[:, 3 * D :], NN)).reshape(sb, R, D)


def sub_samples(sl, R):
    sb = max(1, min(sl, 256 // R))
    return sb, sl // sb


def cost(flops, nbytes, trans=0):
    return pl.CostEstimate(flops=int(flops), bytes_accessed=int(nbytes), transcendentals=int(trans))


ANY = pl.BlockSpec(memory_space=pl.ANY)


def qkvg_call(ids, act, cond, bq, wq, got, swapped):
    F, sl, R, D = act.shape
    T = F * R
    sb, nu = sub_samples(sl, R)
    shapes = [wq.shape]
    stacked = pl.BlockSpec((1, sb, R, D), lambda r, u, s: (r, u, 0, 0))
    natural = pl.BlockSpec((sb, R, D), lambda r, u, s: (u, s[r], 0))
    return pl.pallas_call(
        functools.partial(qkvg_kernel, F, shapes),
        grid_spec=pltpu.PrefetchScalarGridSpec(
            num_scalar_prefetch=1,
            grid=(F, nu),
            in_specs=[
                stacked,
                pl.BlockSpec((R, 2 * D), lambda r, u, s: (s[r], 0)),
                pl.BlockSpec((1, D), lambda r, u, s: (0, 0)),
            ]
            + [ANY] * (1 + 2 * (F - 1)),
            out_specs=[natural] * 3 + [stacked],
            scratch_shapes=[
                pltpu.VMEM((D, 4 * D), bf16),
                pltpu.SemaphoreType.DMA((copies_in_group(shapes, F),)),
            ],
        ),
        out_shape=[jax.ShapeDtypeStruct((sl, T, D), bf16)] * 3
        + [jax.ShapeDtypeStruct((F, sl, R, D), f32)],
        compiler_params=pltpu.CompilerParams(
            dimension_semantics=("arbitrary", "arbitrary"), vmem_limit_bytes=60 << 20
        ),
        cost_estimate=cost(8 * sl * T * D * D, 2 * sl * T * D * 6 + 8 * D * D, sl * T * D),
        name="qkvg",
    )(ids, act, cond, bq, wq, *got, *swapped)


def middle_kernel(F, shapes, ids, *refs):
    nin = 2 * (F - 1)
    mix_ref, gate_ref, act_ref, cot_ref, gone_ref, ctwo_ref = refs[:6]
    own = refs[6:9]
    got, swapped = refs[9 : 9 + F - 1], refs[9 + F - 1 : 9 + nin]
    (
        out_ref,
        da_ref,
        gpg_ref,
        mg_ref,
        ctg_ref,
        gog_ref,
        keep_ref,
        give_ref,
        wo,
        wab,
        wout,
        ao,
        aab,
        aout,
        sems,
    ) = refs[9 + nin :]
    c, f = ids[F], ids[F + 1]
    first = (pl.program_id(0) == 0) & (pl.program_id(1) == 0)
    last = (pl.program_id(0) == pl.num_programs(0) - 1) & (
        pl.program_id(1) == pl.num_programs(1) - 1
    )

    @pl.when(first)
    def _():
        copies = weight_copies(shapes, F, c, f, own, got, swapped, (wo, wab, wout), sems)
        for x in copies:
            x.start()
        ao[...] = jnp.zeros_like(ao)
        aab[...] = jnp.zeros_like(aab)
        aout[...] = jnp.zeros_like(aout)
        for x in copies:
            x.wait()

    _, sb, R, D = act_ref.shape
    H = wout.shape[0]
    gate = flat_rows(gate_ref[0])
    mix = flat_rows(mix_ref[...])
    branch = (gate * mix).astype(bf16)
    attn_out = dg(branch, wo[...], NN)
    sig_one = sigmoid(gone_ref[...])
    gate_one = tile_samples(sig_one, sb)
    middle = flat_rows(act_ref[0].astype(f32)) + gate_one * attn_out
    n, inv = stats_of(middle)
    sig_scale = sigmoid(ctwo_ref[:, :D])
    scale = tile_samples(sig_scale, sb)
    x2 = (scale * n + tile_samples(ctwo_ref[:, D : 2 * D], sb)).astype(bf16)
    up = dg(x2, wab[:, H:], NN)
    gp = dg(x2, wab[:, :H], NN)
    sg = sigmoid(gp)
    silu = gp * sg
    hidden = (silu * up).astype(bf16)
    ffn = dg(hidden, wout[...], NN)
    sig_two = sigmoid(ctwo_ref[:, 2 * D :])
    gate_two = tile_samples(sig_two, sb)
    out_ref[0] = (middle + gate_two * ffn).astype(bf16).reshape(sb, R, D)

    upstream = flat_rows(cot_ref[0].astype(f32))
    fg = (upstream * gate_two).astype(bf16)
    g_two = over_samples(upstream * ffn, sb) * (sig_two * (1.0 - sig_two))
    aout[...] += dg(hidden, fg, TN)
    hg = dg(fg, wout[...], NT)
    ga = (hg * up * sg * (1.0 + gp * (1.0 - sg))).astype(bf16)
    gb = (hg * silu).astype(bf16)
    aab[:, :H] += dg(x2, ga, TN)
    aab[:, H:] += dg(x2, gb, TN)
    xg = dg(ga, wab[:, :H], NT) + dg(gb, wab[:, H:], NT)
    g_scale = over_samples(xg * n, sb) * (sig_scale * (1.0 - sig_scale))
    g_shift = over_samples(xg, sb)
    inc = xg * scale
    mg = upstream + inv * (
        inc
        - jnp.mean(inc, axis=-1, keepdims=True)
        - n * jnp.mean(inc * n, axis=-1, keepdims=True)
    )
    mg_ref[0] = mg.reshape(sb, R, D)
    og = (mg * gate_one).astype(bf16)
    g_one = over_samples(mg * attn_out, sb) * (sig_one * (1.0 - sig_one))
    ao[...] += dg(branch, og, TN)
    bg = dg(og, wo[...], NT)
    da_ref[...] = (bg * gate).astype(bf16).reshape(sb, R, D)
    gpg_ref[0] = (bg * mix * (gate * (1.0 - gate))).astype(bf16).reshape(sb, R, D)

    @pl.when(pl.program_id(1) == 0)
    def _():
        ctg_ref[:, :D] = g_scale
        ctg_ref[:, D : 2 * D] = g_shift
        ctg_ref[:, 2 * D :] = g_two
        gog_ref[...] = g_one

    @pl.when(pl.program_id(1) > 0)
    def _():
        ctg_ref[:, :D] += g_scale
        ctg_ref[:, D : 2 * D] += g_shift
        ctg_ref[:, 2 * D :] += g_two
        gog_ref[...] += g_one

    @pl.when(last)
    def _():
        pack_grads(shapes, F, c, (ao, aab, aout), keep_ref, give_ref)


def middle_call(ids, mix, gate, act, cot, cond_one, cond_two, wo, wab, wout, got, swapped):
    F, sl, R, D = act.shape
    T = F * R
    H = wout.shape[0] * F
    sb, nu = sub_samples(sl, R)
    shapes = [wo.shape, wab.shape, wout.shape]
    rows = sum(r * (n // 2 // 384) for r, n in shapes)
    stacked = pl.BlockSpec((1, sb, R, D), lambda r, u, s: (r, u, 0, 0))
    natural = pl.BlockSpec((sb, R, D), lambda r, u, s: (u, s[r], 0))
    whole = pl.BlockSpec((F, rows, 384), lambda r, u, s: (0, 0, 0), pipeline_mode=pl.Buffered(1))
    flops = 3 * 2 * sl * T * D * (D + 3 * H)
    return pl.pallas_call(
        functools.partial(middle_kernel, F, shapes),
        grid_spec=pltpu.PrefetchScalarGridSpec(
            num_scalar_prefetch=1,
            grid=(F, nu),
            in_specs=[
                natural,
                stacked,
                stacked,
                stacked,
                pl.BlockSpec((R, D), lambda r, u, s: (s[r], 2)),
                pl.BlockSpec((R, 3 * D), lambda r, u, s: (s[r], 0)),
            ]
            + [ANY] * (3 + 2 * (F - 1)),
            out_specs=[
                stacked,
                natural,
                stacked,
                stacked,
                pl.BlockSpec((R, 3 * D), lambda r, u, s: (s[r], 0)),
                pl.BlockSpec((R, D), lambda r, u, s: (s[r], 0)),
                whole,
                whole,
            ],
            scratch_shapes=[
                pltpu.VMEM((D, D), bf16),
                pltpu.VMEM((D, 2 * H), bf16),
                pltpu.VMEM((H, D), bf16),
                pltpu.VMEM((D, D), f32),
                pltpu.VMEM((D, 2 * H), f32),
                pltpu.VMEM((H, D), f32),
                pltpu.SemaphoreType.DMA((copies_in_group(shapes, F),)),
            ],
        ),
        out_shape=[
            jax.ShapeDtypeStruct((F, sl, R, D), bf16),
            jax.ShapeDtypeStruct((sl, T, D), bf16),
            jax.ShapeDtypeStruct((F, sl, R, D), bf16),
            jax.ShapeDtypeStruct((F, sl, R, D), f32),
            jax.ShapeDtypeStruct((T, 3 * D), f32),
            jax.ShapeDtypeStruct((T, D), f32),
            jax.ShapeDtypeStruct((F, rows, 384), bf16),
            jax.ShapeDtypeStruct((F, rows, 384), bf16),
        ],
        compiler_params=pltpu.CompilerParams(
            dimension_semantics=("arbitrary", "arbitrary"), vmem_limit_bytes=63 << 20
        ),
        cost_estimate=cost(flops, sl * T * D * 24, sl * T * H),
        name="middle",
    )(ids, mix, gate, act, cot, cond_one, cond_two, wo, wab, wout, *got, *swapped)


def back_kernel(F, shapes, ids, *refs):
    nin = 2 * (F - 1)
    act_ref, cond_ref, dq_ref, dk_ref, dv_ref, gpg_ref, mg_ref, wq_hbm = refs[:8]
    got, swapped = refs[8 : 8 + F - 1], refs[8 + F - 1 : 8 + nin]
    ag_ref, cg_ref, bq_ref, keep_ref, give_ref, w, acc, sems = refs[8 + nin :]
    c, f = ids[F], ids[F + 1]
    first = (pl.program_id(0) == 0) & (pl.program_id(1) == 0)
    last = (pl.program_id(0) == pl.num_programs(0) - 1) & (
        pl.program_id(1) == pl.num_programs(1) - 1
    )

    @pl.when(first)
    def _():
        copies = weight_copies(shapes, F, c, f, (wq_hbm,), got, swapped, (w,), sems)
        for x in copies:
            x.start()
        acc[...] = jnp.zeros_like(acc)
        bq_ref[...] = jnp.zeros_like(bq_ref)
        for x in copies:
            x.wait()

    _, sb, R, D = act_ref.shape
    n, inv = stats_of(flat_rows(act_ref[0].astype(f32)))
    sig_scale = sigmoid(cond_ref[:, :D])
    scale = tile_samples(sig_scale, sb)
    x = (scale * n + tile_samples(cond_ref[:, D : 2 * D], sb)).astype(bf16)
    dq = flat_rows(dq_ref[...])
    bq_ref[...] += jnp.sum(dq, axis=0, keepdims=True)
    xg = None
    grads = (dq.astype(bf16), flat_rows(dk_ref[...]), flat_rows(dv_ref[...]), flat_rows(gpg_ref[0]))
    for i, g in enumerate(grads):
        acc[:, i * D : (i + 1) * D] += dg(x, g, TN)
        part = dg(g, w[:, i * D : (i + 1) * D], NT)
        xg = part if xg is None else xg + part
    g_scale = over_samples(xg * n, sb) * (sig_scale * (1.0 - sig_scale))
    g_shift = over_samples(xg, sb)
    inc = xg * scale
    ag = flat_rows(mg_ref[0]) + inv * (
        inc
        - jnp.mean(inc, axis=-1, keepdims=True)
        - n * jnp.mean(inc * n, axis=-1, keepdims=True)
    )
    ag_ref[0] = ag.astype(bf16).reshape(sb, R, D)

    @pl.when(pl.program_id(1) == 0)
    def _():
        cg_ref[:, :D] = g_scale
        cg_ref[:, D:] = g_shift

    @pl.when(pl.program_id(1) > 0)
    def _():
        cg_ref[:, :D] += g_scale
        cg_ref[:, D:] += g_shift

    @pl.when(last)
    def _():
        pack_grads(shapes, F, c, (acc,), keep_ref, give_ref)


def back_call(ids, act, cond, dq, dk, dv, gpg, mg, wq, got, swapped):
    F, sl, R, D = act.shape
    T = F * R
    sb, nu = sub_samples(sl, R)
    shapes = [wq.shape]
    rows = sum(r * (n // 2 // 384) for r, n in shapes)
    stacked = pl.BlockSpec((1, sb, R, D), lambda r, u, s: (r, u, 0, 0))
    natural = pl.BlockSpec((sb, R, D), lambda r, u, s: (u, s[r], 0))
    whole = pl.BlockSpec((F, rows, 384), lambda r, u, s: (0, 0, 0), pipeline_mode=pl.Buffered(1))
    return pl.pallas_call(
        functools.partial(back_kernel, F, shapes),
        grid_spec=pltpu.PrefetchScalarGridSpec(
            num_scalar_prefetch=1,
            grid=(F, nu),
            in_specs=[
                stacked,
                pl.BlockSpec((R, 2 * D), lambda r, u, s: (s[r], 0)),
                natural,
                natural,
                natural,
                stacked,
                stacked,
            ]
            + [ANY] * (1 + 2 * (F - 1)),
            out_specs=[
                stacked,
                pl.BlockSpec((R, 2 * D), lambda r, u, s: (s[r], 0)),
                pl.BlockSpec((1, D), lambda r, u, s: (0, 0)),
                whole,
                whole,
            ],
            scratch_shapes=[
                pltpu.VMEM((D, 4 * D), bf16),
                pltpu.VMEM((D, 4 * D), f32),
                pltpu.SemaphoreType.DMA((copies_in_group(shapes, F),)),
            ],
        ),
        out_shape=[
            jax.ShapeDtypeStruct((F, sl, R, D), bf16),
            jax.ShapeDtypeStruct((T, 2 * D), f32),
            jax.ShapeDtypeStruct((1, D), f32),
            jax.ShapeDtypeStruct((F, rows, 384), bf16),
            jax.ShapeDtypeStruct((F, rows, 384), bf16),
        ],
        compiler_params=pltpu.CompilerParams(
            dimension_semantics=("arbitrary", "arbitrary"), vmem_limit_bytes=60 << 20
        ),
        cost_estimate=cost(16 * sl * T * D * D, sl * T * D * 22 + 16 * D * D, sl * T),
        name="back",
    )(ids, act, cond, dq, dk, dv, gpg, mg, wq, *got, *swapped)


class Net:
    def __init__(self, dp, fsdp):
        self.Z, self.F, self.Fh = dp // 2, fsdp, fsdp // 2
        d = lax.axis_index("dp")
        self.z, self.c = d // 2, d % 2
        self.f = lax.axis_index("fsdp")
        self.fh, self.fl = self.f // self.Fh, self.f % self.Fh
        r = jnp.arange(self.F, dtype=jnp.int32)
        blocks = (self.c ^ (r % 2)) * self.Fh + (self.fl ^ (r // 2))
        rows = ((self.c + r // self.Fh) % 2) * self.Fh + (self.fl ^ (r % self.Fh))
        self.ids = jnp.concatenate(
            [blocks, jnp.stack([self.c, self.f]), rows]
        ).astype(jnp.int32)

    def send(self, x, fn):
        F = self.F
        pairs = []
        for z in range(self.Z):
            for c in range(2):
                for f in range(F):
                    z2, c2, f2 = fn(z, c, f)
                    pairs.append(((z * 2 + c) * F + f, (z2 * 2 + c2) * F + f2))
        return lax.ppermute(x, ("dp", "fsdp"), pairs)

    def core_swap(self, x):
        return self.send(x, lambda z, c, f: (z, 1 - c, f))

    def to_owner(self, x, a):
        Fh = self.Fh
        return self.send(x, lambda z, c, f: (z, f // Fh, c * Fh + ((f % Fh) ^ a)))

    def exchange_in(self, x):
        F, Fh = self.F, self.Fh
        sl = x.shape[0] // F
        parts = []
        for a in range(Fh):
            for b in range(2):
                g = (self.fl ^ a) * 2 + (self.fh ^ b)
                part = lax.dynamic_slice_in_dim(x, g * sl, sl, 0)
                parts.append(
                    self.send(part, lambda z, c, f: (z, (f // Fh) ^ b, c * Fh + ((f % Fh) ^ a)))
                )
        return parts

    def exchange_out(self, y):
        F, sl, R, D = y.shape
        Fh = self.Fh
        out = jnp.zeros((F * sl, R, D), y.dtype)
        for a in range(Fh):
            for b in range(2):
                part = self.send(
                    y[a * 2 + b], lambda z, c, f: (z, f // Fh, (c ^ b) * Fh + ((f % Fh) ^ a))
                )
                g = (self.fl ^ a) * 2 + (self.fh ^ b)
                out = lax.dynamic_update_slice_in_dim(out, part, g * sl, 0)
        return out

    def gather_rows(self, x):
        own = [self.to_owner(x, a) for a in range(self.Fh)]
        return own + [self.core_swap(p) for p in own]

    def natural(self, parts, axis):
        R = parts[0].shape[axis]
        shape = parts[0].shape
        out = jnp.zeros(shape[:axis] + (R * self.F,) + shape[axis + 1 :], parts[0].dtype)
        for p, part in enumerate(parts):
            out = lax.dynamic_update_slice_in_dim(out, part, self.ids[self.F + 2 + p] * R, axis)
        return out

    def reduce_rows(self, parts):
        Fh = self.Fh
        out = []
        for a in range(Fh):
            got = self.core_swap(parts[Fh + a])
            half = (parts[a].astype(f32) + got.astype(f32)).astype(got.dtype)
            out.append(self.to_owner(half, a))
        return out

    def core_half(self, x, half):
        n = x.shape[-1]
        x = lax.dynamic_slice_in_dim(x, half * (n // 2), n // 2, x.ndim - 1)
        return [x[..., b * 384 : (b + 1) * 384] for b in range(n // 2 // 384)]

    def pack(self, xs, half):
        blocks = [b for x in xs for b in self.core_half(x, half)]
        return jnp.concatenate(blocks, axis=-2)

    def gather_packed(self, packed):
        F = self.F
        got = [self.send(packed, lambda z, c, f: (z, c, f ^ k)) for k in range(1, F)]
        return got, [self.core_swap(g) for g in got]

    def gather_weight(self, w):
        return lax.all_gather(w, "fsdp", axis=0, tiled=True)

    def reduce_plane(self, keep, give):
        got = self.core_swap(give)
        total = None
        for k in range(self.F):
            mine = lax.dynamic_index_in_dim(keep, self.f ^ k, 0, keepdims=False)
            other = lax.dynamic_index_in_dim(got, self.f ^ k, 0, keepdims=False)
            part = mine.astype(f32) + other.astype(f32)
            if k:
                part = self.send(part.astype(bf16), lambda z, c, f: (z, c, f ^ k)).astype(f32)
            total = part if total is None else total + part
        return total.astype(bf16)

    def reduce_z(self, flat):
        Z = self.Z
        rows = flat.shape[0]
        pad = -rows % Z
        if pad:
            flat = jnp.pad(flat, ((0, pad), (0, 0)))
        bit = 1
        while bit < Z:
            h = flat.shape[0] // 2
            up = (self.z // bit) % 2
            keep = lax.dynamic_slice_in_dim(flat, up * h, h, 0)
            give = lax.dynamic_slice_in_dim(flat, (1 - up) * h, h, 0)
            got = self.send(give, lambda z, c, f: (z ^ bit, c, f))
            flat = (keep.astype(f32) + got.astype(f32)).astype(bf16)
            bit *= 2
        while bit > 1:
            bit //= 2
            up = (self.z // bit) % 2
            got = self.send(flat, lambda z, c, f: (z ^ bit, c, f))
            flat = jnp.concatenate(
                [jnp.where(up == 0, flat, got), jnp.where(up == 0, got, flat)], axis=0
            )
        other = self.core_swap(flat)
        return jnp.where(self.c == 0, flat, other), jnp.where(self.c == 0, other, flat)

    def unpack(self, halves, shapes):
        outs, at = [], 0
        for r, n in shapes:
            nb = n // 2 // 384
            cols = []
            for half in halves:
                for b in range(nb):
                    cols.append(half[at + b * r : at + (b + 1) * r])
            at += nb * r
            outs.append(jnp.concatenate(cols, axis=1).astype(f32))
        return outs


def body(
    dp,
    fsdp,
    act,
    single,
    pair,
    segment,
    padding,
    cotangent,
    gain_s1,
    w_cond1,
    b_cond1,
    w_qkvg,
    b_q,
    gain_z,
    w_pair,
    w_o,
    gain_s2,
    w_cond2,
    b_cond2,
    w_ab,
    w_out,
):
    net = Net(dp, fsdp)
    F, ids = net.F, net.ids
    act, single, pair, segment, padding, cotangent = (
        x[0] for x in (act, single, pair, segment, padding, cotangent)
    )
    S, R, D = act.shape
    T = R * F
    COND = single.shape[1]

    vecs = [gain_s1, b_cond1, b_q, gain_z, w_pair, gain_s2, b_cond2]
    sizes = [v.size for v in vecs]
    srows = -(-sum(sizes) // 768)
    flat = jnp.concatenate([v.reshape(-1) for v in vecs])
    flat = jnp.pad(flat, (0, srows * 768 - flat.shape[0])).reshape(srows, 768)
    smalls = jnp.zeros((F, srows, 768), bf16)
    for k in range(F):
        got = flat if k == 0 else net.send(flat, lambda z, c, f: (z, c, f ^ k))
        smalls = lax.dynamic_update_slice_in_dim(smalls, got[None], net.f ^ k, 0)
    smalls = smalls.reshape(F, srows * 768)
    full, at = [], 0
    for v, n in zip(vecs, sizes):
        full.append(smalls[:, at : at + n].reshape((F * v.shape[0],) + v.shape[1:]).astype(f32))
        at += n
    gs1, bc1, bq, gz, wp, gs2, bc2 = full

    wc1 = net.gather_weight(w_cond1)
    tag = jnp.where(padding == 1, -1, segment)
    cols = jnp.stack([segment.astype(f32), tag.astype(f32)], axis=1)
    cond_in = jnp.concatenate([single, jnp.pad(cols, ((0, 0), (0, 126)))], axis=1)
    cond_in = net.natural(net.gather_rows(cond_in), 0)
    single_all = cond_in[:, :COND]
    seg_col = cond_in[:, COND : COND + 1]
    tag_row = cond_in[:, COND + 1].reshape(1, T)

    act_l = jnp.stack(net.exchange_in(act))
    wq_got, wq_swapped = net.gather_packed(net.pack([w_qkvg], net.c))

    wt = wp.T
    eye = jnp.eye(8, dtype=f32)
    w_rows = (wt[:, None, None, :] * eye[None, :, :, None]).reshape(HEADS * 8, -1).astype(bf16)
    gz_row = gz.reshape(1, -1)
    bias = net.gather_rows(pair_fwd(pair, gz_row, w_rows))

    wc2 = net.gather_weight(w_cond2)
    single_n, _ = norm_stats(single_all)
    single_first = (single_n * gs1).astype(bf16)
    cond_one = dg(single_first, wc1, NN) + bc1
    q, k, v, gate = qkvg_call(
        ids, act_l, cond_one, bq.reshape(1, D), w_qkvg, wq_got, wq_swapped
    )

    mid_got, mid_swapped = net.gather_packed(net.pack([w_o, w_ab, w_out], net.c))
    cot_l = jnp.stack(net.exchange_in(cotangent))
    single_second = (single_n * gs2).astype(bf16)
    cond_two = dg(single_second, wc2, NN) + bc2

    mix, lse = attn_fwd(ids, seg_col, tag_row, q, k, v, bias)
    out, d_attn, gate_proj, mid_grad, cond_two_grad, gate_one_grad, keep, give = middle_call(
        ids, mix, gate, act_l, cot_l, cond_one, cond_two, w_o, w_ab, w_out, mid_got, mid_swapped
    )
    block_out = net.exchange_out(out)[None]

    cond_two_low = cond_two_grad.astype(bf16)
    grad_w_cond2 = dg(single_second, cond_two_low, TN)
    s_two_grad = dg(cond_two_low, wc2, NT)
    piece_mid = net.reduce_plane(keep, give)
    g4 = grad_w_cond2.astype(bf16).reshape(F, -1, 3 * D)
    piece_c2 = net.reduce_plane(net.pack([g4], net.c), net.pack([g4], 1 - net.c))
    early = [w_o.shape, w_ab.shape, w_out.shape, w_cond2.shape]
    total_wo, total_wab, total_wout, total_wc2 = net.unpack(
        net.reduce_z(jnp.concatenate([piece_mid, piece_c2], axis=0)), early
    )

    dq, dk, dv, db = attn_bwd(ids, seg_col, tag_row, q, k, v, d_attn, lse, bias)
    db = net.reduce_rows(db)
    ag, cond_one_part, bq_grad, keep, give = back_call(
        ids, act_l, cond_one, dq, dk, dv, gate_proj, mid_grad, w_qkvg, wq_got, wq_swapped
    )
    act_grad = net.exchange_out(ag)[None]
    cond_one_grad = jnp.concatenate([cond_one_part, gate_one_grad], axis=1)
    cond_one_low = cond_one_grad.astype(bf16)
    grad_w_cond1 = dg(single_first, cond_one_low, TN)
    s_one_grad = dg(cond_one_low, wc1, NT)
    s_grad = s_one_grad * gs1 + s_two_grad * gs2
    s_parts = [
        lax.dynamic_slice_in_dim(s_grad, ids[F + 2 + p] * R, R, 0) for p in range(F)
    ]
    s_grad = functools.reduce(jnp.add, net.reduce_rows(s_parts))
    local_n, local_inv = norm_stats(single)
    single_grad = norm_back(local_n, local_inv, s_grad)[None]

    wc = wt * gz_row
    wc = wc - jnp.mean(wc, axis=1, keepdims=True)
    wc = (wc[None, :, None, :] * eye[:, None, :, None]).reshape(8, HEADS * 8, -1)
    wc_hi = wc.astype(bf16)
    wc = jnp.concatenate([wc_hi, (wc - wc_hi.astype(f32)).astype(bf16)], axis=1)
    pair_grad, gw = pair_bwd(pair, gz_row, wc, db)
    grad_w_pair = jnp.sum(gw.reshape(HEADS, 8, -1), axis=1).T
    grad_gain_z = jnp.sum(wp * grad_w_pair, axis=1) / gz

    small_grads = [
        jnp.sum(s_one_grad * single_n, axis=0),
        jnp.sum(cond_one_grad, axis=0),
        bq_grad,
        grad_gain_z,
        grad_w_pair,
        jnp.sum(s_two_grad * single_n, axis=0),
        jnp.sum(cond_two_grad, axis=0),
    ]
    sg = jnp.concatenate([g.reshape(F, -1) for g in small_grads], axis=1)
    sg = jnp.pad(sg, ((0, 0), (0, srows * 768 - sg.shape[1]))).reshape(F, srows, 768)
    g4 = [grad_w_cond1.astype(bf16).reshape(F, -1, 3 * D), sg.astype(bf16)]
    piece_wq = net.reduce_plane(keep, give)
    piece_c1 = net.reduce_plane(net.pack(g4, net.c), net.pack(g4, 1 - net.c))
    late = [w_qkvg.shape, w_cond1.shape, (srows, 768)]
    total_wq, total_wc1, total_small = net.unpack(
        net.reduce_z(jnp.concatenate([piece_wq, piece_c1], axis=0)), late
    )
    total_small = total_small.reshape(-1)
    outs, at = [], 0
    for v_, n in zip(vecs, sizes):
        outs.append(total_small[at : at + n].reshape(v_.shape))
        at += n
    total_gs1, total_bc1, total_bq, total_gz, total_wp, total_gs2, total_bc2 = outs
    return (
        block_out,
        act_grad,
        single_grad,
        pair_grad[None],
        total_gs1,
        total_wc1,
        total_bc1,
        total_wq,
        total_bq,
        total_gz,
        total_wp,
        total_wo,
        total_gs2,
        total_wc2,
        total_bc2,
        total_wab,
        total_wout,
    )


def solution(mesh):
    return jax.shard_map(
        functools.partial(body, mesh.shape["dp"], mesh.shape["fsdp"]),
        mesh=mesh,
        in_specs=(
            P("dp", None, "fsdp", None),
            P("dp", "fsdp", None),
            P("dp", "fsdp", None, None),
            P("dp", "fsdp"),
            P("dp", "fsdp"),
            P("dp", None, "fsdp", None),
            P("fsdp"),
            P("fsdp", None),
            P("fsdp"),
            P("fsdp", None),
            P("fsdp"),
            P("fsdp"),
            P("fsdp", None),
            P("fsdp", None),
            P("fsdp"),
            P("fsdp", None),
            P("fsdp"),
            P("fsdp", None),
            P("fsdp", None),
        ),
        out_specs=(
            P("dp", None, "fsdp", None),
            P("dp", None, "fsdp", None),
            P("dp", "fsdp", None),
            P("dp", "fsdp", None, None),
            P("fsdp"),
            P("fsdp", None),
            P("fsdp"),
            P("fsdp", None),
            P("fsdp"),
            P("fsdp"),
            P("fsdp", None),
            P("fsdp", None),
            P("fsdp"),
            P("fsdp", None),
            P("fsdp"),
            P("fsdp", None),
            P("fsdp", None),
        ),
        check_vma=False,
    )
```

time: 1320 us -> 1000 us (0.76)
  Pallas kernels: 0 us -> 441 us
  matrix products: 419 us -> 15.6 us
  other arithmetic: 209 us -> 55.5 us
  local copies, waits for them, and re-layouts: 179 us -> 53.2 us
  starting transfers between devices: 1.82 us -> 91.8 us
  waiting for transfers between devices: 404 us -> 321 us
  blocking collectives: 77.2 us -> 0 us
    pallas_call x0 -> x7, Pallas kernels: none -> 441 us  [the longest x1 96.2 us: pair_bwd(): pl.pallas_call(functools.partial(pair_bwd_kernel, P), grid=(R // G,), in_...]
    dot_general x27 -> x6, matrix products: 419 us -> 15.6 us  [dg(): return lax.dot_general(a, b, dims, preferred_element_type=f32)]
    ppermute x0 -> x73, waiting for transfers between devices: none -> 320 us  [send(): return lax.ppermute(x, ('dp', 'fsdp'), pairs)]
    all_gather x8 -> x2, waiting for transfers between devices: 196 us -> 0.01 us  [gather_weight(): return lax.all_gather(w, 'fsdp', axis=0, tiled=True)]
    reduce_scatter x8 -> x0, waiting for transfers between devices: 179 us -> none  [the longest x1 60.2 us: body(): lax.psum_scatter(grad_w_qkvg.astype(jnp.bfloat16), 'fsdp', scatter_dimens...]
    ppermute x0 -> x73, starting transfers between devices: none -> 91.8 us  [send(): return lax.ppermute(x, ('dp', 'fsdp'), pairs)]
    reduce_sum x8 -> x5, other arithmetic: 96.9 us -> 5.35 us  [the longest x1 2.59 us: body(): jnp.sum(cond_two_grad, axis=0)]
    unnamed x152 -> x149, local copies, waits for them, and re-layouts: 74.2 us -> 17.3 us
  transfers between devices with their start and end apart: 18 -> 75, of which waited for: 11 -> 24; matrix products, arithmetic and copies ran while one was open for 50% -> 11% of each run, Pallas kernels for 0% -> 36%
where the time goes in v1:
time: 1000 us; the launch traced here: 997 us
  Pallas kernels  441 us (44%)
  waiting for transfers between devices  321 us (32%)
  starting transfers between devices  91.8 us (9%)
  other arithmetic  55.5 us (6%)
  local copies, waits for them, and re-layouts  53.2 us (5%)
  between operations  18.6 us (2%)
  matrix products  15.6 us (2%)
    ppermute x73, waiting for transfers between devices, send(): return lax.ppermute(x, ('dp', 'fsdp'), pairs)  320 us
    pallas_call x1, Pallas kernels, pair_bwd(): pl.pallas_call(functools.partial(pair_bwd_kernel, P), grid=(R // G,), in_...  96.2 us
    ppermute x73, starting transfers between devices, send(): return lax.ppermute(x, ('dp', 'fsdp'), pairs)  91.8 us
    pallas_call x1, Pallas kernels, attn_bwd(): pl.pallas_call(functools.partial(attn_bwd_kernel, F, min(T, 512)), grid_s...  89 us
    pallas_call x1, Pallas kernels, middle_call(): pl.pallas_call(functools.partial(middle_kernel, F, shapes), grid_spec=plt...  84.6 us
    pallas_call x1, Pallas kernels, attn_fwd(): pl.pallas_call(functools.partial(attn_fwd_kernel, F, min(T, 256)), grid_s...  63.4 us
    pallas_call x1, Pallas kernels, pair_fwd(): pl.pallas_call(pair_fwd_kernel, grid=(R // G,), in_specs=[pl.BlockSpec((G...  51.4 us
    pallas_call x1, Pallas kernels, back_call(): pl.pallas_call(functools.partial(back_kernel, F, shapes), grid_spec=pltpu...  36.3 us
  transfers between devices with their start and end apart: 75, of which 24 were waited for; matrix products, arithmetic and copies ran while one was open for 11% of the time, Pallas kernels for 36%

profile of v1, /device:TPU:0, one launch (start us, length us, event | category | flops | bytes accessed | tf_op | source)
XLA Modules:
  0.0 997.2 jit_solution(5748633135091489992)
XLA Ops:
  15.9 4.1 concatenate.78
  52.3 51.4 %pair_fwd.1 = bf16[16,128,512]{2,1,0:T(8,128)(2,1)S(1)} custom-call(bf16[128,512,128]{2,1,0:T(8,128)(2,1)} %bitcast.156, f32[1,128]{1,0:T(1,128)S(1)} %reshape.363.gain_ref, bf16[128,1024]{1,0:T(8,128)(2,1)S(1)} %fusion.31.w_ref), custom_call_target="tpu_custom_call" | custom-call | flops 2147483648 | bytes 25165824 | tf_op jit(solution)/shard_map/pair_fwd/pallas_call | solution.py:263
  105.6 7.4 collective-permute-start.21
  117.0 7.5 collective-permute-done.6
  124.5 17.0 %collective-permute-done.7 = bf16[4,128,768]{2,1,0:T(8,128)(2,1)} collective-permute-done((bf16[4,128,768]{2,1,0:T(8,128)(2,1)}, bf16[4,128,768]{2,1,0:T(8,128)(2,1)}, u32[]{:S(2)}, u32[]{:S(2)}) %collective-permute-start.7) | collective-permute-done | bytes 786464 | tf_op jit(solution)/shard_map/ppermute | solution.py:796
  144.8 44.8 %collective-permute-done.22 = bf16[4,128,768]{2,1,0:T(8,128)(2,1)S(1)} collective-permute-done((bf16[4,128,768]{2,1,0:T(8,128)(2,1)}, bf16[4,128,768]{2,1,0:T(8,128)(2,1)S(1)}, u32[]{:S(2)}, u32[]{:S(2)}) %collective-permute-start.22) | collective-permute-done | bytes 786464 | tf_op jit(solution)/shard_map/ppermute | solution.py:796
  190.5 12.5 %collective-permute-done.23 = bf16[4,128,768]{2,1,0:T(8,128)(2,1)S(1)} collective-permute-done((bf16[4,128,768]{2,1,0:T(8,128)(2,1)}, bf16[4,128,768]{2,1,0:T(8,128)(2,1)S(1)}, u32[]{:S(2)}, u32[]{:S(2)}) %collective-permute-start.23) | collective-permute-done | bytes 786464 | tf_op jit(solution)/shard_map/ppermute | solution.py:796
  203.5 16.5 %collective-permute-done.24 = bf16[4,128,768]{2,1,0:T(8,128)(2,1)S(1)} collective-permute-done((bf16[4,128,768]{2,1,0:T(8,128)(2,1)}, bf16[4,128,768]{2,1,0:T(8,128)(2,1)S(1)}, u32[]{:S(2)}, u32[]{:S(2)}) %collective-permute-start.24) | collective-permute-done | bytes 786464 | tf_op jit(solution)/shard_map/ppermute | solution.py:796
  228.4 13.7 %collective-permute-done.25.refs_9_ = bf16[1344,384]{1,0:T(8,128)(2,1)} collective-permute-done((bf16[1344,384]{1,0:T(8,128)(2,1)}, bf16[1344,384]{1,0:T(8,128)(2,1)}, u32[]{:S(2)}, u32[]{:S(2)}) %collective-permute-start.25) | collective-permute-done | bytes 1032224 | tf_op jit(solution)/shard_map/ppermute | solution.py:796
  242.6 20.6 %collective-permute-done.27.refs_11_ = bf16[1344,384]{1,0:T(8,128)(2,1)} collective-permute-done((bf16[1344,384]{1,0:T(8,128)(2,1)}, bf16[1344,384]{1,0:T(8,128)(2,1)}, u32[]{:S(2)}, u32[]{:S(2)}) %collective-permute-start.27) | collective-permute-done | bytes 1032224 | tf_op jit(solution)/shard_map/ppermute | solution.py:796
  263.2 5.1 convolution_add_fusion.1.refs_1_.refs_4_
  268.3 5.1 convolution_add_fusion.refs_5_
  274.4 20.5 %qkvg.1 = (bf16[4,512,768]{2,1,0:T(8,128)(2,1)}, bf16[4,512,768]{2,1,0:T(8,128)(2,1)}, bf16[4,512,768]{2,1,0:T(8,128)(2,1)}, f32[4,4,128,768]{3,2,1,0:T(8,128)}) custom-call(s32[10]{0:T(128)} %pad_add_fusion.ids, bf16[4,4,128,768]{3,2,1,0:T(8,128)(2,1)} %pad_maximum_fusion.refs_0_.refs_2_, f32[512,2304]{1,0:T(8,128)} %convolution_add_fusion.1.refs_1_.refs_4_, ...), custom_call_target="tpu_custom_call" | custom-call | flops 9663676416 | bytes 23592960 | tf_op jit(solution)/shard_map/qkvg/pallas_call | solution.py:466
  294.9 63.4 %attn_fwd.1 = (f32[4,512,768]{2,1,0:T(8,128)}, f32[4,512,128]{2,1,0:T(8,128)}) custom-call(s32[10]{0:T(128)} %pad_add_fusion.ids, f32[512,1]{1,0:T(8,128)} %get-tuple-element.233.seg_ref, f32[1,512]{1,0:T(1,128)} %bitcast.178, bf16[4,512,768]{2,1,0:T(8,128)(2,1)} %get-tuple-element.45.q_ref, bf16[4,512,768]{2,1,0:T(8,128)(2,1)} %get-tuple-element.46.k_ref, ...), custom_call_target="tpu_custom_call" | custom-call | flops 17179869184 | bytes 24117248 | tf_op jit(solution)/shard_map/attn_fwd/pallas_call | solution.py:114
  358.4 84.6 %middle.1 = (bf16[4,4,128,768]{3,2,1,0:T(8,128)(2,1)}, bf16[4,512,768]{2,1,0:T(8,128)(2,1)}, bf16[4,4,128,768]{3,2,1,0:T(8,128)(2,1)}, f32[4,4,128,768]{3,2,1,0:...) custom-call(s32[10]{0:T(128)} %pad_add_fusion.ids, ...), custom_call_target="tpu_custom_call" | custom-call | flops 50734301184 | bytes 37748736 | tf_op jit(solution)/shard_map/middle/pallas_call | solution.py:611
  443.2 89.0 %attn_bwd.1 = (f32[4,512,768]{2,1,0:T(8,128)}, bf16[4,512,768]{2,1,0:T(8,128)(2,1)}, bf16[4,512,768]{2,1,0:T(8,128)(2,1)}, bf16[16,128,512]{2,1,0:T(8,128)(2,1)}...) custom-call(s32[10]{0:T(128)} %pad_add_fusion.ids, ...), custom_call_target="tpu_custom_call" | custom-call | flops 25769803776 | bytes 41943040 | tf_op jit(solution)/shard_map/attn_bwd/pallas_call | solution.py:211
  532.2 36.3 %back.1 = (bf16[4,4,128,768]{3,2,1,0:T(8,128)(2,1)}, f32[512,1536]{1,0:T(8,128)}, f32[1,768]{1,0:T(1,128)}, bf16[4,768,384]{2,1,0:T(8,128)(2,1)}, bf16[4,768,384]{2,1,0:T(8,128)(2,1)}) custom-call(s32[10]{0:T(128)} %pad_add_fusion.ids, bf16[4,4,128,768]{3,2,1,0:T(8,128)(2,1)} %pad_maximum_fusion.refs_0_.refs_2_, ...), custom_call_target="tpu_custom_call" | custom-call | flops 19327352832 | bytes 44040192 | tf_op jit(solution)/shard_map/back/pallas_call | solution.py:731
  587.1 7.4 collective-permute-start.35
  601.5 17.2 %collective-permute-start.44 = (bf16[16,128,512]{2,1,0:T(8,128)(2,1)}, bf16[16,128,512]{2,1,0:T(8,128)(2,1)}, u32[]{:S(2)}, u32[]{:S(2)}) collective-permute-start(bf16[16,128,512]{2,1,0:T(8,128)(2,1)} %add_convert_fusion.1), channel_id=1, source_target_pairs={{0,0},{1,1},{2,4},{3,5},{4,2},{5,3},{6,6},{7,7},{8,8},{9,9},{10,12... | collective-permute-start | bytes 6291464 | tf_op jit(solution)/shard_map/ppermute | solution.py:796
  629.2 22.4 %collective-permute-done.36 = bf16[4,128,768]{2,1,0:T(8,128)(2,1)S(1)} collective-permute-done((bf16[4,128,768]{2,1,0:T(8,128)(2,1)}, bf16[4,128,768]{2,1,0:T(8,128)(2,1)S(1)}, u32[]{:S(2)}, u32[]{:S(2)}) %collective-permute-start.36) | collective-permute-done | bytes 786464 | tf_op jit(solution)/shard_map/ppermute | solution.py:796
  664.7 96.2 %pair_bwd.1 = (bf16[128,512,128]{2,1,0:T(8,128)(2,1)}, f32[128,128]{1,0:T(8,128)S(1)}) custom-call(bf16[128,512,128]{2,1,0:T(8,128)(2,1)} %bitcast.157, f32[1,128]{1,0:T(1,128)S(1)} %copy-done.1, bf16[8,256,128]{2,1,0:T(8,128)(2,1)S(1)} %pad_maximum_fusion.10.wc_ref, bf16[16,128,512]{2,1,0:T(8,128)(2,1)} %collective-permute-done.44.refs_0_, ...), custom_call_target="tpu_custom_call" | custom-call | flops 4294967296 | bytes 41943040 | tf_op jit(solution)/shard_map/pair_bwd/pallas_call | solution.py:327
  778.0 7.7 collective-permute-done.50
  791.6 15.8 %collective-permute-done.61 = bf16[1344,384]{1,0:T(8,128)(2,1)S(1)} collective-permute-done((bf16[1344,384]{1,0:T(8,128)(2,1)S(1)}, bf16[1344,384]{1,0:T(8,128)(2,1)S(1)}, u32[]{:S(2)}, u32[]{:S(2)}) %collective-permute-start.61) | collective-permute-done | bytes 1032224 | tf_op jit(solution)/shard_map/ppermute | solution.py:796
  809.4 20.6 %collective-permute-done.63 = bf16[1344,384]{1,0:T(8,128)(2,1)S(1)} collective-permute-done((bf16[1344,384]{1,0:T(8,128)(2,1)S(1)}, bf16[1344,384]{1,0:T(8,128)(2,1)S(1)}, u32[]{:S(2)}, u32[]{:S(2)}) %collective-permute-start.63) | collective-permute-done | bytes 1032224 | tf_op jit(solution)/shard_map/ppermute | solution.py:796
  834.7 33.5 %collective-permute-done.52 = bf16[291,384]{1,0:T(8,128)(2,1)S(1)} collective-permute-done((bf16[291,384]{1,0:T(8,128)(2,1)S(1)}, bf16[291,384]{1,0:T(8,128)(2,1)S(1)}, u32[]{:S(2)}, u32[]{:S(2)}) %collective-permute-start.52) | collective-permute-done | bytes 223520 | tf_op jit(solution)/shard_map/ppermute | solution.py:796
  877.7 19.4 %collective-permute-done.55 = bf16[530,384]{1,0:T(8,128)(2,1)S(1)} collective-permute-done((bf16[530,384]{1,0:T(8,128)(2,1)S(1)}, bf16[530,384]{1,0:T(8,128)(2,1)S(1)}, u32[]{:S(2)}, u32[]{:S(2)}) %collective-permute-start.55) | collective-permute-done | bytes 407072 | tf_op jit(solution)/shard_map/ppermute | solution.py:796
  903.8 14.8 %collective-permute-done.56 = bf16[265,384]{1,0:T(8,128)(2,1)S(1)} collective-permute-done((bf16[265,384]{1,0:T(8,128)(2,1)S(1)}, bf16[265,384]{1,0:T(8,128)(2,1)S(1)}, u32[]{:S(2)}, u32[]{:S(2)}) %collective-permute-start.56) | collective-permute-done | bytes 203552 | tf_op jit(solution)/shard_map/ppermute | solution.py:796
  918.8 11.0 %collective-permute-done.69 = bf16[408,384]{1,0:T(8,128)(2,1)S(1)} collective-permute-done((bf16[408,384]{1,0:T(8,128)(2,1)S(1)}, bf16[408,384]{1,0:T(8,128)(2,1)S(1)}, u32[]{:S(2)}, u32[]{:S(2)}) %collective-permute-start.69) | collective-permute-done | bytes 313376 | tf_op jit(solution)/shard_map/ppermute | solution.py:796
  929.9 11.0 %collective-permute-done.57 = bf16[265,384]{1,0:T(8,128)(2,1)S(1)} collective-permute-done((bf16[265,384]{1,0:T(8,128)(2,1)S(1)}, bf16[265,384]{1,0:T(8,128)(2,1)S(1)}, u32[]{:S(2)}, u32[]{:S(2)}) %collective-permute-start.57) | collective-permute-done | bytes 203552 | tf_op jit(solution)/shard_map/ppermute | solution.py:796
  941.2 5.3 collective-permute-done.70
  947.4 7.9 collective-permute-done.58
  955.9 12.8 %collective-permute-done.71 = bf16[816,384]{1,0:T(8,128)(2,1)S(1)} collective-permute-done((bf16[816,384]{1,0:T(8,128)(2,1)S(1)}, bf16[816,384]{1,0:T(8,128)(2,1)S(1)}, u32[]{:S(2)}, u32[]{:S(2)}) %collective-permute-start.71) | collective-permute-done | bytes 626720 | tf_op jit(solution)/shard_map/ppermute | solution.py:796
  (446 shorter events, 175.9 us)
Async XLA Ops:
  7.2 256.0 %all-gather.3.cloned.1.call-start = ((), (), s32[]{:S(2)}) async-start(), calls=%async_computation | async-start | bytes 2211840 | tf_op jit(solution)/shard_map/all_gather | solution.py:867
  7.9 260.4 %all-gather.5.cloned.1.call-start = ((), (), s32[]{:S(2)}) async-start(), calls=%async_computation.1 | async-start | bytes 2211840 | tf_op jit(solution)/shard_map/all_gather | solution.py:867
  42.0 71.0 %collective-permute-start.4 = (bf16[4,128,768]{2,1,0:T(8,128)(2,1)}, bf16[4,128,768]{2,1,0:T(8,128)(2,1)S(1)}, u32[]{:S(2)}, u32[]{:S(2)}) collective-permute-start(bf16[4,128,768]{2,1,0:T(8,128)(2,1)} %get-tuple-element.198), channel_id=1, source_target_pairs={{0,0},{1,1},{2,4},{3,5},{4,2},{5,3},{6,6},{7,7},{8,8},{9,9},{10,12... | collective-permute-start | bytes 2359304 | tf_op jit(solution)/shard_map/ppermute | solution.py:796
  43.8 71.1 %collective-permute-start.5 = (bf16[4,128,768]{2,1,0:T(8,128)(2,1)}, bf16[4,128,768]{2,1,0:T(8,128)(2,1)}, u32[]{:S(2)}, u32[]{:S(2)}) collective-permute-start(bf16[4,128,768]{2,1,0:T(8,128)(2,1)} %get-tuple-element.199), channel_id=1, source_target_pairs={{0,4},{1,5},{2,0},{3,1},{4,6},{5,7},{6,2},{7,3},{8,12},{9,13},{10,... | collective-permute-start | bytes 2359304 | tf_op jit(solution)/shard_map/ppermute | solution.py:796
  46.2 57.5 %collective-permute-start.11 = (bf16[768,384]{1,0:T(8,128)(2,1)}, bf16[768,384]{1,0:T(8,128)(2,1)}, u32[]{:S(2)}, u32[]{:S(2)}) collective-permute-start(bf16[768,384]{1,0:T(8,128)(2,1)} %pad_maximum_fusion.9), channel_id=1, source_target_pairs={{0,1},{1,0},{2,3},{3,2},{4,5},{5,4},{6,7},{7,6},{8,9},{9,8},{10,11... | collective-permute-start | bytes 1769480 | tf_op jit(solution)/shard_map/ppermute | solution.py:796
  49.1 55.1 %collective-permute-start.12 = (bf16[768,384]{1,0:T(8,128)(2,1)}, bf16[768,384]{1,0:T(8,128)(2,1)S(1)}, u32[]{:S(2)}, u32[]{:S(2)}) collective-permute-start(bf16[768,384]{1,0:T(8,128)(2,1)} %pad_maximum_fusion.9), channel_id=1, source_target_pairs={{0,2},{1,3},{2,0},{3,1},{4,6},{5,7},{6,4},{7,5},{8,10},{9,11},{10,... | collective-permute-start | bytes 1769480 | tf_op jit(solution)/shard_map/ppermute | solution.py:796
  49.7 55.9 %collective-permute-start.13 = (bf16[768,384]{1,0:T(8,128)(2,1)}, bf16[768,384]{1,0:T(8,128)(2,1)S(1)}, u32[]{:S(2)}, u32[]{:S(2)}) collective-permute-start(bf16[768,384]{1,0:T(8,128)(2,1)} %pad_maximum_fusion.9), channel_id=1, source_target_pairs={{0,3},{1,2},{2,1},{3,0},{4,7},{5,6},{6,5},{7,4},{8,11},{9,10},{10,... | collective-permute-start | bytes 1769480 | tf_op jit(solution)/shard_map/ppermute | solution.py:796
  113.0 108.7 %collective-permute-start.17 = (bf16[16,128,512]{2,1,0:T(8,128)(2,1)S(1)}, bf16[16,128,512]{2,1,0:T(8,128)(2,1)}, u32[]{:S(2)}, u32[]{:S(2)}) collective-permute-start(bf16[16,128,512]{2,1,0:T(8,128)(2,1)S(1)} %pair_fwd.1), channel_id=1, source_target_pairs={{0,0},{1,1},{2,4},{3,5},{4,2},{5,3},{6,6},{7,7},{8,8},{9,9},{10,12... | collective-permute-start | bytes 6291464 | tf_op jit(solution)/shard_map/ppermute | solution.py:796
  114.9 107.0 %collective-permute-start.18 = (bf16[16,128,512]{2,1,0:T(8,128)(2,1)S(1)}, bf16[16,128,512]{2,1,0:T(8,128)(2,1)}, u32[]{:S(2)}, u32[]{:S(2)}) collective-permute-start(bf16[16,128,512]{2,1,0:T(8,128)(2,1)S(1)} %pair_fwd.1), channel_id=1, source_target_pairs={{0,1},{1,0},{2,5},{3,4},{4,3},{5,2},{6,7},{7,6},{8,9},{9,8},{10,13... | collective-permute-start | bytes 6291464 | tf_op jit(solution)/shard_map/ppermute | solution.py:796
  124.5 65.1 %collective-permute-start.22 = (bf16[4,128,768]{2,1,0:T(8,128)(2,1)}, bf16[4,128,768]{2,1,0:T(8,128)(2,1)S(1)}, u32[]{:S(2)}, u32[]{:S(2)}) collective-permute-start(bf16[4,128,768]{2,1,0:T(8,128)(2,1)} %get-tuple-element.195), channel_id=1, source_target_pairs={{0,4},{1,5},{2,0},{3,1},{4,6},{5,7},{6,2},{7,3},{8,12},{9,13},{10,... | collective-permute-start | bytes 2359304 | tf_op jit(solution)/shard_map/ppermute | solution.py:796
  141.5 61.5 %collective-permute-start.23 = (bf16[4,128,768]{2,1,0:T(8,128)(2,1)}, bf16[4,128,768]{2,1,0:T(8,128)(2,1)S(1)}, u32[]{:S(2)}, u32[]{:S(2)}) collective-permute-start(bf16[4,128,768]{2,1,0:T(8,128)(2,1)} %get-tuple-element.197), channel_id=1, source_target_pairs={{0,1},{1,0},{2,5},{3,4},{4,3},{5,2},{6,7},{7,6},{8,9},{9,8},{10,13... | collective-permute-start | bytes 2359304 | tf_op jit(solution)/shard_map/ppermute | solution.py:796
  141.8 78.2 %collective-permute-start.24 = (bf16[4,128,768]{2,1,0:T(8,128)(2,1)}, bf16[4,128,768]{2,1,0:T(8,128)(2,1)S(1)}, u32[]{:S(2)}, u32[]{:S(2)}) collective-permute-start(bf16[4,128,768]{2,1,0:T(8,128)(2,1)} %get-tuple-element.196), channel_id=1, source_target_pairs={{0,5},{1,4},{2,1},{3,0},{4,7},{5,6},{6,3},{7,2},{8,13},{9,12},{10,... | collective-permute-start | bytes 2359304 | tf_op jit(solution)/shard_map/ppermute | solution.py:796
  221.7 73.2 %collective-permute-start.19 = (bf16[16,128,512]{2,1,0:T(8,128)(2,1)}, bf16[16,128,512]{2,1,0:T(8,128)(2,1)}, u32[]{:S(2)}, u32[]{:S(2)}) collective-permute-start(bf16[16,128,512]{2,1,0:T(8,128)(2,1)} %collective-permute-done.17.refs_0_), channel_id=1, source_target_pairs={{0,4},{1,5},{2,6},{3,7},{4,0},{5,1},{6,2},{7,3},{8,12},{9,13},{10,... | collective-permute-start | bytes 6291464 | tf_op jit(solution)/shard_map/ppermute | solution.py:796
  221.9 73.0 %collective-permute-start.20 = (bf16[16,128,512]{2,1,0:T(8,128)(2,1)}, bf16[16,128,512]{2,1,0:T(8,128)(2,1)}, u32[]{:S(2)}, u32[]{:S(2)}) collective-permute-start(bf16[16,128,512]{2,1,0:T(8,128)(2,1)} %collective-permute-done.18.refs_1_), channel_id=1, source_target_pairs={{0,4},{1,5},{2,6},{3,7},{4,0},{5,1},{6,2},{7,3},{8,12},{9,13},{10,... | collective-permute-start | bytes 6291464 | tf_op jit(solution)/shard_map/ppermute | solution.py:796
  273.4 85.0 %collective-permute-start.28 = (bf16[1344,384]{1,0:T(8,128)(2,1)}, bf16[1344,384]{1,0:T(8,128)(2,1)}, u32[]{:S(2)}, u32[]{:S(2)}) collective-permute-start(bf16[1344,384]{1,0:T(8,128)(2,1)} %collective-permute-done.25.refs_9_), channel_id=1, source_target_pairs={{0,4},{1,5},{2,6},{3,7},{4,0},{5,1},{6,2},{7,3},{8,12},{9,13},{10,... | collective-permute-start | bytes 3096584 | tf_op jit(solution)/shard_map/ppermute | solution.py:796
  273.9 84.5 %collective-permute-start.29 = (bf16[1344,384]{1,0:T(8,128)(2,1)}, bf16[1344,384]{1,0:T(8,128)(2,1)}, u32[]{:S(2)}, u32[]{:S(2)}) collective-permute-start(bf16[1344,384]{1,0:T(8,128)(2,1)} %collective-permute-done.26.refs_10_), channel_id=1, source_target_pairs={{0,4},{1,5},{2,6},{3,7},{4,0},{5,1},{6,2},{7,3},{8,12},{9,13},{10,... | collective-permute-start | bytes 3096584 | tf_op jit(solution)/shard_map/ppermute | solution.py:796
  274.0 84.4 %collective-permute-start.30 = (bf16[1344,384]{1,0:T(8,128)(2,1)}, bf16[1344,384]{1,0:T(8,128)(2,1)}, u32[]{:S(2)}, u32[]{:S(2)}) collective-permute-start(bf16[1344,384]{1,0:T(8,128)(2,1)} %collective-permute-done.27.refs_11_), channel_id=1, source_target_pairs={{0,4},{1,5},{2,6},{3,7},{4,0},{5,1},{6,2},{7,3},{8,12},{9,13},{10,... | collective-permute-start | bytes 3096584 | tf_op jit(solution)/shard_map/ppermute | solution.py:796
  443.0 323.8 %collective-permute-start.60 = (bf16[4,1344,384]{2,1,0:T(8,128)(2,1)}, bf16[4,1344,384]{2,1,0:T(8,128)(2,1)}, u32[]{:S(2)}, u32[]{:S(2)}) collective-permute-start(bf16[4,1344,384]{2,1,0:T(8,128)(2,1)} %get-tuple-element.72), channel_id=1, source_target_pairs={{0,4},{1,5},{2,6},{3,7},{4,0},{5,1},{6,2},{7,3},{8,12},{9,13},{10,... | collective-permute-start | bytes 12386312 | tf_op jit(solution)/shard_map/ppermute | solution.py:796
  568.5 90.1 %collective-permute-start.47 = (bf16[4,768,384]{2,1,0:T(8,128)(2,1)}, bf16[4,768,384]{2,1,0:T(8,128)(2,1)}, u32[]{:S(2)}, u32[]{:S(2)}) collective-permute-start(bf16[4,768,384]{2,1,0:T(8,128)(2,1)} %get-tuple-element.68), channel_id=1, source_target_pairs={{0,4},{1,5},{2,6},{3,7},{4,0},{5,1},{6,2},{7,3},{8,12},{9,13},{10,... | collective-permute-start | bytes 7077896 | tf_op jit(solution)/shard_map/ppermute | solution.py:796
  600.4 62.3 %collective-permute-start.46 = (bf16[16,128,512]{2,1,0:T(8,128)(2,1)}, bf16[16,128,512]{2,1,0:T(8,128)(2,1)S(1)}, u32[]{:S(2)}, u32[]{:S(2)}) collective-permute-start(bf16[16,128,512]{2,1,0:T(8,128)(2,1)} %add_convert_fusion), channel_id=1, source_target_pairs={{0,1},{1,0},{2,5},{3,4},{4,3},{5,2},{6,7},{7,6},{8,9},{9,8},{10,13... | collective-permute-start | bytes 6291464 | tf_op jit(solution)/shard_map/ppermute | solution.py:796
  601.5 62.2 %collective-permute-start.44 = (bf16[16,128,512]{2,1,0:T(8,128)(2,1)}, bf16[16,128,512]{2,1,0:T(8,128)(2,1)}, u32[]{:S(2)}, u32[]{:S(2)}) collective-permute-start(bf16[16,128,512]{2,1,0:T(8,128)(2,1)} %add_convert_fusion.1), channel_id=1, source_target_pairs={{0,0},{1,1},{2,4},{3,5},{4,2},{5,3},{6,6},{7,7},{8,8},{9,9},{10,12... | collective-permute-start | bytes 6291464 | tf_op jit(solution)/shard_map/ppermute | solution.py:796
  657.7 106.1 %collective-permute-start.65 = (bf16[288,384]{1,0:T(8,128)(2,1)}, bf16[288,384]{1,0:T(8,128)(2,1)}, u32[]{:S(2)}, u32[]{:S(2)}) collective-permute-start(bf16[288,384]{1,0:T(8,128)(2,1)} %get-tuple-element.204), channel_id=1, source_target_pairs={{0,1},{1,0},{2,3},{3,2},{4,5},{5,4},{6,7},{7,6},{8,9},{9,8},{10,11... | collective-permute-start | bytes 663560 | tf_op jit(solution)/shard_map/ppermute | solution.py:796
  658.6 106.9 %collective-permute-start.66 = (bf16[288,384]{1,0:T(8,128)(2,1)}, bf16[288,384]{1,0:T(8,128)(2,1)}, u32[]{:S(2)}, u32[]{:S(2)}) collective-permute-start(bf16[288,384]{1,0:T(8,128)(2,1)} %get-tuple-element.206), channel_id=1, source_target_pairs={{0,2},{1,3},{2,0},{3,1},{4,6},{5,7},{6,4},{7,5},{8,10},{9,11},{10,... | collective-permute-start | bytes 663560 | tf_op jit(solution)/shard_map/ppermute | solution.py:796
  662.7 111.3 %collective-permute-start.48 = (bf16[768,384]{1,0:T(8,128)(2,1)}, bf16[768,384]{1,0:T(8,128)(2,1)}, u32[]{:S(2)}, u32[]{:S(2)}) collective-permute-start(bf16[768,384]{1,0:T(8,128)(2,1)} %get-tuple-element.183), channel_id=1, source_target_pairs={{0,1},{1,0},{2,3},{3,2},{4,5},{5,4},{6,7},{7,6},{8,9},{9,8},{10,11... | collective-permute-start | bytes 1769480 | tf_op jit(solution)/shard_map/ppermute | solution.py:796
  663.7 111.4 %collective-permute-start.49 = (bf16[768,384]{1,0:T(8,128)(2,1)}, bf16[768,384]{1,0:T(8,128)(2,1)}, u32[]{:S(2)}, u32[]{:S(2)}) collective-permute-start(bf16[768,384]{1,0:T(8,128)(2,1)} %get-tuple-element.185), channel_id=1, source_target_pairs={{0,2},{1,3},{2,0},{3,1},{4,6},{5,7},{6,4},{7,5},{8,10},{9,11},{10,... | collective-permute-start | bytes 1769480 | tf_op jit(solution)/shard_map/ppermute | solution.py:796
  785.7 89.1 %collective-permute-start.37 = (bf16[4,128,768]{2,1,0:T(8,128)(2,1)S(1)}, bf16[4,128,768]{2,1,0:T(8,128)(2,1)S(1)}, u32[]{:S(2)}, u32[]{:S(2)}) collective-permute-start(bf16[4,128,768]{2,1,0:T(8,128)(2,1)S(1)} %copy-done.27), channel_id=1, source_target_pairs={{0,1},{1,0},{2,5},{3,4},{4,3},{5,2},{6,7},{7,6},{8,9},{9,8},{10,13... | collective-permute-start | bytes 2359304 | tf_op jit(solution)/shard_map/ppermute | solution.py:796
  788.8 87.4 %collective-permute-start.38 = (bf16[4,128,768]{2,1,0:T(8,128)(2,1)S(1)}, bf16[4,128,768]{2,1,0:T(8,128)(2,1)S(1)}, u32[]{:S(2)}, u32[]{:S(2)}) collective-permute-start(bf16[4,128,768]{2,1,0:T(8,128)(2,1)S(1)} %copy-done.25), channel_id=1, source_target_pairs={{0,3},{1,2},{2,7},{3,6},{4,1},{5,0},{6,5},{7,4},{8,11},{9,10},{10,... | collective-permute-start | bytes 2359304 | tf_op jit(solution)/shard_map/ppermute | solution.py:796
  807.4 60.7 %collective-permute-start.52 = (bf16[291,384]{1,0:T(8,128)(2,1)S(1)}, bf16[291,384]{1,0:T(8,128)(2,1)S(1)}, u32[]{:S(2)}, u32[]{:S(2)}) collective-permute-start(bf16[291,384]{1,0:T(8,128)(2,1)S(1)} %get-tuple-element.234), channel_id=1, source_target_pairs={{0,1},{1,0},{2,3},{3,2},{4,5},{5,4},{6,7},{7,6},{8,9},{9,8},{10,11... | collective-permute-start | bytes 670472 | tf_op jit(solution)/shard_map/ppermute | solution.py:796
  808.5 60.4 %collective-permute-start.53 = (bf16[291,384]{1,0:T(8,128)(2,1)S(1)}, bf16[291,384]{1,0:T(8,128)(2,1)S(1)}, u32[]{:S(2)}, u32[]{:S(2)}) collective-permute-start(bf16[291,384]{1,0:T(8,128)(2,1)S(1)} %get-tuple-element.236), channel_id=1, source_target_pairs={{0,2},{1,3},{2,0},{3,1},{4,6},{5,7},{6,4},{7,5},{8,10},{9,11},{10,... | collective-permute-start | bytes 670472 | tf_op jit(solution)/shard_map/ppermute | solution.py:796
  868.9 72.3 %collective-permute-start.32 = (bf16[4,128,768]{2,1,0:T(8,128)(2,1)S(1)}, bf16[4,128,768]{2,1,0:T(8,128)(2,1)S(1)}, u32[]{:S(2)}, u32[]{:S(2)}) collective-permute-start(bf16[4,128,768]{2,1,0:T(8,128)(2,1)S(1)} %copy-done.28), channel_id=1, source_target_pairs={{0,2},{1,3},{2,6},{3,7},{4,0},{5,1},{6,4},{7,5},{8,10},{9,11},{10,... | collective-permute-start | bytes 2359304 | tf_op jit(solution)/shard_map/ppermute | solution.py:796
  876.2 79.5 %collective-permute-start.33 = (bf16[4,128,768]{2,1,0:T(8,128)(2,1)S(1)}, bf16[4,128,768]{2,1,0:T(8,128)(2,1)S(1)}, u32[]{:S(2)}, u32[]{:S(2)}) collective-permute-start(bf16[4,128,768]{2,1,0:T(8,128)(2,1)S(1)} %copy-done.26), channel_id=1, source_target_pairs={{0,1},{1,0},{2,5},{3,4},{4,3},{5,2},{6,7},{7,6},{8,9},{9,8},{10,13... | collective-permute-start | bytes 2359304 | tf_op jit(solution)/shard_map/ppermute | solution.py:796
  897.2 58.7 %collective-permute-start.34 = (bf16[4,128,768]{2,1,0:T(8,128)(2,1)S(1)}, bf16[4,128,768]{2,1,0:T(8,128)(2,1)S(1)}, u32[]{:S(2)}, u32[]{:S(2)}) collective-permute-start(bf16[4,128,768]{2,1,0:T(8,128)(2,1)S(1)} %copy-done.24), channel_id=1, source_target_pairs={{0,3},{1,2},{2,7},{3,6},{4,1},{5,0},{6,5},{7,4},{8,11},{9,10},{10,... | collective-permute-start | bytes 2359304 | tf_op jit(solution)/shard_map/ppermute | solution.py:796
  (101 other events, 2119.3 us)
Sparse Core Ops, SparseCore 0:
  9.9 36.5 all-gather.2
  48.2 55.2 all-gather.4

commit v2 on v1

v2 whole, which is shorter than its diff:
```python
import functools

import jax
import jax.numpy as jnp
from jax import lax
from jax.experimental import pallas as pl
from jax.experimental.pallas import tpu as pltpu
from jax.sharding import Mesh
from jax.sharding import PartitionSpec as P

HEADS = 16
HEAD = 48
FF = 1536
EPS = 1e-05
LOG2E = 1.4426950408889634
NEG = -1000000000.0
f32 = jnp.float32
bf16 = jnp.bfloat16
NT = (((1,), (1,)), ((), ()))
NN = (((1,), (0,)), ((), ()))
TN = (((0,), (0,)), ((), ()))


def norm_stats(values):
    average = jnp.mean(values, axis=-1, keepdims=True)
    centred = values - average
    inverse = lax.rsqrt(jnp.mean(centred * centred, axis=-1, keepdims=True) + EPS)
    return (centred * inverse, inverse)


def norm_back(normed, inverse, incoming):
    return inverse * (
        incoming
        - jnp.mean(incoming, axis=-1, keepdims=True)
        - normed * jnp.mean(incoming * normed, axis=-1, keepdims=True)
    )


def sig_slope(values):
    sigma_val = jax.nn.sigmoid(values)
    return sigma_val * (1.0 - sigma_val)


def dg(a, b, dims):
    return lax.dot_general(a, b, dims, preferred_element_type=f32)


def cost(flops, nbytes, trans=0):
    return pl.CostEstimate(flops=int(flops), bytes_accessed=int(nbytes), transcendentals=int(trans))


ANY = pl.BlockSpec(memory_space=pl.ANY)


def head_window(h, D):
    tile = jnp.minimum((h * HEAD) // 128, D // 128 - 2)
    return pl.multiple_of(tile * 128, 128), h * HEAD - tile * 128


def masked_bias(F, ids, seg_ref, tag_ref, parts, bm):
    for p in range(F):
        R = parts[p].shape[1]
        row = pl.multiple_of(ids[F + 2 + p] * R, 16)
        bm[pl.ds(row, R), :] = jnp.where(
            seg_ref[pl.ds(row, R), :] == tag_ref[...], parts[p][0].astype(f32) * LOG2E, -jnp.inf
        )


def head_scores(q, k, bm):
    s = dg(q, k, NT)
    return jnp.where(bm > -jnp.inf, s * (HEAD**-0.5 * LOG2E) + bm, NEG * LOG2E)


def attn_fwd_kernel(F, nd, RB, ids, seg_ref, tag_ref, q_ref, k_ref, v_ref, *refs):
    parts = refs[:F]
    o_ref, lse_ref, bm = refs[F + nd :]
    Sl, T, D = q_ref.shape
    h = pl.program_id(0)

    @pl.when(h == 0)
    def _():
        o_ref[...] = jnp.zeros_like(o_ref)
        lse_ref[...] = jnp.zeros_like(lse_ref)

    start, off = head_window(h, D)
    masked_bias(F, ids, seg_ref, tag_ref, parts, bm)
    lane = lax.broadcasted_iota(jnp.int32, (1, 256), 1)
    mine = (lane >= off) & (lane < off + HEAD)
    column = lax.broadcasted_iota(jnp.int32, (1, 128), 1) == h
    win = pl.ds(start, 256)

    def sample(s, _):
        kw = k_ref[s, :, win]
        vw = v_ref[s, :, win]
        vw = jnp.where(mine, vw, jnp.zeros_like(vw))
        for r in range(0, T, RB):
            rows = pl.ds(r, RB)
            qw = q_ref[s, rows, win]
            sc = head_scores(jnp.where(mine, qw, jnp.zeros_like(qw)), kw, bm[rows, :])
            m = jnp.max(sc, axis=-1, keepdims=True)
            p = jnp.exp2(sc - m)
            l = jnp.sum(p, axis=-1, keepdims=True)
            o_ref[s, rows, win] += dg(p.astype(bf16), vw, NN) * (1.0 / l)
            lse_ref[s, rows, :] = jnp.where(column, m + jnp.log2(l), lse_ref[s, rows, :])
        return 0

    lax.fori_loop(0, Sl, sample, 0, unroll=min(Sl, 4))


def resident(shape, last=0):
    at = (0,) * (len(shape) - 1) + (last,)
    return pl.BlockSpec(shape, lambda h, s: at, pipeline_mode=pl.Buffered(1))


def attn_fwd(ids, seg, tag, q, k, v, parts, group, deps=()):
    Sl, T, D = q.shape
    F = len(parts)
    H, R = parts[0].shape[:2]
    W = H * HEAD
    lanes = resident((Sl, T, W), group)
    part = pl.BlockSpec((1, R, T), lambda h, s: (h, 0, 0))
    outs = [jax.ShapeDtypeStruct((Sl, T, W), f32), jax.ShapeDtypeStruct((Sl, T, 128), f32)]
    return pl.pallas_call(
        functools.partial(attn_fwd_kernel, F, len(deps), min(T, 256)),
        grid_spec=pltpu.PrefetchScalarGridSpec(
            num_scalar_prefetch=1,
            grid=(H,),
            in_specs=[resident(seg.shape), resident(tag.shape), lanes, lanes, lanes]
            + [part] * F
            + [ANY] * len(deps),
            out_specs=[resident(x.shape) for x in outs],
            scratch_shapes=[pltpu.VMEM((T, T), f32)],
        ),
        out_shape=outs,
        compiler_params=pltpu.CompilerParams(
            dimension_semantics=("arbitrary",), vmem_limit_bytes=60 << 20
        ),
        cost_estimate=cost(Sl * H * T * T * 3700, Sl * T * W * 10 + H * T * T * 2, Sl * H * T * T),
        name="attn_fwd",
    )(ids, seg, tag, q, k, v, *parts, *deps)


def attn_bwd_kernel(F, nd, RB, ids, seg_ref, tag_ref, q_ref, k_ref, v_ref, do_ref, lse_ref, *refs):
    parts, refs = refs[:F], refs[nd:]
    dq_ref, dk_ref, dv_ref = refs[F : F + 3]
    db_refs = refs[F + 3 : F + 3 + F]
    bm, dbacc, pb, dsb, qt, dot, dkt, dvt = refs[F + 3 + F :]
    Sl, T, D = q_ref.shape
    h = pl.program_id(0)

    @pl.when(h == 0)
    def _():
        dq_ref[...] = jnp.zeros_like(dq_ref)

        def turn(s, _):
            qt[s] = q_ref[s].T
            dot[s] = do_ref[s].T
            return 0

        lax.fori_loop(0, Sl, turn, 0)

    start, off = head_window(h, D)
    masked_bias(F, ids, seg_ref, tag_ref, parts, bm)
    lane = lax.broadcasted_iota(jnp.int32, (1, 256), 1)
    mine = (lane >= off) & (lane < off + HEAD)
    column = lax.broadcasted_iota(jnp.int32, (1, 128), 1) == h
    win = pl.ds(start, 256)
    here = pl.ds(pl.multiple_of(h * HEAD, 16), HEAD)
    root = HEAD**-0.5
    dbacc[...] = jnp.zeros_like(dbacc)

    U = min(Sl, 2)

    def sample(s, u):
        kw = k_ref[s, :, win]
        vw = v_ref[s, :, win]
        km = jnp.where(mine, kw, jnp.zeros_like(kw))
        for r in range(0, T, RB):
            rows = pl.ds(r, RB)
            qw = q_ref[s, rows, win]
            gw = do_ref[s, rows, win]
            sc = head_scores(jnp.where(mine, qw, jnp.zeros_like(qw)), kw, bm[rows, :])
            lse = jnp.sum(
                jnp.where(column, lse_ref[s, rows, :], 0.0), axis=-1, keepdims=True
            )
            p = jnp.exp2(sc - lse)
            dp = dg(jnp.where(mine, gw, jnp.zeros_like(gw)), vw, NT)
            delta = jnp.sum(p * dp, axis=-1, keepdims=True)
            ds = (p * (dp - delta)).astype(bf16)
            pb[u, rows, :] = p.astype(bf16)
            dsb[u, rows, :] = ds
            dbacc[rows, :] += ds.astype(f32)
            dq_ref[s, rows, win] += dg(ds, km, NN) * root
        dvt[s, here, :] = dg(dot[s, here, :], pb[u], NN).astype(bf16)
        dkt[s, here, :] = (dg(qt[s, here, :], dsb[u], NN) * root).astype(bf16)

    def samples(i, _):
        for u in range(U):
            sample(i * U + u, u)
        return 0

    lax.fori_loop(0, Sl // U, samples, 0)
    for p in range(F):
        R = db_refs[p].shape[1]
        row = pl.multiple_of(ids[F + 2 + p] * R, 16)
        db_refs[p][0] = dbacc[pl.ds(row, R), :].astype(bf16)

    @pl.when(h == pl.num_programs(0) - 1)
    def _():
        def turn(s, _):
            dk_ref[s] = dkt[s].T
            dv_ref[s] = dvt[s].T
            return 0

        lax.fori_loop(0, Sl, turn, 0)


def attn_bwd(ids, seg, tag, q, k, v, do, lse, parts, group, deps=()):
    Sl, T, D = q.shape
    F = len(parts)
    H, R = parts[0].shape[:2]
    W = H * HEAD
    lanes = resident((Sl, T, W), group)
    part = pl.BlockSpec((1, R, T), lambda h, s: (h, 0, 0))
    outs = [
        jax.ShapeDtypeStruct((Sl, T, W), f32),
        jax.ShapeDtypeStruct((Sl, T, W), bf16),
        jax.ShapeDtypeStruct((Sl, T, W), bf16),
    ]
    res = pl.pallas_call(
        functools.partial(attn_bwd_kernel, F, len(deps), min(T, 512)),
        grid_spec=pltpu.PrefetchScalarGridSpec(
            num_scalar_prefetch=1,
            grid=(H,),
            in_specs=[resident(seg.shape), resident(tag.shape)]
            + [lanes] * 4
            + [resident(lse.shape)]
            + [part] * F
            + [ANY] * len(deps),
            out_specs=[resident(x.shape) for x in outs] + [part] * F,
            scratch_shapes=[
                pltpu.VMEM((T, T), f32),
                pltpu.VMEM((T, T), f32),
                pltpu.VMEM((2, T, T), bf16),
                pltpu.VMEM((2, T, T), bf16),
                pltpu.VMEM((Sl, W, T), bf16),
                pltpu.VMEM((Sl, W, T), bf16),
                pltpu.VMEM((Sl, W, T), bf16),
                pltpu.VMEM((Sl, W, T), bf16),
            ],
        ),
        out_shape=outs + [jax.ShapeDtypeStruct((H, R, T), bf16)] * F,
        compiler_params=pltpu.CompilerParams(
            dimension_semantics=("arbitrary",), vmem_limit_bytes=63 << 20
        ),
        cost_estimate=cost(Sl * H * T * T * 6200, Sl * T * W * 16 + H * T * T * 4, Sl * H * T * T),
        name="attn_bwd",
    )(ids, seg, tag, q, k, v, do, lse, *parts, *deps)
    return res[0], res[1], res[2], list(res[3:])


def pair_norm(x, ones):
    cen = x.astype(f32) - dg(x, ones, NN)
    inv = lax.rsqrt(dg((cen * cen).astype(bf16), ones, NN) + EPS)
    return cen * inv, inv


def pair_fwd_kernel(U, pair_ref, gain_ref, w_ref, *refs):
    first_ref, second_ref, low = refs[-3:]
    G, T, C = pair_ref.shape
    ones = jnp.full((C, C), 1.0 / C, bf16)

    def rows(i, _):
        x = pair_ref[pl.ds(i * U, U)].reshape(U * T, C)
        n, _ = pair_norm(x, ones)
        y = (n * gain_ref[...]).astype(bf16)
        for u in range(U):
            low[:, pl.ds(pl.multiple_of((i * U + u) * C, 128), C)] = y[u * T : (u + 1) * T]
        return 0

    if U == G:
        rows(0, 0)
    else:
        lax.fori_loop(0, G // U, rows, 0)
    res = dg(w_ref[...], low[...], NT)
    res = res.reshape(res.shape[0] // G, G, T).astype(bf16)
    H = res.shape[0] // 2
    first_ref[...] = res[:H]
    second_ref[...] = res[H:]


def pair_fwd(pair, gain, w_rows, deps=(), U=8):
    R, T, C = pair.shape
    G = 8
    H = w_rows.shape[0] // G
    return pl.pallas_call(
        functools.partial(pair_fwd_kernel, U),
        grid=(R // G,),
        in_specs=[
            pl.BlockSpec((G, T, C), lambda i: (i, 0, 0)),
            pl.BlockSpec((1, C), lambda i: (0, 0)),
            pl.BlockSpec((H * G, G * C), lambda i: (0, 0)),
        ]
        + [ANY] * len(deps),
        out_specs=[pl.BlockSpec((H // 2, G, T), lambda i: (0, i, 0))] * 2,
        out_shape=[jax.ShapeDtypeStruct((H // 2, R, T), bf16)] * 2,
        scratch_shapes=[pltpu.VMEM((T, G * C), bf16)],
        compiler_params=pltpu.CompilerParams(
            dimension_semantics=("arbitrary",), vmem_limit_bytes=40 << 20
        ),
        cost_estimate=cost(R * T * C * 3150, R * T * C * 3, R * T * C),
        name="pair_fwd",
    )(pair, gain, w_rows, *deps)


def pair_bwd_kernel(P, nd, U, pair_ref, gain_ref, wc_ref, *refs):
    firsts, seconds = refs[:P], refs[P : 2 * P]
    out_ref, gw_ref, acc, turned = refs[2 * P + nd :]
    G, T, C = pair_ref.shape
    H = 2 * firsts[0].shape[0]
    ones = jnp.full((C, C), 1.0 / C, bf16)

    @pl.when(pl.program_id(0) == 0)
    def _():
        acc[...] = jnp.zeros_like(acc)

    halves = []
    for parts in (firsts, seconds):
        total = parts[0][...].astype(f32)
        for p in range(1, P):
            total = total + parts[p][...].astype(f32)
        halves.append(total.reshape(H // 2 * G, T))
    flat = jnp.concatenate(halves, axis=0)
    low8 = flat.astype(bf16)
    cols = low8.T
    turned[:, : H * G] = cols
    turned[:, H * G :] = cols

    def rows(i, _):
        x = pair_ref[pl.ds(i * U, U)].reshape(U * T, C)
        n, inv = pair_norm(x, ones)
        low = (n * gain_ref[...]).astype(bf16)
        gs = []
        for u in range(U):
            acc[i * U + u] += dg(low8, low[u * T : (u + 1) * T], NN)
            gs.append(dg(turned[...], wc_ref[i * U + u], NN))
        g = jnp.concatenate(gs, axis=0) if U > 1 else gs[0]
        mean = dg((g * n).astype(bf16), ones, NN)
        out_ref[pl.ds(i * U, U)] = (inv * (g - n * mean)).astype(bf16).reshape(U, T, C)
        return 0

    if U == G:
        rows(0, 0)
    else:
        lax.fori_loop(0, G // U, rows, 0)

    @pl.when(pl.program_id(0) == pl.num_programs(0) - 1)
    def _():
        at = lax.broadcasted_iota(jnp.int32, (H * G, 1), 0) % G
        picked = jnp.zeros((H * G, C), f32)
        for i in range(G):
            picked = picked + jnp.where(at == i, acc[i], 0.0)
        gw_ref[...] = picked


def pair_bwd(pair, gain, wc, firsts, seconds, deps=(), U=8):
    R, T, C = pair.shape
    G = 8
    H = 2 * firsts[0].shape[0]
    P = len(firsts)
    rows = pl.BlockSpec((G, T, C), lambda i: (i, 0, 0))
    return pl.pallas_call(
        functools.partial(pair_bwd_kernel, P, len(deps), U),
        grid=(R // G,),
        in_specs=[
            rows,
            pl.BlockSpec((1, C), lambda i: (0, 0)),
            pl.BlockSpec((G, 2 * H * G, C), lambda i: (0, 0, 0)),
        ]
        + [pl.BlockSpec((H // 2, G, T), lambda i: (0, i, 0))] * (2 * P)
        + [ANY] * len(deps),
        out_specs=[
            rows,
            pl.BlockSpec((H * G, C), lambda i: (0, 0)),
        ],
        out_shape=[
            jax.ShapeDtypeStruct((R, T, C), bf16),
            jax.ShapeDtypeStruct((H * G, C), f32),
        ],
        scratch_shapes=[
            pltpu.VMEM((G, H * G, C), f32),
            pltpu.VMEM((T, 2 * H * G), bf16),
        ],
        compiler_params=pltpu.CompilerParams(
            dimension_semantics=("arbitrary",), vmem_limit_bytes=50 << 20
        ),
        cost_estimate=cost(R * T * C * 5500, R * T * C * 6, R * T * C),
        name="pair_bwd",
    )(pair, gain, wc, *firsts, *seconds, *deps)


def stats_of(x):
    mean = jnp.mean(x, axis=-1, keepdims=True)
    cen = x - mean
    inv = lax.rsqrt(jnp.mean(cen * cen, axis=-1, keepdims=True) + EPS)
    return cen * inv, inv


def sigmoid(x):
    return 1.0 / (1.0 + jnp.exp(-x))


def flat_rows(x):
    return x.reshape(x.shape[0] * x.shape[1], x.shape[2])


def over_samples(x, sb):
    R = x.shape[0] // sb
    total = x[:R]
    for i in range(1, sb):
        total = total + x[i * R : (i + 1) * R]
    return total


def tile_samples(x, sb):
    return x if sb == 1 else jnp.concatenate([x] * sb, axis=0)


def weight_copies(shapes, F, c, f, own, got, swapped, dst, sems):
    copies = []

    def add(src, to):
        copies.append(pltpu.make_async_copy(src, to, sems.at[len(copies)]))

    for i, (r, n) in enumerate(shapes):
        add(own[i], dst[i].at[pl.ds(pl.multiple_of(f * r, 16), r), :])
    for k in range(1, F):
        for packed, half in ((got[k - 1], c), (swapped[k - 1], 1 - c)):
            at = 0
            for i, (r, n) in enumerate(shapes):
                row = pl.multiple_of((f ^ k) * r, 16)
                for b in range(n // 2 // 384):
                    col = pl.multiple_of(half * (n // 2) + b * 384, 128)
                    add(
                        packed.at[pl.ds(at, r), :],
                        dst[i].at[pl.ds(row, r), pl.ds(col, 384)],
                    )
                    at += padded(r)
    return copies


def gathered_copies(shapes, F, c, got, swapped, dst, sems):
    copies = []
    for g in range(F):
        for packed, half in ((got, c), (swapped, 1 - c)):
            at = 0
            for i, (r, n) in enumerate(shapes):
                for b in range(n // 2 // 384):
                    col = pl.multiple_of(half * (n // 2) + b * 384, 128)
                    copies.append(
                        pltpu.make_async_copy(
                            packed.at[g, pl.ds(at, r), :],
                            dst[i].at[pl.ds(g * r, r), pl.ds(col, 384)],
                            sems.at[len(copies)],
                        )
                    )
                    at += padded(r)
    return copies


def padded(r):
    return -(-r // 16) * 16


def packed_rows(shapes):
    return sum(padded(r) * (n // 2 // 384) for r, n in shapes)


def part_map(p, nu):
    return lambda r, u, s: (jnp.where(r == p, u, jnp.where(r < p, 0, nu - 1)), 0, 0)


def part_specs(F, nu, sb, R, D, buffers=2):
    return [
        pl.BlockSpec((sb, R, D), part_map(p, nu), pipeline_mode=pl.Buffered(buffers))
        for p in range(F)
    ]


def choose(parts, scratch):
    for p, ref in enumerate(parts):

        @pl.when(pl.program_id(0) == p)
        def _(ref=ref):
            scratch[...] = ref[...]

    return flat_rows(scratch[...].astype(f32))


def store_part(parts, value):
    for p, ref in enumerate(parts):

        @pl.when(pl.program_id(0) == p)
        def _(ref=ref):
            ref[...] = value


def copies_in_group(shapes, F):
    return len(shapes) + (F - 1) * 2 * sum(n // 2 // 384 for _, n in shapes)


def pack_grads(shapes, F, c, accs, keep_ref, give_ref, stage=None, sems=None):
    copies = []
    for g in range(F):
        for x in copies:
            x.wait()
        at = 0
        for (r, n), acc in zip(shapes, accs):
            for b in range(n // 2 // 384):
                for i, (ref, half) in enumerate(((keep_ref, c), (give_ref, 1 - c))):
                    col = pl.multiple_of(half * (n // 2) + b * 384, 128)
                    block = acc[g * r : (g + 1) * r, pl.ds(col, 384)].astype(bf16)
                    if stage is None:
                        ref[g, at : at + r, :] = block
                    else:
                        stage[i, at : at + r, :] = block
                at += padded(r)
        if stage is not None:
            copies = [
                pltpu.make_async_copy(stage.at[i], ref.at[g], sems.at[i])
                for i, ref in enumerate((keep_ref, give_ref))
            ]
            for x in copies:
                x.start()
    for x in copies:
        x.wait()


def qkvg_kernel(F, shapes, ids, *refs):
    nin = 2 * (F - 1)
    acts, refs = refs[:F], refs[F:]
    cond_ref, bq_ref, wq_hbm = refs[:3]
    got, swapped = refs[3 : 3 + F - 1], refs[3 + F - 1 : 3 + nin]
    q_ref, k_ref, v_ref, g_ref, token_ref, w, xs, sems = refs[3 + nin :]
    token_ref[...] = jnp.zeros_like(token_ref)
    c, f = ids[F], ids[F + 1]

    @pl.when((pl.program_id(0) == 0) & (pl.program_id(1) == 0))
    def _():
        copies = weight_copies(shapes, F, c, f, (wq_hbm,), got, swapped, (w,), sems)
        for x in copies:
            x.start()
        for x in copies:
            x.wait()

    sb, R, D = xs.shape
    n, _ = stats_of(choose(acts, xs))
    scale = tile_samples(sigmoid(cond_ref[:, :D]), sb)
    shift = tile_samples(cond_ref[:, D : 2 * D], sb)
    x = (scale * n + shift).astype(bf16)
    q_ref[...] = (dg(x, w[:, :D], NN) + bq_ref[...]).astype(bf16).reshape(sb, R, D)
    k_ref[...] = dg(x, w[:, D : 2 * D], NN).astype(bf16).reshape(sb, R, D)
    v_ref[...] = dg(x, w[:, 2 * D : 3 * D], NN).astype(bf16).reshape(sb, R, D)
    g_ref[0] = sigmoid(dg(x, w[:, 3 * D :], NN)).reshape(sb, R, D)


def sub_samples(sl, R):
    sb = max(1, min(sl, 256 // R))
    return sb, sl // sb


def qkvg_call(ids, acts, cond, bq, wq, got, swapped):
    F = len(acts)
    sl, R, D = acts[0].shape
    T = F * R
    sb, nu = sub_samples(sl, R)
    shapes = [wq.shape]
    stacked = pl.BlockSpec((1, sb, R, D), lambda r, u, s: (r, u, 0, 0))
    natural = pl.BlockSpec((sb, R, D), lambda r, u, s: (u, s[r], 0))
    return pl.pallas_call(
        functools.partial(qkvg_kernel, F, shapes),
        grid_spec=pltpu.PrefetchScalarGridSpec(
            num_scalar_prefetch=1,
            grid=(F, nu),
            in_specs=part_specs(F, nu, sb, R, D)
            + [
                pl.BlockSpec((R, 2 * D), lambda r, u, s: (s[r], 0)),
                pl.BlockSpec((1, D), lambda r, u, s: (0, 0)),
            ]
            + [ANY] * (1 + 2 * (F - 1)),
            out_specs=[natural] * 3 + [stacked, pl.BlockSpec((1, 128), lambda r, u, s: (0, 0))],
            scratch_shapes=[
                pltpu.VMEM((D, 4 * D), bf16),
                pltpu.VMEM((sb, R, D), bf16),
                pltpu.SemaphoreType.DMA((copies_in_group(shapes, F),)),
            ],
        ),
        out_shape=[jax.ShapeDtypeStruct((sl, T, D), bf16)] * 3
        + [jax.ShapeDtypeStruct((F, sl, R, D), f32), jax.ShapeDtypeStruct((1, 128), f32)],
        compiler_params=pltpu.CompilerParams(
            dimension_semantics=("arbitrary", "arbitrary"), vmem_limit_bytes=60 << 20
        ),
        cost_estimate=cost(19 * sl * T * D * D, 2 * sl * T * D * 6 + 8 * D * D, sl * T * D),
        name="qkvg",
    )(ids, *acts, cond, bq, wq, *got, *swapped)


def middle_kernel(F, shapes, ids, *refs):
    acts, cots, refs = refs[:F], refs[F : 2 * F], refs[2 * F :]
    mix_a, mix_b, gate_ref, gone_ref, ctwo_ref = refs[:5]
    got, swapped = refs[5:7]
    outs, refs = refs[7 : 7 + F], refs[7 + F :]
    (
        da_ref,
        gpg_ref,
        mg_ref,
        ctg_ref,
        gog_ref,
        keep_ref,
        give_ref,
        wo,
        wab,
        wout,
        ao,
        aab,
        aout,
        xs,
        ys,
        stage,
        sems,
        out_sems,
    ) = refs
    c = ids[F]
    first = (pl.program_id(0) == 0) & (pl.program_id(1) == 0)
    last = (pl.program_id(0) == pl.num_programs(0) - 1) & (
        pl.program_id(1) == pl.num_programs(1) - 1
    )

    @pl.when(first)
    def _():
        copies = gathered_copies(shapes, F, c, got, swapped, (wo, wab, wout), sems)
        for x in copies:
            x.start()
        ao[...] = jnp.zeros_like(ao)
        aab[...] = jnp.zeros_like(aab)
        aout[...] = jnp.zeros_like(aout)
        for x in copies:
            x.wait()

    sb, R, D = xs.shape
    H = wout.shape[0]
    gate = flat_rows(gate_ref[0])
    mix = jnp.concatenate([flat_rows(mix_a[...]), flat_rows(mix_b[...])], axis=1)
    branch = (gate * mix).astype(bf16)
    attn_out = dg(branch, wo[...], NN)
    sig_one = sigmoid(gone_ref[...])
    gate_one = tile_samples(sig_one, sb)
    middle = choose(acts, xs) + gate_one * attn_out
    n, inv = stats_of(middle)
    sig_scale = sigmoid(ctwo_ref[:, :D])
    scale = tile_samples(sig_scale, sb)
    x2 = (scale * n + tile_samples(ctwo_ref[:, D : 2 * D], sb)).astype(bf16)
    up = dg(x2, wab[:, H:], NN)
    gp = dg(x2, wab[:, :H], NN)
    sg = sigmoid(gp)
    silu = gp * sg
    hidden = (silu * up).astype(bf16)
    ffn = dg(hidden, wout[...], NN)
    sig_two = sigmoid(ctwo_ref[:, 2 * D :])
    gate_two = tile_samples(sig_two, sb)
    store_part(outs, (middle + gate_two * ffn).astype(bf16).reshape(sb, R, D))

    upstream = choose(cots, ys)
    fg = (upstream * gate_two).astype(bf16)
    g_two = over_samples(upstream * ffn, sb) * (sig_two * (1.0 - sig_two))
    aout[...] += dg(hidden, fg, TN)
    hg = dg(fg, wout[...], NT)
    ga = (hg * up * sg * (1.0 + gp * (1.0 - sg))).astype(bf16)
    gb = (hg * silu).astype(bf16)
    aab[:, :H] += dg(x2, ga, TN)
    aab[:, H:] += dg(x2, gb, TN)
    xg = dg(ga, wab[:, :H], NT) + dg(gb, wab[:, H:], NT)
    g_scale = over_samples(xg * n, sb) * (sig_scale * (1.0 - sig_scale))
    g_shift = over_samples(xg, sb)
    inc = xg * scale
    mg = upstream + inv * (
        inc
        - jnp.mean(inc, axis=-1, keepdims=True)
        - n * jnp.mean(inc * n, axis=-1, keepdims=True)
    )
    mg_ref[0] = mg.reshape(sb, R, D)
    og = (mg * gate_one).astype(bf16)
    g_one = over_samples(mg * attn_out, sb) * (sig_one * (1.0 - sig_one))
    ao[...] += dg(branch, og, TN)
    bg = dg(og, wo[...], NT)
    da_ref[...] = (bg * gate).astype(bf16).reshape(sb, R, D)
    gpg_ref[0] = (bg * mix * (gate * (1.0 - gate))).astype(bf16).reshape(sb, R, D)

    @pl.when(pl.program_id(1) == 0)
    def _():
        ctg_ref[:, :D] = g_scale
        ctg_ref[:, D : 2 * D] = g_shift
        ctg_ref[:, 2 * D :] = g_two
        gog_ref[...] = g_one

    @pl.when(pl.program_id(1) > 0)
    def _():
        ctg_ref[:, :D] += g_scale
        ctg_ref[:, D : 2 * D] += g_shift
        ctg_ref[:, 2 * D :] += g_two
        gog_ref[...] += g_one

    @pl.when(last)
    def _():
        pack_grads(shapes, F, c, (ao, aab, aout), keep_ref, give_ref, stage, out_sems)


def middle_call(ids, acts, cots, mix_a, mix_b, gate, cond_one, cond_two, shapes, got, swapped):
    F = len(acts)
    sl, R, D = acts[0].shape
    T = F * R
    H = shapes[2][0] * F
    sb, nu = sub_samples(sl, R)
    copies = 2 * F * sum(n // 2 // 384 for _, n in shapes)
    rows = packed_rows(shapes)
    stacked = pl.BlockSpec((1, sb, R, D), lambda r, u, s: (r, u, 0, 0))
    natural = pl.BlockSpec((sb, R, D), lambda r, u, s: (u, s[r], 0))
    lanes = pl.BlockSpec((sb, R, D // 2), lambda r, u, s: (u, s[r], 0))
    flops = 12 * sl * T * D * (D + 3 * H)
    res = pl.pallas_call(
        functools.partial(middle_kernel, F, shapes),
        grid_spec=pltpu.PrefetchScalarGridSpec(
            num_scalar_prefetch=1,
            grid=(F, nu),
            in_specs=part_specs(F, nu, sb, R, D) * 2
            + [
                lanes,
                lanes,
                stacked,
                pl.BlockSpec((R, D), lambda r, u, s: (s[r], 2)),
                pl.BlockSpec((R, 3 * D), lambda r, u, s: (s[r], 0)),
            ]
            + [ANY] * 2,
            out_specs=part_specs(F, nu, sb, R, D)
            + [
                natural,
                stacked,
                stacked,
                pl.BlockSpec((R, 3 * D), lambda r, u, s: (s[r], 0)),
                pl.BlockSpec((R, D), lambda r, u, s: (s[r], 0)),
                ANY,
                ANY,
            ],
            scratch_shapes=[
                pltpu.VMEM((D, D), bf16),
                pltpu.VMEM((D, 2 * H), bf16),
                pltpu.VMEM((H, D), bf16),
                pltpu.VMEM((D, D), f32),
                pltpu.VMEM((D, 2 * H), f32),
                pltpu.VMEM((H, D), f32),
                pltpu.VMEM((sb, R, D), bf16),
                pltpu.VMEM((sb, R, D), bf16),
                pltpu.VMEM((2, rows, 384), bf16),
                pltpu.SemaphoreType.DMA((copies,)),
                pltpu.SemaphoreType.DMA((2,)),
            ],
        ),
        out_shape=[jax.ShapeDtypeStruct((sl, R, D), bf16)] * F
        + [
            jax.ShapeDtypeStruct((sl, T, D), bf16),
            jax.ShapeDtypeStruct((F, sl, R, D), bf16),
            jax.ShapeDtypeStruct((F, sl, R, D), f32),
            jax.ShapeDtypeStruct((T, 3 * D), f32),
            jax.ShapeDtypeStruct((T, D), f32),
            jax.ShapeDtypeStruct((F, rows, 384), bf16),
            jax.ShapeDtypeStruct((F, rows, 384), bf16),
        ],
        compiler_params=pltpu.CompilerParams(
            dimension_semantics=("arbitrary", "arbitrary"), vmem_limit_bytes=63 << 20
        ),
        cost_estimate=cost(flops, sl * T * D * 24, sl * T * H),
        name="middle",
    )(ids, *acts, *cots, mix_a, mix_b, gate, cond_one, cond_two, got, swapped)
    return list(res[:F]), *res[F:]


def back_weight_kernel(F, nd, shapes, ids, *refs):
    acts, refs = refs[:F], refs[F:]
    cond_ref, dq_a, dq_b, dk_a, dk_b, dv_a, dv_b, gpg_ref = refs[:8]
    bq_ref, keep_ref, give_ref, acc, xs = refs[8 + nd :]
    D = acts[0].shape[2]
    first = (pl.program_id(0) == 0) & (pl.program_id(1) == 0)
    last = (pl.program_id(0) == pl.num_programs(0) - 1) & (
        pl.program_id(1) == pl.num_programs(1) - 1
    )

    @pl.when(first)
    def _():
        acc[...] = jnp.zeros_like(acc)
        bq_ref[...] = jnp.zeros_like(bq_ref)

    sb = xs.shape[0]
    n, _ = stats_of(choose(acts, xs))
    scale = tile_samples(sigmoid(cond_ref[:, :D]), sb)
    x = (scale * n + tile_samples(cond_ref[:, D : 2 * D], sb)).astype(bf16)
    for i, refs_i in enumerate(((dq_a, dq_b), (dk_a, dk_b), (dv_a, dv_b))):
        g = jnp.concatenate([flat_rows(y[...]) for y in refs_i], axis=1)
        if i == 0:
            bq_ref[...] += jnp.sum(g, axis=0, keepdims=True)
        acc[:, i * D : (i + 1) * D] += dg(x, g.astype(bf16), TN)
    acc[:, 3 * D :] += dg(x, flat_rows(gpg_ref[0]), TN)

    @pl.when(last)
    def _():
        pack_grads(shapes, F, ids[F], (acc,), keep_ref, give_ref)


def back_data_kernel(F, nd, shapes, cshape, ids, *refs):
    nin = 2 * (F - 1)
    acts, refs = refs[:F], refs[F:]
    cond_ref, dq_a, dq_b, dk_a, dk_b, dv_a, dv_b, gpg_ref, mg_ref = refs[:9]
    s_ref, gog_ref, wc_ref, wq_hbm = refs[9:13]
    got, swapped = refs[13 : 13 + F - 1], refs[13 + F - 1 : 13 + nin]
    ags, refs = refs[13 + nin + nd : 13 + nin + nd + F], refs[13 + nin + nd + F :]
    sg_ref, sum_ref, keep_ref, give_ref, w, cg, acc, xs, sems = refs
    c, f = ids[F], ids[F + 1]
    last = (pl.program_id(0) == pl.num_programs(0) - 1) & (
        pl.program_id(1) == pl.num_programs(1) - 1
    )
    first = (pl.program_id(0) == 0) & (pl.program_id(1) == 0)

    @pl.when(first)
    def _():
        copies = weight_copies(shapes, F, c, f, (wq_hbm,), got, swapped, (w,), sems)
        for x in copies:
            x.start()
        for x in copies:
            x.wait()

    sb, R, D = xs.shape
    n, inv = stats_of(choose(acts, xs))
    sig_scale = sigmoid(cond_ref[:, :D])
    scale = tile_samples(sig_scale, sb)
    xg = dg(flat_rows(gpg_ref[0]), w[:, 3 * D :], NT)
    for i, refs_i in enumerate(((dq_a, dq_b), (dk_a, dk_b), (dv_a, dv_b))):
        g = jnp.concatenate([flat_rows(y[...]) for y in refs_i], axis=1).astype(bf16)
        xg = xg + dg(g, w[:, i * D : (i + 1) * D], NT)
    g_scale = over_samples(xg * n, sb) * (sig_scale * (1.0 - sig_scale))
    g_shift = over_samples(xg, sb)
    inc = xg * scale
    ag = flat_rows(mg_ref[0]) + inv * (
        inc
        - jnp.mean(inc, axis=-1, keepdims=True)
        - n * jnp.mean(inc * n, axis=-1, keepdims=True)
    )
    store_part(ags, ag.astype(bf16).reshape(sb, R, D))

    rows = pl.ds(pl.multiple_of(ids[pl.program_id(0)] * R, 16), R)

    @pl.when(pl.program_id(1) == 0)
    def _():
        cg[rows, :D] = g_scale
        cg[rows, D : 2 * D] = g_shift
        cg[rows, 2 * D :] = gog_ref[rows, :]

    @pl.when(pl.program_id(1) > 0)
    def _():
        cg[rows, :D] += g_scale
        cg[rows, D : 2 * D] += g_shift

    @pl.when(last)
    def _():
        cond_grads(F, cshape, c, s_ref, cg[...], wc_ref, sg_ref, sum_ref, keep_ref, give_ref, acc)


def back_weight(ids, acts, cond, dqkv, gpg, wq_shape, deps=()):
    F = len(acts)
    sl, R, D = acts[0].shape
    T = F * R
    sb, nu = sub_samples(sl, R)
    rows = packed_rows([wq_shape])
    stacked = pl.BlockSpec((1, sb, R, D), lambda r, u, s: (r, u, 0, 0))
    lanes = pl.BlockSpec((sb, R, D // 2), lambda r, u, s: (u, s[r], 0))
    whole = pl.BlockSpec((F, rows, 384), lambda r, u, s: (0, 0, 0), pipeline_mode=pl.Buffered(1))
    return pl.pallas_call(
        functools.partial(back_weight_kernel, F, len(deps), [wq_shape]),
        grid_spec=pltpu.PrefetchScalarGridSpec(
            num_scalar_prefetch=1,
            grid=(F, nu),
            in_specs=part_specs(F, nu, sb, R, D)
            + [pl.BlockSpec((R, 2 * D), lambda r, u, s: (s[r], 0))]
            + [lanes] * 6
            + [stacked]
            + [ANY] * len(deps),
            out_specs=[pl.BlockSpec((1, D), lambda r, u, s: (0, 0)), whole, whole],
            scratch_shapes=[pltpu.VMEM((D, 4 * D), f32), pltpu.VMEM((sb, R, D), bf16)],
        ),
        out_shape=[
            jax.ShapeDtypeStruct((1, D), f32),
            jax.ShapeDtypeStruct((F, rows, 384), bf16),
            jax.ShapeDtypeStruct((F, rows, 384), bf16),
        ],
        compiler_params=pltpu.CompilerParams(
            dimension_semantics=("arbitrary", "arbitrary"), vmem_limit_bytes=60 << 20
        ),
        cost_estimate=cost(17 * sl * T * D * D, sl * T * D * 16 + 12 * D * D, sl * T),
        name="back_weight",
    )(ids, *acts, cond, *dqkv, gpg, *deps)


def back_data(ids, acts, cond, dqkv, gpg, mg, s_low, gog, wc, wq, got, swapped, deps=()):
    F = len(acts)
    sl, R, D = acts[0].shape
    T = F * R
    sb, nu = sub_samples(sl, R)
    shapes = [wq.shape]
    C, N = s_low.shape[1], wc.shape[2]
    cshape = (C // F, N)
    crows = packed_rows([cshape])

    def once(shape):
        return pl.BlockSpec(
            shape, lambda r, u, s: (0,) * len(shape), pipeline_mode=pl.Buffered(1)
        )

    outs = [
        jax.ShapeDtypeStruct((T, C), f32),
        jax.ShapeDtypeStruct((1, N), f32),
        jax.ShapeDtypeStruct((F, crows, 384), bf16),
        jax.ShapeDtypeStruct((F, crows, 384), bf16),
    ]
    stacked = pl.BlockSpec((1, sb, R, D), lambda r, u, s: (r, u, 0, 0))
    lanes = pl.BlockSpec((sb, R, D // 2), lambda r, u, s: (u, s[r], 0))
    res = pl.pallas_call(
        functools.partial(back_data_kernel, F, len(deps), shapes, cshape),
        grid_spec=pltpu.PrefetchScalarGridSpec(
            num_scalar_prefetch=1,
            grid=(F, nu),
            in_specs=part_specs(F, nu, sb, R, D)
            + [pl.BlockSpec((R, 2 * D), lambda r, u, s: (s[r], 0))]
            + [lanes] * 6
            + [stacked, stacked]
            + [once(x.shape) for x in (s_low, gog, wc)]
            + [ANY] * (1 + 2 * (F - 1) + len(deps)),
            out_specs=part_specs(F, nu, sb, R, D) + [once(x.shape) for x in outs],
            scratch_shapes=[
                pltpu.VMEM((D, 4 * D), bf16),
                pltpu.VMEM((T, N), f32),
                pltpu.VMEM((C, N), f32),
                pltpu.VMEM((sb, R, D), bf16),
                pltpu.SemaphoreType.DMA((copies_in_group(shapes, F),)),
            ],
        ),
        out_shape=[jax.ShapeDtypeStruct((sl, R, D), bf16)] * F + outs,
        compiler_params=pltpu.CompilerParams(
            dimension_semantics=("arbitrary", "arbitrary"), vmem_limit_bytes=60 << 20
        ),
        cost_estimate=cost(17 * sl * T * D * D, sl * T * D * 22 + 8 * D * D, sl * T),
        name="back_data",
    )(ids, *acts, cond, *dqkv, gpg, mg, s_low, gog, wc, wq, *got, *swapped, *deps)
    return list(res[:F]), *res[F:]


def prepare_kernel(F, nd, groups, ids, *refs):
    xs, refs = refs[:F], refs[F:]
    weights = sum(len(g) for g in groups)
    ws, refs = list(refs[:weights]), refs[weights + nd :]
    for x, out in zip(xs, refs):
        out[...] = x[...]

    @pl.when(pl.program_id(0) == 0)
    def _():
        for shapes, packed in zip(groups, refs[F:]):
            at = 0
            for r, n in shapes:
                w = ws.pop(0)
                for b in range(n // 2 // 384):
                    col = pl.multiple_of(ids[F] * (n // 2) + b * 384, 128)
                    packed[at : at + r, :] = w[:, pl.ds(col, 384)]
                    at += padded(r)


def prepare(ids, x, groups=(), deps=()):
    S, R, D = x.shape
    F = (ids.shape[0] - 2) // 3
    sl = S // F
    steps = 4
    shapes = [[w.shape for w in g] for g in groups]
    rows = [packed_rows(s) for s in shapes]

    def group(p):
        return pl.BlockSpec((sl, R // steps, D), lambda i, s: (s[2 * F + 2 + p], i, 0))

    part = pl.BlockSpec((sl, R // steps, D), lambda i, s: (0, i, 0))
    weights = [w for g in groups for w in g]
    res = pl.pallas_call(
        functools.partial(prepare_kernel, F, len(deps), shapes),
        grid_spec=pltpu.PrefetchScalarGridSpec(
            num_scalar_prefetch=1,
            grid=(steps,),
            in_specs=[group(p) for p in range(F)]
            + [pl.BlockSpec(w.shape, lambda i, s: (0, 0)) for w in weights]
            + [ANY] * len(deps),
            out_specs=[part] * F + [pl.BlockSpec((n, 384), lambda i, s: (0, 0)) for n in rows],
        ),
        out_shape=[jax.ShapeDtypeStruct((sl, R, D), x.dtype)] * F
        + [jax.ShapeDtypeStruct((n, 384), bf16) for n in rows],
        compiler_params=pltpu.CompilerParams(
            dimension_semantics=("arbitrary",), vmem_limit_bytes=40 << 20
        ),
        cost_estimate=cost(5e9, S * R * D * 4),
        name="prepare",
    )(ids, *([x] * F), *weights, *deps)
    return list(res[:F]), *res[F:]


def place_kernel(F, ids, *refs):
    parts, out = refs[:F], refs[-1]
    for p, ref in enumerate(parts):

        @pl.when(pl.program_id(0) == p)
        def _(ref=ref):
            out[...] = ref[...]


def place(ids, parts, deps=()):
    F = len(parts)
    sl, R, D = parts[0].shape

    def fetch(p):
        return pl.BlockSpec((sl, R, D), lambda i, s: (0, 0, 0), pipeline_mode=pl.Buffered(1))

    return pl.pallas_call(
        functools.partial(place_kernel, F),
        grid_spec=pltpu.PrefetchScalarGridSpec(
            num_scalar_prefetch=1,
            grid=(F,),
            in_specs=[fetch(p) for p in range(F)] + [ANY] * len(deps),
            out_specs=pl.BlockSpec((sl, R, D), lambda i, s: (s[2 * F + 2 + i], 0, 0)),
        ),
        out_shape=jax.ShapeDtypeStruct((F * sl, R, D), parts[0].dtype),
        compiler_params=pltpu.CompilerParams(
            dimension_semantics=("arbitrary",), vmem_limit_bytes=40 << 20
        ),
        cost_estimate=cost(4e9, F * sl * R * D * 4),
        name="place",
    )(ids, *parts, *deps)


def terms_kernel(F, n, ids, *refs):
    outs = refs[-F:]
    for p in range(F):

        @pl.when(pl.program_id(0) == p)
        def _(p=p):
            at = 0
            for own, got in zip(refs[:n], refs[n : 2 * n]):
                rows = own.shape[1]
                outs[p][at : at + rows, :] = (own[0].astype(f32) + got[0].astype(f32)).astype(bf16)
                at += rows


def terms(ids, keeps, gots, deps=()):
    F, _, W = keeps[0].shape
    rows = sum(x.shape[1] for x in keeps)
    shards = [
        pl.BlockSpec((1, x.shape[1], W), lambda k, s: (s[F + 1] ^ k, 0, 0)) for x in keeps
    ]
    out = pl.BlockSpec((rows, W), lambda k, s: (0, 0), pipeline_mode=pl.Buffered(1))
    return pl.pallas_call(
        functools.partial(terms_kernel, F, len(keeps)),
        grid_spec=pltpu.PrefetchScalarGridSpec(
            num_scalar_prefetch=1,
            grid=(F,),
            in_specs=shards * 2 + [ANY] * len(deps),
            out_specs=[out] * F,
        ),
        out_shape=[jax.ShapeDtypeStruct((rows, W), bf16)] * F,
        compiler_params=pltpu.CompilerParams(
            dimension_semantics=("arbitrary",), vmem_limit_bytes=40 << 20
        ),
        cost_estimate=cost(5e9, F * rows * W * 6),
        name="terms",
    )(ids, *keeps, *gots, *deps)


def cond_grads(F, shape, c, s_ref, cg, w_ref, sg_ref, sum_ref, keep_ref, give_ref, acc):
    sum_ref[...] = jnp.sum(cg, axis=0, keepdims=True)
    low = cg.astype(bf16)
    acc[...] = dg(s_ref[...], low, TN)
    r = shape[0]
    sg_ref[...] = jnp.concatenate([dg(low, w_ref[g, :r, :], NT) for g in range(F)], axis=1)
    pack_grads([shape], F, c, (acc,), keep_ref, give_ref)


def cond_back_kernel(F, shape, ids, s_ref, cg_ref, w_ref, *refs):
    sg_ref, sum_ref, keep_ref, give_ref, acc = refs[-5:]
    cond_grads(
        F, shape, ids[F], s_ref, cg_ref[...], w_ref, sg_ref, sum_ref, keep_ref, give_ref, acc
    )


def cond_back(ids, s_low, cg, w, F, deps=()):
    T, C = s_low.shape
    N = cg.shape[1]
    shape = (C // F, N)
    rows = packed_rows([shape])
    vmem = pl.BlockSpec(memory_space=pltpu.VMEM)
    return pl.pallas_call(
        functools.partial(cond_back_kernel, F, shape),
        in_specs=[pl.BlockSpec(memory_space=pltpu.SMEM)] + [vmem] * 3 + [ANY] * len(deps),
        out_specs=[vmem] * 4,
        out_shape=[
            jax.ShapeDtypeStruct((T, C), f32),
            jax.ShapeDtypeStruct((1, N), f32),
            jax.ShapeDtypeStruct((F, rows, 384), bf16),
            jax.ShapeDtypeStruct((F, rows, 384), bf16),
        ],
        scratch_shapes=[pltpu.VMEM((C, N), f32)],
        compiler_params=pltpu.CompilerParams(vmem_limit_bytes=50 << 20),
        cost_estimate=cost(8e9, T * N * 4),
        name="cond_back",
    )(ids, s_low, cg, w, *deps)


def unpack_kernel(groups, ids_c, *refs):
    n = len(groups)
    c = ids_c[0]
    outs = list(refs[2 * n :])
    for i, shapes in enumerate(groups):
        at = 0
        for r, cols in shapes:
            out = outs.pop(0)
            for b in range(cols // 2 // 384):
                for ref, half in ((refs[2 * i], c), (refs[2 * i + 1], 1 - c)):
                    col = pl.multiple_of(half * (cols // 2) + b * 384, 128)
                    out[:, pl.ds(col, 384)] = ref[at : at + r, :].astype(f32)
                at += padded(r)


def unpack(c, groups):
    vmem = pl.BlockSpec(memory_space=pltpu.VMEM)
    shapes = [s for _, _, g in groups for s in g]
    return pl.pallas_call(
        functools.partial(unpack_kernel, [g for _, _, g in groups]),
        in_specs=[pl.BlockSpec(memory_space=pltpu.SMEM)] + [vmem] * (2 * len(groups)),
        out_specs=[vmem] * len(shapes),
        out_shape=[jax.ShapeDtypeStruct(s, f32) for s in shapes],
        compiler_params=pltpu.CompilerParams(vmem_limit_bytes=40 << 20),
        cost_estimate=cost(5e9, sum(r * n for r, n in shapes) * 6),
        name="unpack",
    )(c.reshape(1).astype(jnp.int32), *[x for a, b, _ in groups for x in (a, b)])


def cond_fwd_kernel(F, shape, at, natural, ids, single_ref, gain_ref, bias_ref, *refs):
    r, n = shape
    refs, (s_ref, cond_ref, w) = refs[:-3], refs[-3:]
    c, f = ids[F], ids[F + 1]
    step = padded(r)

    def put(g, packed, half):
        for b in range(n // 2 // 384):
            col = pl.multiple_of(half * (n // 2) + b * 384, 128)
            w[g, :r, pl.ds(col, 384)] = packed(at + b * step)

    if natural:
        for g in range(F):
            for ref, half in zip(refs, (c, 1 - c)):
                put(g, lambda row, ref=ref, g=g: ref[g, row : row + r, :], half)
    else:
        w[f, :r, :] = refs[0][...]
        for k in range(1, F):
            for ref, half in ((refs[k], c), (refs[F - 1 + k], 1 - c)):
                put(f ^ k, lambda row, ref=ref: ref[row : row + r, :], half)
    x, _ = stats_of(single_ref[...])
    s_ref[...] = (x * gain_ref[...]).astype(bf16)
    total = bias_ref[...]
    for g in range(F):
        total = total + dg(s_ref[:, g * r : (g + 1) * r], w[g, :r, :], NN)
    cond_ref[...] = total


def cond_fwd(ids, single, gain, bias, shape, at, arrays, natural):
    T, C = single.shape
    r, n = shape
    F = C // r
    vmem = pl.BlockSpec(memory_space=pltpu.VMEM)
    return pl.pallas_call(
        functools.partial(cond_fwd_kernel, F, shape, at, natural),
        in_specs=[pl.BlockSpec(memory_space=pltpu.SMEM)] + [vmem] * (3 + len(arrays)),
        out_specs=[vmem] * 3,
        out_shape=[
            jax.ShapeDtypeStruct((T, C), bf16),
            jax.ShapeDtypeStruct((T, n), f32),
            jax.ShapeDtypeStruct((F, padded(r), n), bf16),
        ],
        compiler_params=pltpu.CompilerParams(vmem_limit_bytes=60 << 20),
        cost_estimate=cost(6e9, T * n * 4),
        name="cond_fwd",
    )(ids, single, gain, bias, *arrays)


class Net:
    def __init__(self, dp, fsdp):
        self.Z, self.F, self.Fh = dp // 2, fsdp, fsdp // 2
        self.z, self.c = lax.axis_index("z"), lax.axis_index("core")
        self.f = lax.axis_index("fsdp")
        self.fh, self.fl = self.f // self.Fh, self.f % self.Fh
        r = jnp.arange(self.F, dtype=jnp.int32)
        blocks = (self.c ^ (r % 2)) * self.Fh + (self.fl ^ (r // 2))
        rows = ((self.c + r // self.Fh) % 2) * self.Fh + (self.fl ^ (r % self.Fh))
        groups = (self.fl ^ (r // 2)) * 2 + (self.fh ^ (r % 2))
        self.ids = jnp.concatenate(
            [blocks, jnp.stack([self.c, self.f]), rows, groups]
        ).astype(jnp.int32)

    def send(self, x, fn):
        F = self.F
        pairs = []
        for z in range(self.Z):
            for c in range(2):
                for f in range(F):
                    z2, c2, f2 = fn(z, c, f)
                    pairs.append(((z * 2 + c) * F + f, (z2 * 2 + c2) * F + f2))
        others = [p for p in pairs if p[0] != p[1]]
        got = lax.ppermute(x, ("z", "core", "fsdp"), others)
        return got if len(others) == len(pairs) else jnp.where(self.c == self.fh, x, got)

    def core_swap(self, x):
        return self.send(x, lambda z, c, f: (z, 1 - c, f))

    def to_owner(self, x, a):
        Fh = self.Fh
        return self.send(x, lambda z, c, f: (z, f // Fh, c * Fh + ((f % Fh) ^ a)))

    def exchange_in(self, parts):
        Fh = self.Fh
        return [
            self.send(
                p,
                lambda z, c, f: (z, (f // Fh) ^ (i % 2), c * Fh + ((f % Fh) ^ (i // 2))),
            )
            for i, p in enumerate(parts)
        ]

    def exchange_out(self, parts):
        Fh = self.Fh
        return [
            self.send(
                p,
                lambda z, c, f: (z, f // Fh, (c ^ (i % 2)) * Fh + ((f % Fh) ^ (i // 2))),
            )
            for i, p in enumerate(parts)
        ]

    def gather_rows(self, x):
        own = [self.to_owner(x, a) for a in range(self.Fh)]
        return own + [self.core_swap(p) for p in own]

    def chip_sum(self, parts):
        Fh = self.Fh
        out = []
        for a in range(Fh):
            got = self.core_swap(parts[Fh + a])
            out.append((parts[a].astype(f32) + got.astype(f32)).astype(got.dtype))
        return out

    def to_owners(self, parts):
        return [self.to_owner(p, a) for a, p in enumerate(parts)]

    def gather_packed(self, packed, *held):
        F = self.F
        got = [self.send(packed, lambda z, c, f: (z, c, f ^ k)) for k in range(1, F)]
        got, *held = tie(got, *held)
        return got, [self.core_swap(g) for g in got], *held

    def plane_send(self, parts):
        return list(parts[:1]) + [
            self.send(parts[k], lambda z, c, f: (z, c, f ^ k)) for k in range(1, self.F)
        ]

    def all_steps(self):
        pairs = [lambda z, c, f: (z, 1 - c, f)]
        bit = 1
        while bit < self.F:
            pairs.append(lambda z, c, f, bit=bit: (z, c, f ^ bit))
            bit *= 2
        bit = 1
        while bit < self.Z:
            pairs.append(lambda z, c, f, bit=bit: (z ^ bit, c, f))
            bit *= 2
        return [lambda x, fn=fn: x + self.send(x, fn) for fn in pairs]

    def z_steps(self):
        def add(x, bit):
            got = self.send(x, lambda z, c, f: (z ^ bit, c, f))
            return (x.astype(f32) + got.astype(f32)).astype(bf16)

        steps, bit = [], 1
        while bit < self.Z:
            steps.append(functools.partial(add, bit=bit))
            bit *= 2
        return steps + [lambda x: (x, self.core_swap(x))]


def total_of(parts):
    return functools.reduce(jnp.add, [p.astype(f32) for p in parts])


def lockstep(*lanes):
    values = [v for v, _ in lanes]
    for i in range(max(len(steps) for _, steps in lanes)):
        values = [steps[i](v) if i < len(steps) else v for v, (_, steps) in zip(values, lanes)]
        values = tie(*values)
    return values


def tie(*xs):
    return lax.optimization_barrier(xs)


def body(
    dp,
    fsdp,
    act,
    single,
    pair,
    segment,
    padding,
    cotangent,
    gain_s1,
    w_cond1,
    b_cond1,
    w_qkvg,
    b_q,
    gain_z,
    w_pair,
    w_o,
    gain_s2,
    w_cond2,
    b_cond2,
    w_ab,
    w_out,
):
    net = Net(dp, fsdp)
    F, ids = net.F, net.ids
    act, single, pair, segment, padding, cotangent = (
        x[0] for x in (act, single, pair, segment, padding, cotangent)
    )
    S, R, D = act.shape
    T = R * F
    COND = single.shape[1]

    vecs = [gain_s1, b_cond1, b_q, gain_z, w_pair, gain_s2, b_cond2]
    sizes = [v.size for v in vecs]
    COND = single.shape[1]
    wide = COND + 128
    vrows = -(-sum(sizes) // (8 * wide)) * 8
    flat = jnp.concatenate([v.reshape(-1) for v in vecs]).astype(f32)
    flat = jnp.pad(flat, (0, vrows * wide - flat.shape[0])).reshape(vrows, wide)
    tag = jnp.where(padding == 1, -1, segment)
    cols = jnp.stack([segment.astype(f32), tag.astype(f32)], axis=1)
    table = jnp.concatenate([single, jnp.pad(cols, ((0, 0), (0, 126)))], axis=1)
    table = jnp.concatenate([table, flat], axis=0)
    table = lax.all_gather(table, ("core", "fsdp"))
    mid_weights = [w_o, w_ab, w_out, w_cond2]
    mid_shapes = [w.shape for w in mid_weights]
    acts, packed, mid_packed = prepare(ids, act, [[w_qkvg, w_cond1], mid_weights])
    acts = net.exchange_in(acts)
    share = mid_packed.shape[0] // net.Z
    mid_got = lax.dynamic_slice_in_dim(mid_packed, net.z * share, share, 0)
    table, mid_got = tie(table, mid_got)
    mid_got = lax.all_gather(mid_got, ("fsdp", "z")).reshape(F, net.Z * share, 384)

    table = lax.dynamic_slice_in_dim(table, net.fh * F, F, 0)
    single_all = table[:, :R, :COND].reshape(T, COND)
    seg_col = table[:, :R, COND].reshape(T, 1)
    tag_row = table[:, :R, COND + 1].reshape(1, T)
    smalls = table[:, R:].reshape(F, vrows * wide)
    full, at = [], 0
    for v, n in zip(vecs, sizes):
        full.append(smalls[:, at : at + n].reshape((F * v.shape[0],) + v.shape[1:]))
        at += n
    gs1, bc1, bq, gz, wp, gs2, bc2 = full

    wt = wp.T
    eye = jnp.eye(8, dtype=f32)
    w_rows = (wt[:, None, None, :] * eye[None, :, :, None]).reshape(HEADS * 8, -1).astype(bf16)
    gz_row = gz.reshape(1, -1)
    bias_a, bias_b = pair_fwd(pair, gz_row, w_rows)
    acts, packed, bias_a, bias_b = tie(acts, packed, bias_a, bias_b)
    one_got, one_swapped, bias_a, bias_b = net.gather_packed(packed, bias_a, bias_b)
    bias_a, bias_b = net.gather_rows(bias_a), net.gather_rows(bias_b)

    single_first, cond_one, wc1 = cond_fwd(
        ids,
        single_all,
        gs1.reshape(1, -1),
        bc1.reshape(1, -1),
        w_cond1.shape,
        packed_rows([w_qkvg.shape]),
        [w_cond1, *one_got, *one_swapped],
        False,
    )
    q, k, v, gate, token = qkvg_call(
        ids, acts, cond_one, bq.reshape(1, D), w_qkvg, one_got, one_swapped
    )

    cots = net.exchange_in(prepare(ids, cotangent, deps=[token])[0])
    mix_a, lse_a = attn_fwd(ids, seg_col, tag_row, q, k, v, bias_a, 0)
    mid_got, mix_a = tie(mid_got, mix_a)
    mid_swapped = net.core_swap(mid_got)
    mix_b, lse_b = attn_fwd(ids, seg_col, tag_row, q, k, v, bias_b, 1)
    single_second, cond_two, wc2 = cond_fwd(
        ids,
        single_all,
        gs2.reshape(1, -1),
        bc2.reshape(1, -1),
        w_cond2.shape,
        packed_rows(mid_shapes[:3]),
        [mid_got, mid_swapped],
        True,
    )
    outs, d_attn, gate_proj, mid_grad, cond_two_grad, gate_one_grad, keep, give = middle_call(
        ids, acts, cots, mix_a, mix_b, gate, cond_one, cond_two, mid_shapes[:3], mid_got, mid_swapped
    )
    outs = net.exchange_out(outs)
    got = net.core_swap(give)
    s_two_grad, grad_b_cond2, keep_c, give_c = cond_back(ids, single_second, cond_two_grad, wc2, F)
    got_c = net.core_swap(give_c)
    mid_sum = []
    for x, y in ((keep, got), (keep_c, got_c)):
        x = (x.astype(f32) + y.astype(f32)).astype(bf16)
        mid_sum.append(jnp.swapaxes(x.reshape(F, net.Z, x.shape[1] // net.Z, 384), 0, 1))
    mid_sum = jnp.concatenate(mid_sum, axis=2)

    dq_a, dk_a, dv_a, db_a = attn_bwd(
        ids, seg_col, tag_row, q, k, v, d_attn, lse_a, bias_a, 0, deps=[mid_sum]
    )
    mid_sum = lax.psum_scatter(mid_sum, "z", scatter_dimension=0)
    outs, db_a = tie(outs, db_a)
    db_a = net.chip_sum(db_a)
    dq_b, dk_b, dv_b, db_b = attn_bwd(
        ids, seg_col, tag_row, q, k, v, d_attn, lse_b, bias_b, 1, deps=db_a
    )
    db_a, db_b, mid_sum = tie(net.to_owners(db_a), db_b, mid_sum)
    db_b = net.chip_sum(db_b)
    mid_sum = net.plane_send(
        [lax.dynamic_index_in_dim(mid_sum, net.f ^ k_, 0, keepdims=False) for k_ in range(F)]
    )
    dqkv = (dq_a, dq_b, dk_a, dk_b, dv_a, dv_b)
    bq_grad, keep, give = back_weight(
        ids, acts, cond_one, dqkv, gate_proj, w_qkvg.shape, deps=db_b
    )
    db_b, give, mid_sum = tie(net.to_owners(db_b), give, mid_sum)
    mid_sum = lax.all_gather(total_of(mid_sum).astype(bf16), "z", axis=0)
    block_out = place(ids, outs, deps=[give])
    wq_parts = terms(ids, [keep], [net.core_swap(give)], deps=[block_out])
    ags, s_one_grad, grad_b_cond1, keep, give = back_data(
        ids,
        acts,
        cond_one,
        dqkv,
        gate_proj,
        mid_grad,
        single_first,
        gate_one_grad,
        wc1,
        w_qkvg,
        one_got,
        one_swapped,
        deps=wq_parts[:1],
    )
    wq_parts, keep, give, ags = tie(net.plane_send(wq_parts), keep, give, ags)
    wq_sum = lax.psum(total_of(wq_parts).astype(bf16), "z")
    late_parts = terms(ids, [keep], [net.core_swap(give)])
    ags = net.exchange_out(ags)

    wc = wt * gz_row
    wc = wc - jnp.mean(wc, axis=1, keepdims=True)
    wc = (wc[None, :, None, :] * eye[:, None, :, None]).reshape(8, HEADS * 8, -1)
    wc_hi = wc.astype(bf16)
    wc = jnp.concatenate([wc_hi, (wc - wc_hi.astype(f32)).astype(bf16)], axis=1)
    pair_grad, gw = pair_bwd(pair, gz_row, wc, db_a, db_b, deps=late_parts[:1])
    late_parts, gw, s_one_grad, mid_sum, wq_sum, ags = tie(
        late_parts, gw, s_one_grad, mid_sum, wq_sum, ags
    )

    s_grad = s_one_grad * gs1 + s_two_grad * gs2
    s_parts = [
        lax.dynamic_slice_in_dim(s_grad, ids[F + 2 + p] * R, R, 0) for p in range(F)
    ]
    flat = [grad_b_cond1, bq_grad, grad_b_cond2, jnp.sum(gw.reshape(HEADS, 8, -1), axis=1)]
    flat = jnp.concatenate([g.reshape(-1, 128) for g in flat], axis=0)
    shares = [packed_rows(mid_shapes[:3]) // net.Z, packed_rows(mid_shapes[3:]) // net.Z]
    mid_sum = jnp.concatenate(
        [mid_sum[:, : shares[0]].reshape(-1, 384), mid_sum[:, shares[0] :].reshape(-1, 384)], axis=0
    )
    late_sum, flat, s_parts, mid_sum, wq_sum = lockstep(
        (late_parts, [lambda x: total_of(net.plane_send(x)).astype(bf16)] + net.z_steps()),
        (flat, net.all_steps()),
        (s_parts, [net.chip_sum, net.to_owners]),
        (mid_sum, [lambda x: (x, net.core_swap(x))]),
        (wq_sum, [lambda x: (x, net.core_swap(x))]),
    )
    total_wo, total_wab, total_wout, total_wc2, total_wq = unpack(
        net.c, [(*mid_sum, mid_shapes), (*wq_sum, [w_qkvg.shape])]
    )
    (total_wc1,) = unpack(net.c, [(*late_sum, [w_cond1.shape])])
    local_n, local_inv = norm_stats(single)
    single_grad = norm_back(local_n, local_inv, functools.reduce(jnp.add, s_parts))[None]
    grad_w_pair = flat[-HEADS:].T
    grad_gain_z = jnp.sum(wp * grad_w_pair, axis=1) / gz
    small, at = [], 0
    for n in (3 * D, D, 3 * D):
        small.append(flat[at // 128 : (at + n) // 128].reshape(-1))
        at += n
    small = [*small[:2], grad_gain_z, grad_w_pair, small[2]]
    total_bc1, total_bq, total_gz, total_wp, total_bc2 = (
        lax.dynamic_slice_in_dim(g, net.f * v_.shape[0], v_.shape[0], 0)
        for g, v_ in zip(small, [b_cond1, b_q, gain_z, w_pair, b_cond2])
    )
    total_gs1, total_gs2 = (
        jnp.sum(w.astype(f32) * g, axis=1) / gain.astype(f32)
        for w, g, gain in ((w_cond1, total_wc1, gain_s1), (w_cond2, total_wc2, gain_s2))
    )
    return (
        block_out[None],
        place(ids, ags, deps=[gw])[None],
        single_grad,
        pair_grad[None],
        total_gs1,
        total_wc1,
        total_bc1,
        total_wq,
        total_bq,
        total_gz,
        total_wp,
        total_wo,
        total_gs2,
        total_wc2,
        total_bc2,
        total_wab,
        total_wout,
    )


def solution(mesh):
    dp, fsdp = mesh.shape["dp"], mesh.shape["fsdp"]
    split = Mesh(mesh.devices.reshape(dp // 2, 2, fsdp), ("z", "core", "fsdp"))
    return jax.shard_map(
        functools.partial(body, dp, fsdp),
        mesh=split,
        in_specs=(
            P(("z", "core"), None, "fsdp", None),
            P(("z", "core"), "fsdp", None),
            P(("z", "core"), "fsdp", None, None),
            P(("z", "core"), "fsdp"),
            P(("z", "core"), "fsdp"),
            P(("z", "core"), None, "fsdp", None),
            P("fsdp"),
            P("fsdp", None),
            P("fsdp"),
            P("fsdp", None),
            P("fsdp"),
            P("fsdp"),
            P("fsdp", None),
            P("fsdp", None),
            P("fsdp"),
            P("fsdp", None),
            P("fsdp"),
            P("fsdp", None),
            P("fsdp", None),
        ),
        out_specs=(
            P(("z", "core"), None, "fsdp", None),
            P(("z", "core"), None, "fsdp", None),
            P(("z", "core"), "fsdp", None),
            P(("z", "core"), "fsdp", None, None),
            P("fsdp"),
            P("fsdp", None),
            P("fsdp"),
            P("fsdp", None),
            P("fsdp"),
            P("fsdp"),
            P("fsdp", None),
            P("fsdp", None),
            P("fsdp"),
            P("fsdp", None),
            P("fsdp"),
            P("fsdp", None),
            P("fsdp", None),
        ),
        check_vma=False,
    )
```

time: 1000 us -> 751 us (0.75)
  waiting for transfers between devices: 321 us -> 102 us
  Pallas kernels: 441 us -> 410 us
  starting transfers between devices: 91.8 us -> 118 us
  matrix products: 15.6 us -> 0 us
  other arithmetic: 55.5 us -> 40.3 us
    ppermute x73 -> x66, waiting for transfers between devices: 320 us -> 84.6 us  [send(): got = lax.ppermute(x, ('z', 'core', 'fsdp'), others)]
    pallas_call x5 -> x19, Pallas kernels: 336 us -> 296 us  [the longest x2 86.1 us: attn_bwd(): pl.pallas_call(functools.partial(attn_bwd_kernel, F, len(deps), min(T, 51...]
    ppermute x73 -> x66, starting transfers between devices: 91.8 us -> 117 us  [send(): got = lax.ppermute(x, ('z', 'core', 'fsdp'), others)]
    all_gather x2 -> x3, waiting for transfers between devices: 0.01 us -> 17.2 us  [the longest x1 17.2 us: body(): table = lax.all_gather(table, ('core', 'fsdp'))]
    dot_general x6 -> x0, matrix products: 15.6 us -> none  [dg(): return lax.dot_general(a, b, dims, preferred_element_type=f32)]
    convert_element_type x25 -> x11, other arithmetic: 27.4 us -> 14.9 us  [the longest x4 8.81 us: chip_sum(): out.append((parts[a].astype(f32) + got.astype(f32)).astype(got.dtype))]
    unnamed x149 -> x147, local copies, waits for them, and re-layouts: 17.3 us -> 24.3 us
  transfers between devices with their start and end apart: 75 -> 71, of which waited for: 24 -> 15; matrix products, arithmetic and copies ran while one was open for 11% -> 7% of each run, Pallas kernels for 36% -> 42%
where the time goes in v2:
time: 751 us; the launch traced here: 745 us
  Pallas kernels  410 us (55%)
  starting transfers between devices  118 us (16%)
  waiting for transfers between devices  102 us (14%)
  local copies, waits for them, and re-layouts  57.1 us (8%)
  other arithmetic  40.3 us (5%)
  between operations  18.1 us (2%)
    ppermute x66, starting transfers between devices, send(): got = lax.ppermute(x, ('z', 'core', 'fsdp'), others)  117 us
    pallas_call x1, Pallas kernels, middle_call(): pl.pallas_call(functools.partial(middle_kernel, F, shapes), grid_spec=plt...  91.7 us
    pallas_call x2, Pallas kernels, attn_bwd(): pl.pallas_call(functools.partial(attn_bwd_kernel, F, len(deps), min(T, 51...  86.1 us
    ppermute x66, waiting for transfers between devices, send(): got = lax.ppermute(x, ('z', 'core', 'fsdp'), others)  84.6 us
    pallas_call x2, Pallas kernels, attn_fwd(): pl.pallas_call(functools.partial(attn_fwd_kernel, F, len(deps), min(T, 25...  51.1 us
    pallas_call x1, Pallas kernels, pair_bwd(): pl.pallas_call(functools.partial(pair_bwd_kernel, P, len(deps), U), grid=...  34.6 us
    pallas_call x1, Pallas kernels, back_data(): pl.pallas_call(functools.partial(back_data_kernel, F, len(deps), shapes,...  30.9 us
    unnamed x147, local copies, waits for them, and re-layouts  24.3 us
  transfers between devices with their start and end apart: 71, of which 15 were waited for; matrix products, arithmetic and copies ran while one was open for 7% of the time, Pallas kernels for 42%

profile of v2, /device:TPU:0, one launch (start us, length us, event | category | flops | bytes accessed | tf_op | source)
XLA Modules:
  0.0 744.7 jit_solution(9216123422660135155)
XLA Ops:
  9.0 4.1 concatenate.26
  28.5 3.5 collective-permute-start.1
  35.3 17.2 %all-gather.7.cloned.1.call-done = f32[1088,512]{1,0:T(8,128)} async-done(((f32[136,512]{1,0:T(8,128)}), f32[1088,512]{1,0:T(8,128)}) %all-gather.7.cloned.1.call-update) | async-done | bytes 2228240 | tf_op jit(solution)/shard_map/all_gather | solution.py:1365
  52.5 4.9 copy.100
  60.8 20.2 %pair_fwd.1 = (bf16[8,128,512]{2,1,0:T(8,128)(2,1)S(1)}, bf16[8,128,512]{2,1,0:T(8,128)(2,1)S(1)}) custom-call(bf16[128,512,128]{2,1,0:T(8,128)(2,1)} %bitcast.110, f32[1,128]{1,0:T(1,128)S(1)} %reshape_reshape.18.gain_ref, bf16[128,1024]{1,0:T(8,128)(2,1)S(1)} %fusion.3.w_ref), custom_call_target="tpu_custom_call" | custom-call | flops 26424115200 | bytes 25165824 | tf_op jit(solution)/shard_map/pair_fwd/pallas_call | solution.py:296
  82.3 7.5 %collective-permute-start.5 = (bf16[1056,384]{1,0:T(8,128)(2,1)S(1)}, bf16[1056,384]{1,0:T(8,128)(2,1)}, u32[]{:S(2)}, u32[]{:S(2)}) collective-permute-start(bf16[1056,384]{1,0:T(8,128)(2,1)S(1)} %get-tuple-element.214), channel_id=1, source_target_pairs={{0,2},{1,3},{2,0},{3,1},{4,6},{5,7},{6,4},{7,5},{8,10},{9,11},{10,... | collective-permute-start | bytes 2433032 | tf_op jit(solution)/shard_map/ppermute | solution.py:1226
  89.8 10.6 %collective-permute-done.4.refs_1_.refs_7_.refs_17_ = bf16[1056,384]{1,0:T(8,128)(2,1)} collective-permute-done((bf16[1056,384]{1,0:T(8,128)(2,1)S(1)}, bf16[1056,384]{1,0:T(8,128)(2,1)}, u32[]{:S(2)}, u32[]{:S(2)}) %collective-permute-start.4) | collective-permute-done | bytes 811040 | tf_op jit(solution)/shard_map/ppermute | solution.py:1226
  100.4 28.4 %collective-permute-done.5.refs_2_.refs_8_.refs_18_ = bf16[1056,384]{1,0:T(8,128)(2,1)} collective-permute-done((bf16[1056,384]{1,0:T(8,128)(2,1)S(1)}, bf16[1056,384]{1,0:T(8,128)(2,1)}, u32[]{:S(2)}, u32[]{:S(2)}) %collective-permute-start.5) | collective-permute-done | bytes 811040 | tf_op jit(solution)/shard_map/ppermute | solution.py:1226
  140.4 8.5 %cond_fwd.2 = (bf16[512,384]{1,0:T(8,128)(2,1)}, f32[512,2304]{1,0:T(8,128)}, bf16[4,96,2304]{2,1,0:T(8,128)(2,1)}) custom-call(s32[14]{0:T(128)} %copy-done.12, f32[512,384]{1,0:T(8,128)} %bitcast.90, f32[1,384]{1,0:T(1,128)} %reshape_reshape.19.gain_ref, f32[1,2304]{1,0:T(1,128)} %reshape_reshape.20.bias_ref, bf16[96,2304]{1,0:T(8,128)(2,1)} %refs_0_.1, ...), custom_call_target="tpu_custom_call" | custom-call | flops 6000000000 | bytes 4718592 | tf_op jit(solution)/shard_map/cond_fwd/pallas_call | solution.py:1188
  149.0 20.3 %collective-permute-start.16 = (bf16[8,128,512]{2,1,0:T(8,128)(2,1)S(1)}, bf16[8,128,512]{2,1,0:T(8,128)(2,1)}, u32[]{:S(2)}, u32[]{:S(2)}) collective-permute-start(bf16[8,128,512]{2,1,0:T(8,128)(2,1)S(1)} %broadcast_select_fusion.3.refs_0_), channel_id=1, source_target_pairs={{0,4},{1,5},{2,6},{3,7},{4,0},{5,1},{6,2},{7,3},{8,12},{9,13},{10,... | collective-permute-start | bytes 3145736 | tf_op jit(solution)/shard_map/ppermute | solution.py:1226
  170.5 21.6 %qkvg.1 = (bf16[4,512,768]{2,1,0:T(8,128)(2,1)}, bf16[4,512,768]{2,1,0:T(8,128)(2,1)}, bf16[4,512,768]{2,1,0:T(8,128)(2,1)}, f32[4,4,128,768]{3,2,1,0:T(8,128)}, f32[1,128]{1,0:T(1,128)}) custom-call(s32[14]{0:T(128)} %copy-done.12, bf16[4,128,768]{2,1,0:T(8,128)(2,1)} %broadcast_select_fusion.7.refs_0_, ...), custom_call_target="tpu_custom_call" | custom-call | flops 22951231488 | bytes 23592960 | tf_op jit(solution)/shard_map/qkvg/pallas_call | solution.py:580
  193.1 25.6 %attn_fwd.2 = (f32[4,512,384]{2,1,0:T(8,128)}, f32[4,512,128]{2,1,0:T(8,128)}) custom-call(s32[14]{0:T(128)} %copy-done.12, f32[512,1]{1,0:T(8,128)} %copy.105.seg_ref, f32[1,512]{1,0:T(1,128)} %bitcast.106, bf16[4,512,768]{2,1,0:T(8,128)(2,1)} %get-tuple-element.227.q_ref, bf16[4,512,768]{2,1,0:T(8,128)(2,1)} %get-tuple-element.228.k_ref, ...), custom_call_target="tpu_custom_call" | custom-call | flops 31037849600 | bytes 12058624 | tf_op jit(solution)/shard_map/attn_fwd/pallas_call | solution.py:123
  229.5 15.3 %collective-permute-done.19.refs_1_ = bf16[8,128,512]{2,1,0:T(8,128)(2,1)} collective-permute-done((bf16[8,128,512]{2,1,0:T(8,128)(2,1)S(1)}, bf16[8,128,512]{2,1,0:T(8,128)(2,1)}, u32[]{:S(2)}, u32[]{:S(2)}) %collective-permute-start.19) | collective-permute-done | bytes 1048608 | tf_op jit(solution)/shard_map/ppermute | solution.py:1226
  253.0 25.5 %attn_fwd.3 = (f32[4,512,384]{2,1,0:T(8,128)}, f32[4,512,128]{2,1,0:T(8,128)}) custom-call(s32[14]{0:T(128)} %copy-done.12, f32[512,1]{1,0:T(8,128)} %copy.105.seg_ref, f32[1,512]{1,0:T(1,128)} %bitcast.107, bf16[4,512,768]{2,1,0:T(8,128)(2,1)} %get-tuple-element.227.q_ref, bf16[4,512,768]{2,1,0:T(8,128)(2,1)} %get-tuple-element.228.k_ref, ...), custom_call_target="tpu_custom_call" | custom-call | flops 31037849600 | bytes 12058624 | tf_op jit(solution)/shard_map/attn_fwd/pallas_call | solution.py:123
  278.5 10.0 %cond_fwd.3 = (bf16[512,384]{1,0:T(8,128)(2,1)}, f32[512,2304]{1,0:T(8,128)}, bf16[4,96,2304]{2,1,0:T(8,128)(2,1)}) custom-call(s32[14]{0:T(128)} %copy-done.12, f32[512,384]{1,0:T(8,128)} %bitcast.91, f32[1,384]{1,0:T(1,128)} %reshape_reshape.22.gain_ref, f32[1,2304]{1,0:T(1,128)} %reshape_reshape.23.bias_ref, bf16[4,1632,384]{2,1,0:T(8,128)(2,1)} %bitcast.113, ...), custom_call_target="tpu_custom_call" | custom-call | flops 6000000000 | bytes 4718592 | tf_op jit(solution)/shard_map/cond_fwd/pallas_call | solution.py:1188
  289.3 91.7 %middle.1 = (bf16[4,128,768]{2,1,0:T(8,128)(2,1)}, bf16[4,128,768]{2,1,0:T(8,128)(2,1)}, bf16[4,128,768]{2,1,0:T(8,128)(2,1)}, bf16[4,128,768]{2,1,0:T(8,128)(2,...) custom-call(s32[14]{0:T(128)} %copy-done.12, ...), custom_call_target="tpu_custom_call" | custom-call | flops 101468602368 | bytes 37748736 | tf_op jit(solution)/shard_map/middle/pallas_call | solution.py:730
  382.2 6.8 cond_back.1
  394.0 3.5 collective-permute-start.26
  404.2 43.0 %attn_bwd.2 = (f32[4,512,384]{2,1,0:T(8,128)}, bf16[4,512,384]{2,1,0:T(8,128)(2,1)}, bf16[4,512,384]{2,1,0:T(8,128)(2,1)}, bf16[8,128,512]{2,1,0:T(8,128)(2,1)},...) custom-call(s32[14]{0:T(128)} %copy-done.12, f32[512,1]{1,0:T(8,128)} %copy.105.seg_ref, ...), custom_call_target="tpu_custom_call" | custom-call | flops 52009369600 | bytes 20971520 | tf_op jit(solution)/shard_map/attn_bwd/pallas_call | solution.py:230
  455.9 43.1 %attn_bwd.3 = (f32[4,512,384]{2,1,0:T(8,128)}, bf16[4,512,384]{2,1,0:T(8,128)(2,1)}, bf16[4,512,384]{2,1,0:T(8,128)(2,1)}, bf16[8,128,512]{2,1,0:T(8,128)(2,1)},...) custom-call(s32[14]{0:T(128)} %copy-done.12, f32[512,1]{1,0:T(8,128)} %copy.105.seg_ref, ...), custom_call_target="tpu_custom_call" | custom-call | flops 52009369600 | bytes 20971520 | tf_op jit(solution)/shard_map/attn_bwd/pallas_call | solution.py:230
  516.5 22.2 %back_weight.1 = (f32[1,768]{1,0:T(1,128)}, bf16[4,768,384]{2,1,0:T(8,128)(2,1)}, bf16[4,768,384]{2,1,0:T(8,128)(2,1)}) custom-call(s32[14]{0:T(128)} %copy-done.12, bf16[4,128,768]{2,1,0:T(8,128)(2,1)} %broadcast_select_fusion.7.refs_0_, bf16[4,128,768]{2,1,0:T(8,128)(2,1)} %collective-permute-done.1.refs_1_, ...), custom_call_target="tpu_custom_call" | custom-call | flops 20535312384 | bytes 32243712 | tf_op jit(solution)/shard_map/back_weight/pallas_call | solution.py:885
  540.2 3.7 collective-permute-done.36.refs_3_
  552.8 4.4 place.2.refs_2_
  559.2 4.3 terms.2
  567.8 30.9 %back_data.1 = (bf16[4,128,768]{2,1,0:T(8,128)(2,1)}, bf16[4,128,768]{2,1,0:T(8,128)(2,1)}, bf16[4,128,768]{2,1,0:T(8,128)(2,1)}, bf16[4,128,768]{2,1,0:T(8,128)...) custom-call(s32[14]{0:T(128)} %copy-done.12, ...), custom_call_target="tpu_custom_call" | custom-call | flops 20535312384 | bytes 39321600 | tf_op jit(solution)/shard_map/back_data/pallas_call | solution.py:934
  617.1 34.6 %pair_bwd.1 = (bf16[128,512,128]{2,1,0:T(8,128)(2,1)}, f32[128,128]{1,0:T(8,128)S(1)}) custom-call(bf16[128,512,128]{2,1,0:T(8,128)(2,1)} %bitcast.111, f32[1,128]{1,0:T(1,128)S(1)} %copy-done.11, bf16[8,256,128]{2,1,0:T(8,128)(2,1)S(1)} %pad_maximum_fusion.2.wc_ref, bf16[8,128,512]{2,1,0:T(8,128)(2,1)S(1)} %broadcast_select_fusion.1.refs_0_, ...), custom_call_target="tpu_custom_call" | custom-call | flops 46137344000 | bytes 50331648 | tf_op jit(solution)/shard_map/pair_bwd/pallas_call | solution.py:372
  655.0 14.4 %collective-permute-start.55 = (bf16[1632,384]{1,0:T(8,128)(2,1)S(1)}, bf16[1632,384]{1,0:T(8,128)(2,1)}, u32[]{:S(2)}, u32[]{:S(2)}) collective-permute-start(bf16[1632,384]{1,0:T(8,128)(2,1)S(1)} %pad_maximum_fusion.1.refs_0_), channel_id=1, source_target_pairs={{0,4},{1,5},{2,6},{3,7},{4,0},{5,1},{6,2},{7,3},{8,12},{9,13},{10,... | collective-permute-start | bytes 3760136 | tf_op jit(solution)/shard_map/ppermute | solution.py:1226
  681.6 5.0 collective-permute-done.50
  706.4 6.1 collective-permute-done.61
  712.9 4.1 collective-permute-done.64
  718.7 4.3 place.3
  723.5 4.7 unpack.3
  (400 shorter events, 176.4 us)
Async XLA Ops:
  7.2 45.3 %all-gather.7.cloned.1.call-start = ((), (), s32[]{:S(2)}) async-start(), calls=%async_computation.3 | async-start | bytes 2506752 | tf_op jit(solution)/shard_map/all_gather | solution.py:1365
  14.8 204.0 %all-gather.9.cloned.1.call-start = ((), (), s32[]{:S(2)}) async-start(), calls=%async_computation.4 | async-start | bytes 5326848 | tf_op jit(solution)/shard_map/all_gather | solution.py:1373
  28.5 52.6 %collective-permute-start.1 = (bf16[4,128,768]{2,1,0:T(8,128)(2,1)}, bf16[4,128,768]{2,1,0:T(8,128)(2,1)}, u32[]{:S(2)}, u32[]{:S(2)}) collective-permute-start(bf16[4,128,768]{2,1,0:T(8,128)(2,1)} %get-tuple-element.202), channel_id=1, source_target_pairs={{0,4},{1,5},{2,0},{3,1},{4,6},{5,7},{6,2},{7,3},{8,12},{9,13},{10,... | collective-permute-start | bytes 2359304 | tf_op jit(solution)/shard_map/ppermute | solution.py:1226
  32.0 49.1 %collective-permute-start.2 = (bf16[4,128,768]{2,1,0:T(8,128)(2,1)}, bf16[4,128,768]{2,1,0:T(8,128)(2,1)}, u32[]{:S(2)}, u32[]{:S(2)}) collective-permute-start(bf16[4,128,768]{2,1,0:T(8,128)(2,1)} %get-tuple-element.203), channel_id=1, source_target_pairs={{0,1},{1,0},{2,5},{3,4},{4,3},{5,2},{6,7},{7,6},{8,9},{9,8},{10,13... | collective-permute-start | bytes 2359304 | tf_op jit(solution)/shard_map/ppermute | solution.py:1226
  33.5 47.6 %collective-permute-start.3 = (bf16[4,128,768]{2,1,0:T(8,128)(2,1)}, bf16[4,128,768]{2,1,0:T(8,128)(2,1)}, u32[]{:S(2)}, u32[]{:S(2)}) collective-permute-start(bf16[4,128,768]{2,1,0:T(8,128)(2,1)} %get-tuple-element.204), channel_id=1, source_target_pairs={{0,5},{1,4},{2,1},{3,0},{4,7},{5,6},{6,3},{7,2},{8,13},{9,12},{10,... | collective-permute-start | bytes 2359304 | tf_op jit(solution)/shard_map/ppermute | solution.py:1226
  60.4 440.1 %reduce-scatter.2.cloned.1.call-start = ((), (), s32[]{:S(2)}) async-start(), calls=%async_computation.1 | async-start | bytes 6266880 | tf_op jit(solution)/shard_map/reduce_scatter | solution.py:1440
  82.3 46.5 %collective-permute-start.5 = (bf16[1056,384]{1,0:T(8,128)(2,1)S(1)}, bf16[1056,384]{1,0:T(8,128)(2,1)}, u32[]{:S(2)}, u32[]{:S(2)}) collective-permute-start(bf16[1056,384]{1,0:T(8,128)(2,1)S(1)} %get-tuple-element.214), channel_id=1, source_target_pairs={{0,2},{1,3},{2,0},{3,1},{4,6},{5,7},{6,4},{7,5},{8,10},{9,11},{10,... | collective-permute-start | bytes 2433032 | tf_op jit(solution)/shard_map/ppermute | solution.py:1226
  89.8 39.0 %collective-permute-start.6 = (bf16[1056,384]{1,0:T(8,128)(2,1)S(1)}, bf16[1056,384]{1,0:T(8,128)(2,1)}, u32[]{:S(2)}, u32[]{:S(2)}) collective-permute-start(bf16[1056,384]{1,0:T(8,128)(2,1)S(1)} %get-tuple-element.214), channel_id=1, source_target_pairs={{0,3},{1,2},{2,1},{3,0},{4,7},{5,6},{6,5},{7,4},{8,11},{9,10},{10,... | collective-permute-start | bytes 2433032 | tf_op jit(solution)/shard_map/ppermute | solution.py:1226
  131.1 38.3 %collective-permute-start.15 = (bf16[8,128,512]{2,1,0:T(8,128)(2,1)S(1)}, bf16[8,128,512]{2,1,0:T(8,128)(2,1)}, u32[]{:S(2)}, u32[]{:S(2)}) collective-permute-start(bf16[8,128,512]{2,1,0:T(8,128)(2,1)S(1)} %get-tuple-element.230), channel_id=1, source_target_pairs={{0,1},{1,0},{2,5},{3,4},{4,3},{5,2},{6,7},{7,6},{8,9},{9,8},{10,13... | collective-permute-start | bytes 3145736 | tf_op jit(solution)/shard_map/ppermute | solution.py:1226
  138.6 87.0 %collective-permute-start.18 = (bf16[8,128,512]{2,1,0:T(8,128)(2,1)S(1)}, bf16[8,128,512]{2,1,0:T(8,128)(2,1)}, u32[]{:S(2)}, u32[]{:S(2)}) collective-permute-start(bf16[8,128,512]{2,1,0:T(8,128)(2,1)S(1)} %get-tuple-element.233), channel_id=1, source_target_pairs={{2,4},{3,5},{4,2},{5,3},{10,12},{11,13},{12,10},{13,11},{18,20},{1... | collective-permute-start | bytes 3145736 | tf_op jit(solution)/shard_map/ppermute | solution.py:1226
  149.0 43.1 %collective-permute-start.16 = (bf16[8,128,512]{2,1,0:T(8,128)(2,1)S(1)}, bf16[8,128,512]{2,1,0:T(8,128)(2,1)}, u32[]{:S(2)}, u32[]{:S(2)}) collective-permute-start(bf16[8,128,512]{2,1,0:T(8,128)(2,1)S(1)} %broadcast_select_fusion.3.refs_0_), channel_id=1, source_target_pairs={{0,4},{1,5},{2,6},{3,7},{4,0},{5,1},{6,2},{7,3},{8,12},{9,13},{10,... | collective-permute-start | bytes 3145736 | tf_op jit(solution)/shard_map/ppermute | solution.py:1226
  218.8 59.7 %collective-permute-start.22 = (bf16[4,1632,384]{2,1,0:T(8,128)(2,1)}, bf16[4,1632,384]{2,1,0:T(8,128)(2,1)}, u32[]{:S(2)}, u32[]{:S(2)}) collective-permute-start(bf16[4,1632,384]{2,1,0:T(8,128)(2,1)} %bitcast.112), channel_id=1, source_target_pairs={{0,4},{1,5},{2,6},{3,7},{4,0},{5,1},{6,2},{7,3},{8,12},{9,13},{10,... | collective-permute-start | bytes 15040520 | tf_op jit(solution)/shard_map/ppermute | solution.py:1226
  246.4 42.0 %collective-permute-start.11 = (bf16[4,128,768]{2,1,0:T(8,128)(2,1)}, bf16[4,128,768]{2,1,0:T(8,128)(2,1)}, u32[]{:S(2)}, u32[]{:S(2)}) collective-permute-start(bf16[4,128,768]{2,1,0:T(8,128)(2,1)} %copy-done.21), channel_id=1, source_target_pairs={{0,4},{1,5},{2,0},{3,1},{4,6},{5,7},{6,2},{7,3},{8,12},{9,13},{10,... | collective-permute-start | bytes 2359304 | tf_op jit(solution)/shard_map/ppermute | solution.py:1226
  246.6 41.8 %collective-permute-start.12 = (bf16[4,128,768]{2,1,0:T(8,128)(2,1)S(1)}, bf16[4,128,768]{2,1,0:T(8,128)(2,1)}, u32[]{:S(2)}, u32[]{:S(2)}) collective-permute-start(bf16[4,128,768]{2,1,0:T(8,128)(2,1)S(1)} %get-tuple-element.224), channel_id=1, source_target_pairs={{0,1},{1,0},{2,5},{3,4},{4,3},{5,2},{6,7},{7,6},{8,9},{9,8},{10,13... | collective-permute-start | bytes 2359304 | tf_op jit(solution)/shard_map/ppermute | solution.py:1226
  249.6 38.9 %collective-permute-start.13 = (bf16[4,128,768]{2,1,0:T(8,128)(2,1)S(1)}, bf16[4,128,768]{2,1,0:T(8,128)(2,1)S(1)}, u32[]{:S(2)}, u32[]{:S(2)}) collective-permute-start(bf16[4,128,768]{2,1,0:T(8,128)(2,1)S(1)} %get-tuple-element.225), channel_id=1, source_target_pairs={{0,5},{1,4},{2,1},{3,0},{4,7},{5,6},{6,3},{7,2},{8,13},{9,12},{10,... | collective-permute-start | bytes 2359304 | tf_op jit(solution)/shard_map/ppermute | solution.py:1226
  391.6 55.6 %collective-permute-start.24 = (bf16[4,128,768]{2,1,0:T(8,128)(2,1)}, bf16[4,128,768]{2,1,0:T(8,128)(2,1)}, u32[]{:S(2)}, u32[]{:S(2)}) collective-permute-start(bf16[4,128,768]{2,1,0:T(8,128)(2,1)} %get-tuple-element.239), channel_id=1, source_target_pairs={{0,2},{1,3},{2,6},{3,7},{4,0},{5,1},{6,4},{7,5},{8,10},{9,11},{10,... | collective-permute-start | bytes 2359304 | tf_op jit(solution)/shard_map/ppermute | solution.py:1226
  392.3 54.9 %collective-permute-start.25 = (bf16[4,128,768]{2,1,0:T(8,128)(2,1)}, bf16[4,128,768]{2,1,0:T(8,128)(2,1)}, u32[]{:S(2)}, u32[]{:S(2)}) collective-permute-start(bf16[4,128,768]{2,1,0:T(8,128)(2,1)} %get-tuple-element.240), channel_id=1, source_target_pairs={{0,1},{1,0},{2,5},{3,4},{4,3},{5,2},{6,7},{7,6},{8,9},{9,8},{10,13... | collective-permute-start | bytes 2359304 | tf_op jit(solution)/shard_map/ppermute | solution.py:1226
  394.0 53.2 %collective-permute-start.26 = (bf16[4,128,768]{2,1,0:T(8,128)(2,1)}, bf16[4,128,768]{2,1,0:T(8,128)(2,1)}, u32[]{:S(2)}, u32[]{:S(2)}) collective-permute-start(bf16[4,128,768]{2,1,0:T(8,128)(2,1)} %get-tuple-element.241), channel_id=1, source_target_pairs={{0,3},{1,2},{2,7},{3,6},{4,1},{5,0},{6,5},{7,4},{8,11},{9,10},{10,... | collective-permute-start | bytes 2359304 | tf_op jit(solution)/shard_map/ppermute | solution.py:1226
  404.1 248.3 %all-gather.11.cloned.1.call-start = ((), (), s32[]{:S(2)}) async-start(), calls=%async_computation.5 | async-start | bytes 1566720 | tf_op jit(solution)/shard_map/all_gather | solution.py:1456
  452.7 47.7 %collective-permute-start.32 = (bf16[8,128,512]{2,1,0:T(8,128)(2,1)}, bf16[8,128,512]{2,1,0:T(8,128)(2,1)}, u32[]{:S(2)}, u32[]{:S(2)}) collective-permute-start(bf16[8,128,512]{2,1,0:T(8,128)(2,1)} %add_convert_fusion.3.refs_5_), channel_id=1, source_target_pairs={{0,1},{1,0},{2,5},{3,4},{4,3},{5,2},{6,7},{7,6},{8,9},{9,8},{10,13... | collective-permute-start | bytes 3145736 | tf_op jit(solution)/shard_map/ppermute | solution.py:1226
  454.0 45.0 %collective-permute-start.30 = (bf16[8,128,512]{2,1,0:T(8,128)(2,1)}, bf16[8,128,512]{2,1,0:T(8,128)(2,1)}, u32[]{:S(2)}, u32[]{:S(2)}) collective-permute-start(bf16[8,128,512]{2,1,0:T(8,128)(2,1)} %add_convert_fusion.4.refs_4_), channel_id=1, source_target_pairs={{2,4},{3,5},{4,2},{5,3},{10,12},{11,13},{12,10},{13,11},{18,20},{1... | collective-permute-start | bytes 3145736 | tf_op jit(solution)/shard_map/ppermute | solution.py:1226
  504.3 35.9 %collective-permute-start.37 = (bf16[408,384]{1,0:T(8,128)(2,1)}, bf16[408,384]{1,0:T(8,128)(2,1)}, u32[]{:S(2)}, u32[]{:S(2)}) collective-permute-start(bf16[408,384]{1,0:T(8,128)(2,1)} %get-tuple-element.460), channel_id=1, source_target_pairs={{0,1},{1,0},{2,3},{3,2},{4,5},{5,4},{6,7},{7,6},{8,9},{9,8},{10,11... | collective-permute-start | bytes 940040 | tf_op jit(solution)/shard_map/ppermute | solution.py:1226
  506.4 33.8 %collective-permute-start.38 = (bf16[408,384]{1,0:T(8,128)(2,1)}, bf16[408,384]{1,0:T(8,128)(2,1)}, u32[]{:S(2)}, u32[]{:S(2)}) collective-permute-start(bf16[408,384]{1,0:T(8,128)(2,1)} %get-tuple-element.459), channel_id=1, source_target_pairs={{0,2},{1,3},{2,0},{3,1},{4,6},{5,7},{6,4},{7,5},{8,10},{9,11},{10,... | collective-permute-start | bytes 940040 | tf_op jit(solution)/shard_map/ppermute | solution.py:1226
  507.4 32.8 %collective-permute-start.39 = (bf16[408,384]{1,0:T(8,128)(2,1)S(1)}, bf16[408,384]{1,0:T(8,128)(2,1)}, u32[]{:S(2)}, u32[]{:S(2)}) collective-permute-start(bf16[408,384]{1,0:T(8,128)(2,1)S(1)} %get-tuple-element.458), channel_id=1, source_target_pairs={{0,3},{1,2},{2,1},{3,0},{4,7},{5,6},{6,5},{7,4},{8,11},{9,10},{10,... | collective-permute-start | bytes 940040 | tf_op jit(solution)/shard_map/ppermute | solution.py:1226
  510.4 33.6 %collective-permute-start.36 = (bf16[8,128,512]{2,1,0:T(8,128)(2,1)}, bf16[8,128,512]{2,1,0:T(8,128)(2,1)}, u32[]{:S(2)}, u32[]{:S(2)}) collective-permute-start(bf16[8,128,512]{2,1,0:T(8,128)(2,1)} %add_convert_fusion.1.refs_13_), channel_id=1, source_target_pairs={{0,1},{1,0},{2,5},{3,4},{4,3},{5,2},{6,7},{7,6},{8,9},{9,8},{10,13... | collective-permute-start | bytes 3145736 | tf_op jit(solution)/shard_map/ppermute | solution.py:1226
  552.5 100.0 %all-reduce.4.cloned.1.call-start = ((), (), s32[]{:S(2)}) async-start(), calls=%async_computation.2 | async-start | bytes 1179648 | tf_op jit(solution)/shard_map/psum | solution.py:1475
  564.3 34.4 %collective-permute-start.41 = (bf16[768,384]{1,0:T(8,128)(2,1)}, bf16[768,384]{1,0:T(8,128)(2,1)}, u32[]{:S(2)}, u32[]{:S(2)}) collective-permute-start(bf16[768,384]{1,0:T(8,128)(2,1)} %get-tuple-element.284), channel_id=1, source_target_pairs={{0,1},{1,0},{2,3},{3,2},{4,5},{5,4},{6,7},{7,6},{8,9},{9,8},{10,11... | collective-permute-start | bytes 1769480 | tf_op jit(solution)/shard_map/ppermute | solution.py:1226
  564.3 34.4 %collective-permute-start.42 = (bf16[768,384]{1,0:T(8,128)(2,1)}, bf16[768,384]{1,0:T(8,128)(2,1)}, u32[]{:S(2)}, u32[]{:S(2)}) collective-permute-start(bf16[768,384]{1,0:T(8,128)(2,1)} %get-tuple-element.285), channel_id=1, source_target_pairs={{0,2},{1,3},{2,0},{3,1},{4,6},{5,7},{6,4},{7,5},{8,10},{9,11},{10,... | collective-permute-start | bytes 1769480 | tf_op jit(solution)/shard_map/ppermute | solution.py:1226
  604.3 48.2 %collective-permute-start.46 = (bf16[4,128,768]{2,1,0:T(8,128)(2,1)}, bf16[4,128,768]{2,1,0:T(8,128)(2,1)}, u32[]{:S(2)}, u32[]{:S(2)}) collective-permute-start(bf16[4,128,768]{2,1,0:T(8,128)(2,1)} %get-tuple-element.318), channel_id=1, source_target_pairs={{0,2},{1,3},{2,6},{3,7},{4,0},{5,1},{6,4},{7,5},{8,10},{9,11},{10,... | collective-permute-start | bytes 2359304 | tf_op jit(solution)/shard_map/ppermute | solution.py:1226
  604.3 48.2 %collective-permute-start.47 = (bf16[4,128,768]{2,1,0:T(8,128)(2,1)}, bf16[4,128,768]{2,1,0:T(8,128)(2,1)}, u32[]{:S(2)}, u32[]{:S(2)}) collective-permute-start(bf16[4,128,768]{2,1,0:T(8,128)(2,1)} %get-tuple-element.319), channel_id=1, source_target_pairs={{0,1},{1,0},{2,5},{3,4},{4,3},{5,2},{6,7},{7,6},{8,9},{9,8},{10,13... | collective-permute-start | bytes 2359304 | tf_op jit(solution)/shard_map/ppermute | solution.py:1226
  605.4 47.1 %collective-permute-start.48 = (bf16[4,128,768]{2,1,0:T(8,128)(2,1)}, bf16[4,128,768]{2,1,0:T(8,128)(2,1)}, u32[]{:S(2)}, u32[]{:S(2)}) collective-permute-start(bf16[4,128,768]{2,1,0:T(8,128)(2,1)} %get-tuple-element.320), channel_id=1, source_target_pairs={{0,3},{1,2},{2,7},{3,6},{4,1},{5,0},{6,5},{7,4},{8,11},{9,10},{10,... | collective-permute-start | bytes 2359304 | tf_op jit(solution)/shard_map/ppermute | solution.py:1226
  655.0 32.9 %collective-permute-start.55 = (bf16[1632,384]{1,0:T(8,128)(2,1)S(1)}, bf16[1632,384]{1,0:T(8,128)(2,1)}, u32[]{:S(2)}, u32[]{:S(2)}) collective-permute-start(bf16[1632,384]{1,0:T(8,128)(2,1)S(1)} %pad_maximum_fusion.1.refs_0_), channel_id=1, source_target_pairs={{0,4},{1,5},{2,6},{3,7},{4,0},{5,1},{6,2},{7,3},{8,12},{9,13},{10,... | collective-permute-start | bytes 3760136 | tf_op jit(solution)/shard_map/ppermute | solution.py:1226
  (111 other events, 1395.0 us)
Sparse Core Ops, SparseCore 0:
  14.9 37.5 all-gather.6
  60.5 110.6 all-gather.8
  404.2 89.6 reduce-scatter.1
  552.6 31.5 all-gather.10
  610.0 38.7 all-reduce.3

commit v3 on v2

--- a/solution.py
+++ b/solution.py
@@ -487,10 +487,23 @@
     ]
 
 
-def choose(parts, scratch):
-    for p, ref in enumerate(parts):
-
-        @pl.when(pl.program_id(0) == p)
+def arrived_specs(F, nu, sb, R, D):
+    specs = part_specs(F, nu, sb, R, D)
+    return specs + specs[:1]
+
+
+def arrivals(parts, ids):
+    F = len(parts) - 1
+    step = pl.program_id(0)
+    own = ids[F] == ids[F + 1] // (F // 2)
+    whens = [(step == 0) & ~own] + [step == p for p in range(1, F)] + [(step == 0) & own]
+    return zip(whens, parts)
+
+
+def choose(parts, scratch, ids):
+    for when, ref in arrivals(parts, ids):
+
+        @pl.when(when)
         def _(ref=ref):
             scratch[...] = ref[...]
 
@@ -538,7 +551,7 @@
 
 def qkvg_kernel(F, shapes, ids, *refs):
     nin = 2 * (F - 1)
-    acts, refs = refs[:F], refs[F:]
+    acts, refs = refs[: F + 1], refs[F + 1 :]
     cond_ref, bq_ref, wq_hbm = refs[:3]
     got, swapped = refs[3 : 3 + F - 1], refs[3 + F - 1 : 3 + nin]
     q_ref, k_ref, v_ref, g_ref, token_ref, w, xs, sems = refs[3 + nin :]
@@ -554,7 +567,7 @@
             x.wait()
 
     sb, R, D = xs.shape
-    n, _ = stats_of(choose(acts, xs))
+    n, _ = stats_of(choose(acts, xs, ids))
     scale = tile_samples(sigmoid(cond_ref[:, :D]), sb)
     shift = tile_samples(cond_ref[:, D : 2 * D], sb)
     x = (scale * n + shift).astype(bf16)
@@ -570,7 +583,7 @@
 
 
 def qkvg_call(ids, acts, cond, bq, wq, got, swapped):
-    F = len(acts)
+    F = len(acts) - 1
     sl, R, D = acts[0].shape
     T = F * R
     sb, nu = sub_samples(sl, R)
@@ -582,7 +595,7 @@
         grid_spec=pltpu.PrefetchScalarGridSpec(
             num_scalar_prefetch=1,
             grid=(F, nu),
-            in_specs=part_specs(F, nu, sb, R, D)
+            in_specs=arrived_specs(F, nu, sb, R, D)
             + [
                 pl.BlockSpec((R, 2 * D), lambda r, u, s: (s[r], 0)),
                 pl.BlockSpec((1, D), lambda r, u, s: (0, 0)),
@@ -606,7 +619,7 @@
 
 
 def middle_kernel(F, shapes, ids, *refs):
-    acts, cots, refs = refs[:F], refs[F : 2 * F], refs[2 * F :]
+    acts, cots, refs = refs[: F + 1], refs[F + 1 : 2 * F + 2], refs[2 * F + 2 :]
     mix_a, mix_b, gate_ref, gone_ref, ctwo_ref = refs[:5]
     got, swapped = refs[5:7]
     outs, refs = refs[7 : 7 + F], refs[7 + F :]
@@ -655,7 +668,7 @@
     attn_out = dg(branch, wo[...], NN)
     sig_one = sigmoid(gone_ref[...])
     gate_one = tile_samples(sig_one, sb)
-    middle = choose(acts, xs) + gate_one * attn_out
+    middle = choose(acts, xs, ids) + gate_one * attn_out
     n, inv = stats_of(middle)
     sig_scale = sigmoid(ctwo_ref[:, :D])
     scale = tile_samples(sig_scale, sb)
@@ -670,7 +683,7 @@
     gate_two = tile_samples(sig_two, sb)
     store_part(outs, (middle + gate_two * ffn).astype(bf16).reshape(sb, R, D))
 
-    upstream = choose(cots, ys)
+    upstream = choose(cots, ys, ids)
     fg = (upstream * gate_two).astype(bf16)
     g_two = over_samples(upstream * ffn, sb) * (sig_two * (1.0 - sig_two))
     aout[...] += dg(hidden, fg, TN)
@@ -716,7 +729,7 @@
 
 
 def middle_call(ids, acts, cots, mix_a, mix_b, gate, cond_one, cond_two, shapes, got, swapped):
-    F = len(acts)
+    F = len(acts) - 1
     sl, R, D = acts[0].shape
     T = F * R
     H = shapes[2][0] * F
@@ -732,7 +745,7 @@
         grid_spec=pltpu.PrefetchScalarGridSpec(
             num_scalar_prefetch=1,
             grid=(F, nu),
-            in_specs=part_specs(F, nu, sb, R, D) * 2
+            in_specs=arrived_specs(F, nu, sb, R, D) * 2
             + [
                 lanes,
                 lanes,
@@ -785,7 +798,7 @@
 
 
 def back_weight_kernel(F, nd, shapes, ids, *refs):
-    acts, refs = refs[:F], refs[F:]
+    acts, refs = refs[: F + 1], refs[F + 1 :]
     cond_ref, dq_a, dq_b, dk_a, dk_b, dv_a, dv_b, gpg_ref = refs[:8]
     bq_ref, keep_ref, give_ref, acc, xs = refs[8 + nd :]
     D = acts[0].shape[2]
@@ -800,7 +813,7 @@
         bq_ref[...] = jnp.zeros_like(bq_ref)
 
     sb = xs.shape[0]
-    n, _ = stats_of(choose(acts, xs))
+    n, _ = stats_of(choose(acts, xs, ids))
     scale = tile_samples(sigmoid(cond_ref[:, :D]), sb)
     x = (scale * n + tile_samples(cond_ref[:, D : 2 * D], sb)).astype(bf16)
     for i, refs_i in enumerate(((dq_a, dq_b), (dk_a, dk_b), (dv_a, dv_b))):
@@ -817,7 +830,7 @@
 
 def back_data_kernel(F, nd, shapes, cshape, ids, *refs):
     nin = 2 * (F - 1)
-    acts, refs = refs[:F], refs[F:]
+    acts, refs = refs[: F + 1], refs[F + 1 :]
     cond_ref, dq_a, dq_b, dk_a, dk_b, dv_a, dv_b, gpg_ref, mg_ref = refs[:9]
     s_ref, gog_ref, wc_ref, wq_hbm = refs[9:13]
     got, swapped = refs[13 : 13 + F - 1], refs[13 + F - 1 : 13 + nin]
@@ -838,7 +851,7 @@
             x.wait()
 
     sb, R, D = xs.shape
-    n, inv = stats_of(choose(acts, xs))
+    n, inv = stats_of(choose(acts, xs, ids))
     sig_scale = sigmoid(cond_ref[:, :D])
     scale = tile_samples(sig_scale, sb)
     xg = dg(flat_rows(gpg_ref[0]), w[:, 3 * D :], NT)
@@ -874,7 +887,7 @@
 
 
 def back_weight(ids, acts, cond, dqkv, gpg, wq_shape, deps=()):
-    F = len(acts)
+    F = len(acts) - 1
     sl, R, D = acts[0].shape
     T = F * R
     sb, nu = sub_samples(sl, R)
@@ -887,7 +900,7 @@
         grid_spec=pltpu.PrefetchScalarGridSpec(
             num_scalar_prefetch=1,
             grid=(F, nu),
-            in_specs=part_specs(F, nu, sb, R, D)
+            in_specs=arrived_specs(F, nu, sb, R, D)
             + [pl.BlockSpec((R, 2 * D), lambda r, u, s: (s[r], 0))]
             + [lanes] * 6
             + [stacked]
@@ -909,7 +922,7 @@
 
 
 def back_data(ids, acts, cond, dqkv, gpg, mg, s_low, gog, wc, wq, got, swapped, deps=()):
-    F = len(acts)
+    F = len(acts) - 1
     sl, R, D = acts[0].shape
     T = F * R
     sb, nu = sub_samples(sl, R)
@@ -936,7 +949,7 @@
         grid_spec=pltpu.PrefetchScalarGridSpec(
             num_scalar_prefetch=1,
             grid=(F, nu),
-            in_specs=part_specs(F, nu, sb, R, D)
+            in_specs=arrived_specs(F, nu, sb, R, D)
             + [pl.BlockSpec((R, 2 * D), lambda r, u, s: (s[r], 0))]
             + [lanes] * 6
             + [stacked, stacked]
@@ -1015,27 +1028,24 @@
 
 
 def place_kernel(F, ids, *refs):
-    parts, out = refs[:F], refs[-1]
-    for p, ref in enumerate(parts):
-
-        @pl.when(pl.program_id(0) == p)
+    out = refs[-1]
+    for when, ref in arrivals(refs[: F + 1], ids):
+
+        @pl.when(when)
         def _(ref=ref):
             out[...] = ref[...]
 
 
 def place(ids, parts, deps=()):
-    F = len(parts)
+    F = len(parts) - 1
     sl, R, D = parts[0].shape
-
-    def fetch(p):
-        return pl.BlockSpec((sl, R, D), lambda i, s: (0, 0, 0), pipeline_mode=pl.Buffered(1))
-
+    fetch = pl.BlockSpec((sl, R, D), lambda i, s: (0, 0, 0), pipeline_mode=pl.Buffered(1))
     return pl.pallas_call(
         functools.partial(place_kernel, F),
         grid_spec=pltpu.PrefetchScalarGridSpec(
             num_scalar_prefetch=1,
             grid=(F,),
-            in_specs=[fetch(p) for p in range(F)] + [ANY] * len(deps),
+            in_specs=[fetch] * (F + 1) + [ANY] * len(deps),
             out_specs=pl.BlockSpec((sl, R, D), lambda i, s: (s[2 * F + 2 + i], 0, 0)),
         ),
         out_shape=jax.ShapeDtypeStruct((F * sl, R, D), parts[0].dtype),
@@ -1214,7 +1224,7 @@
             [blocks, jnp.stack([self.c, self.f]), rows, groups]
         ).astype(jnp.int32)
 
-    def send(self, x, fn):
+    def send(self, x, fn, raw=False):
         F = self.F
         pairs = []
         for z in range(self.Z):
@@ -1224,7 +1234,9 @@
                     pairs.append(((z * 2 + c) * F + f, (z2 * 2 + c2) * F + f2))
         others = [p for p in pairs if p[0] != p[1]]
         got = lax.ppermute(x, ("z", "core", "fsdp"), others)
-        return got if len(others) == len(pairs) else jnp.where(self.c == self.fh, x, got)
+        if len(others) == len(pairs) or raw:
+            return got
+        return jnp.where(self.c == self.fh, x, got)
 
     def core_swap(self, x):
         return self.send(x, lambda z, c, f: (z, 1 - c, f))
@@ -1239,9 +1251,10 @@
             self.send(
                 p,
                 lambda z, c, f: (z, (f // Fh) ^ (i % 2), c * Fh + ((f % Fh) ^ (i // 2))),
+                raw=True,
             )
             for i, p in enumerate(parts)
-        ]
+        ] + [parts[0]]
 
     def exchange_out(self, parts):
         Fh = self.Fh
@@ -1249,12 +1262,15 @@
             self.send(
                 p,
                 lambda z, c, f: (z, f // Fh, (c ^ (i % 2)) * Fh + ((f % Fh) ^ (i // 2))),
+                raw=True,
             )
             for i, p in enumerate(parts)
-        ]
+        ] + [parts[0]]
 
     def gather_rows(self, x):
-        own = [self.to_owner(x, a) for a in range(self.Fh)]
+        return [self.to_owner(x, a) for a in range(self.Fh)]
+
+    def both_cores(self, own):
         return own + [self.core_swap(p) for p in own]
 
     def chip_sum(self, parts):
@@ -1268,39 +1284,36 @@
     def to_owners(self, parts):
         return [self.to_owner(p, a) for a, p in enumerate(parts)]
 
-    def gather_packed(self, packed, *held):
+    def gather_packed(self, packed, mid, *held):
         F = self.F
         got = [self.send(packed, lambda z, c, f: (z, c, f ^ k)) for k in range(1, F)]
+        got[:-1], mid = tie(got[:-1], mid)
         got, *held = tie(got, *held)
-        return got, [self.core_swap(g) for g in got], *held
+        return got, [self.core_swap(g) for g in got], mid, *held
 
     def plane_send(self, parts):
         return list(parts[:1]) + [
             self.send(parts[k], lambda z, c, f: (z, c, f ^ k)) for k in range(1, self.F)
         ]
 
+    def tree(self, x, count, fn):
+        parts = [x] + [
+            self.send(x, lambda z, c, f: fn(z, c, f, k)) for k in range(1, count)
+        ]
+        parts = [p.astype(f32) for p in parts]
+        while len(parts) > 1:
+            parts = [parts[i] + parts[i + 1] for i in range(0, len(parts), 2)]
+        return parts[0].astype(x.dtype)
+
+    def over_z(self, x):
+        return self.tree(x, self.Z, lambda z, c, f, k: (z ^ k, c, f))
+
     def all_steps(self):
-        pairs = [lambda z, c, f: (z, 1 - c, f)]
-        bit = 1
-        while bit < self.F:
-            pairs.append(lambda z, c, f, bit=bit: (z, c, f ^ bit))
-            bit *= 2
-        bit = 1
-        while bit < self.Z:
-            pairs.append(lambda z, c, f, bit=bit: (z ^ bit, c, f))
-            bit *= 2
-        return [lambda x, fn=fn: x + self.send(x, fn) for fn in pairs]
-
-    def z_steps(self):
-        def add(x, bit):
-            got = self.send(x, lambda z, c, f: (z ^ bit, c, f))
-            return (x.astype(f32) + got.astype(f32)).astype(bf16)
-
-        steps, bit = [], 1
-        while bit < self.Z:
-            steps.append(functools.partial(add, bit=bit))
-            bit *= 2
-        return steps + [lambda x: (x, self.core_swap(x))]
+        return [
+            lambda x: x + self.core_swap(x),
+            lambda x: self.tree(x, self.F, lambda z, c, f, k: (z, c, f ^ k)),
+            self.over_z,
+        ]
 
 
 def total_of(parts):
@@ -1354,30 +1367,24 @@
     vecs = [gain_s1, b_cond1, b_q, gain_z, w_pair, gain_s2, b_cond2]
     sizes = [v.size for v in vecs]
     COND = single.shape[1]
-    wide = COND + 128
-    vrows = -(-sum(sizes) // (8 * wide)) * 8
-    flat = jnp.concatenate([v.reshape(-1) for v in vecs]).astype(f32)
-    flat = jnp.pad(flat, (0, vrows * wide - flat.shape[0])).reshape(vrows, wide)
     tag = jnp.where(padding == 1, -1, segment)
-    cols = jnp.stack([segment.astype(f32), tag.astype(f32)], axis=1)
-    table = jnp.concatenate([single, jnp.pad(cols, ((0, 0), (0, 126)))], axis=1)
-    table = jnp.concatenate([table, flat], axis=0)
-    table = lax.all_gather(table, ("core", "fsdp"))
+    flat = jnp.concatenate([x.reshape(-1).astype(f32) for x in (segment, tag, *vecs)])
+    vrows = -(-flat.shape[0] // (8 * COND)) * 8
+    flat = jnp.pad(flat, (0, vrows * COND - flat.shape[0])).reshape(vrows, COND)
+    table = lax.all_gather(jnp.concatenate([single, flat], axis=0), ("core", "fsdp"))
     mid_weights = [w_o, w_ab, w_out, w_cond2]
     mid_shapes = [w.shape for w in mid_weights]
     acts, packed, mid_packed = prepare(ids, act, [[w_qkvg, w_cond1], mid_weights])
     acts = net.exchange_in(acts)
     share = mid_packed.shape[0] // net.Z
     mid_got = lax.dynamic_slice_in_dim(mid_packed, net.z * share, share, 0)
-    table, mid_got = tie(table, mid_got)
-    mid_got = lax.all_gather(mid_got, ("fsdp", "z")).reshape(F, net.Z * share, 384)
-
     table = lax.dynamic_slice_in_dim(table, net.fh * F, F, 0)
-    single_all = table[:, :R, :COND].reshape(T, COND)
-    seg_col = table[:, :R, COND].reshape(T, 1)
-    tag_row = table[:, :R, COND + 1].reshape(1, T)
-    smalls = table[:, R:].reshape(F, vrows * wide)
-    full, at = [], 0
+    smalls = table[:, R:].reshape(F, vrows * COND)
+
+    single_all = table[:, :R].reshape(T, COND)
+    seg_col = smalls[:, :R].reshape(T, 1)
+    tag_row = smalls[:, R : 2 * R].reshape(1, T)
+    full, at = [], 2 * R
     for v, n in zip(vecs, sizes):
         full.append(smalls[:, at : at + n].reshape((F * v.shape[0],) + v.shape[1:]))
         at += n
@@ -1389,8 +1396,11 @@
     gz_row = gz.reshape(1, -1)
     bias_a, bias_b = pair_fwd(pair, gz_row, w_rows)
     acts, packed, bias_a, bias_b = tie(acts, packed, bias_a, bias_b)
-    one_got, one_swapped, bias_a, bias_b = net.gather_packed(packed, bias_a, bias_b)
-    bias_a, bias_b = net.gather_rows(bias_a), net.gather_rows(bias_b)
+    one_got, one_swapped, mid_got, bias_a, bias_b = net.gather_packed(
+        packed, mid_got, bias_a, bias_b
+    )
+    mid_got = lax.all_gather(mid_got, ("fsdp", "z")).reshape(F, net.Z * share, 384)
+    bias_a, bias_b = net.both_cores(net.gather_rows(bias_a)), net.gather_rows(bias_b)
 
     single_first, cond_one, wc1 = cond_fwd(
         ids,
@@ -1406,9 +1416,11 @@
         ids, acts, cond_one, bq.reshape(1, D), w_qkvg, one_got, one_swapped
     )
 
-    cots = net.exchange_in(prepare(ids, cotangent, deps=[token])[0])
-    mix_a, lse_a = attn_fwd(ids, seg_col, tag_row, q, k, v, bias_a, 0)
-    mid_got, mix_a = tie(mid_got, mix_a)
+    cots = prepare(ids, cotangent, deps=[token])[0]
+    mix_a, lse_a = attn_fwd(ids, seg_col, tag_row, q, k, v, bias_a, 0, deps=cots)
+    cots = net.exchange_in(cots)
+    mid_got, mix_a, bias_b, cots[1:3] = tie(mid_got, mix_a, bias_b, cots[1:3])
+    bias_b = net.both_cores(bias_b)
     mid_swapped = net.core_swap(mid_got)
     mix_b, lse_b = attn_fwd(ids, seg_col, tag_row, q, k, v, bias_b, 1)
     single_second, cond_two, wc2 = cond_fwd(
@@ -1497,7 +1509,14 @@
         [mid_sum[:, : shares[0]].reshape(-1, 384), mid_sum[:, shares[0] :].reshape(-1, 384)], axis=0
     )
     late_sum, flat, s_parts, mid_sum, wq_sum = lockstep(
-        (late_parts, [lambda x: total_of(net.plane_send(x)).astype(bf16)] + net.z_steps()),
+        (
+            late_parts,
+            [
+                lambda x: total_of(net.plane_send(x)).astype(bf16),
+                net.over_z,
+                lambda x: (x, net.core_swap(x)),
+            ],
+        ),
         (flat, net.all_steps()),
         (s_parts, [net.chip_sum, net.to_owners]),
         (mid_sum, [lambda x: (x, net.core_swap(x))]),

time: 751 us -> 702 us (0.935)
  starting transfers between devices: 118 us -> 84.9 us
  local copies, waits for them, and re-layouts: 57.1 us -> 45.1 us
    ppermute x66 -> x69, starting transfers between devices: 117 us -> 84.7 us  [send(): got = lax.ppermute(x, ('z', 'core', 'fsdp'), others)]
    unnamed x147 -> x141, local copies, waits for them, and re-layouts: 24.3 us -> 22.4 us
    ppermute x66 -> x69, waiting for transfers between devices: 84.6 us -> 85.8 us  [send(): got = lax.ppermute(x, ('z', 'core', 'fsdp'), others)]
  transfers between devices with their start and end apart: 71 -> 74, of which waited for: 15 -> 16; matrix products, arithmetic and copies ran while one was open for 7% -> 6% of each run, Pallas kernels for 42% -> 45%
where the time goes in v3:
time: 702 us; the launch traced here: 697 us
  Pallas kernels  414 us (59%)
  waiting for transfers between devices  101 us (14%)
  starting transfers between devices  84.9 us (12%)
  local copies, waits for them, and re-layouts  45.1 us (6%)
  other arithmetic  33.9 us (5%)
  between operations  17.8 us (3%)
    pallas_call x1, Pallas kernels, middle_call(): pl.pallas_call(functools.partial(middle_kernel, F, shapes), grid_spec=plt...  92.2 us
    pallas_call x2, Pallas kernels, attn_bwd(): pl.pallas_call(functools.partial(attn_bwd_kernel, F, len(deps), min(T, 51...  86.5 us
    ppermute x69, waiting for transfers between devices, send(): got = lax.ppermute(x, ('z', 'core', 'fsdp'), others)  85.8 us
    ppermute x69, starting transfers between devices, send(): got = lax.ppermute(x, ('z', 'core', 'fsdp'), others)  84.7 us
    pallas_call x2, Pallas kernels, attn_fwd(): pl.pallas_call(functools.partial(attn_fwd_kernel, F, len(deps), min(T, 25...  51.1 us
    pallas_call x1, Pallas kernels, pair_bwd(): pl.pallas_call(functools.partial(pair_bwd_kernel, P, len(deps), U), grid=...  34.7 us
    pallas_call x1, Pallas kernels, back_data(): pl.pallas_call(functools.partial(back_data_kernel, F, len(deps), shapes,...  31.1 us
    pallas_call x1, Pallas kernels, qkvg_call(): pl.pallas_call(functools.partial(qkvg_kernel, F, shapes), grid_spec=pltpu...  22.7 us
  transfers between devices with their start and end apart: 74, of which 16 were waited for; matrix products, arithmetic and copies ran while one was open for 6% of the time, Pallas kernels for 45%

profile of v3, /device:TPU:0, one launch (start us, length us, event | category | flops | bytes accessed | tf_op | source)
XLA Modules:
  0.0 696.7 jit_solution(1741041346795724714)
XLA Ops:
  8.8 4.1 concatenate.22
  23.8 3.4 prepare.2
  28.8 3.5 collective-permute-start.1
  33.8 14.7 %all-gather.7.cloned.1.call-done = f32[1088,384]{1,0:T(8,128)} async-done(((f32[136,384]{1,0:T(8,128)}), f32[1088,384]{1,0:T(8,128)}) %all-gather.7.cloned.1.call-update) | async-done | bytes 1671184 | tf_op jit(solution)/shard_map/all_gather | solution.py:1374
  50.2 20.1 %pair_fwd.1 = (bf16[8,128,512]{2,1,0:T(8,128)(2,1)S(1)}, bf16[8,128,512]{2,1,0:T(8,128)(2,1)S(1)}) custom-call(bf16[128,512,128]{2,1,0:T(8,128)(2,1)} %bitcast.112, f32[1,128]{1,0:T(1,128)S(1)} %reshape_reshape.18.gain_ref, bf16[128,1024]{1,0:T(8,128)(2,1)S(1)} %fusion.1.w_ref), custom_call_target="tpu_custom_call" | custom-call | flops 26424115200 | bytes 25165824 | tf_op jit(solution)/shard_map/pair_fwd/pallas_call | solution.py:296
  75.4 18.2 %collective-permute-done.4.refs_1_.refs_8_.refs_18_ = bf16[1056,384]{1,0:T(8,128)(2,1)} collective-permute-done((bf16[1056,384]{1,0:T(8,128)(2,1)}, bf16[1056,384]{1,0:T(8,128)(2,1)}, u32[]{:S(2)}, u32[]{:S(2)}) %collective-permute-start.4) | collective-permute-done | bytes 811040 | tf_op jit(solution)/shard_map/ppermute | solution.py:1236
  95.2 22.0 %collective-permute-done.6.refs_3_.refs_10_.refs_20_ = bf16[1056,384]{1,0:T(8,128)(2,1)S(1)} collective-permute-done((bf16[1056,384]{1,0:T(8,128)(2,1)}, bf16[1056,384]{1,0:T(8,128)(2,1)S(1)}, u32[]{:S(2)}, u32[]{:S(2)}) %collective-permute-start.6) | collective-permute-done | bytes 811040 | tf_op jit(solution)/shard_map/ppermute | solution.py:1236
  129.3 8.5 %cond_fwd.2 = (bf16[512,384]{1,0:T(8,128)(2,1)}, f32[512,2304]{1,0:T(8,128)}, bf16[4,96,2304]{2,1,0:T(8,128)(2,1)}) custom-call(s32[14]{0:T(128)} %copy-done.8, f32[512,384]{1,0:T(8,128)} %bitcast.90, f32[1,384]{1,0:T(1,128)} %reshape_reshape.19.gain_ref, f32[1,2304]{1,0:T(1,128)} %reshape_reshape.20.bias_ref, bf16[96,2304]{1,0:T(8,128)(2,1)} %refs_0_.1, ...), custom_call_target="tpu_custom_call" | custom-call | flops 6000000000 | bytes 4718592 | tf_op jit(solution)/shard_map/cond_fwd/pallas_call | solution.py:1198
  137.9 9.6 %collective-permute-start.13 = (bf16[8,128,512]{2,1,0:T(8,128)(2,1)S(1)}, bf16[8,128,512]{2,1,0:T(8,128)(2,1)}, u32[]{:S(2)}, u32[]{:S(2)}) collective-permute-start(bf16[8,128,512]{2,1,0:T(8,128)(2,1)S(1)} %broadcast_select_fusion.3.refs_0_), channel_id=1, source_target_pairs={{0,4},{1,5},{2,6},{3,7},{4,0},{5,1},{6,2},{7,3},{8,12},{9,13},{10,... | collective-permute-start | bytes 3145736 | tf_op jit(solution)/shard_map/ppermute | solution.py:1236
  147.5 5.5 collective-permute-done.12.refs_1_
  153.1 3.0 collective-permute-start.14
  156.0 22.7 %qkvg.1 = (bf16[4,512,768]{2,1,0:T(8,128)(2,1)}, bf16[4,512,768]{2,1,0:T(8,128)(2,1)}, bf16[4,512,768]{2,1,0:T(8,128)(2,1)}, f32[4,4,128,768]{3,2,1,0:T(8,128)}, f32[1,128]{1,0:T(1,128)}) custom-call(s32[14]{0:T(128)} %copy-done.8, bf16[4,128,768]{2,1,0:T(8,128)(2,1)} %collective-permute-done.refs_0_, bf16[4,128,768]{2,1,0:T(8,128)(2,1)} %collective-permute-done.1.refs_1_, ...), custom_call_target="tpu_custom_call" | custom-call | flops 22951231488 | bytes 23592960 | tf_op jit(solution)/shard_map/qkvg/pallas_call | solution.py:593
  186.2 25.6 %attn_fwd.2 = (f32[4,512,384]{2,1,0:T(8,128)}, f32[4,512,128]{2,1,0:T(8,128)}) custom-call(s32[14]{0:T(128)} %copy-done.8, f32[512,1]{1,0:T(8,128)} %copy.89.seg_ref, f32[1,512]{1,0:T(1,128)} %bitcast.108, bf16[4,512,768]{2,1,0:T(8,128)(2,1)} %get-tuple-element.217.q_ref, bf16[4,512,768]{2,1,0:T(8,128)(2,1)} %get-tuple-element.218.k_ref, ...), custom_call_target="tpu_custom_call" | custom-call | flops 31037849600 | bytes 12058624 | tf_op jit(solution)/shard_map/attn_fwd/pallas_call | solution.py:123
  217.8 3.4 collective-permute-start.19
  225.7 25.5 %attn_fwd.3 = (f32[4,512,384]{2,1,0:T(8,128)}, f32[4,512,128]{2,1,0:T(8,128)}) custom-call(s32[14]{0:T(128)} %copy-done.8, f32[512,1]{1,0:T(8,128)} %copy.89.seg_ref, f32[1,512]{1,0:T(1,128)} %bitcast.109, bf16[4,512,768]{2,1,0:T(8,128)(2,1)} %get-tuple-element.217.q_ref, bf16[4,512,768]{2,1,0:T(8,128)(2,1)} %get-tuple-element.218.k_ref, ...), custom_call_target="tpu_custom_call" | custom-call | flops 31037849600 | bytes 12058624 | tf_op jit(solution)/shard_map/attn_fwd/pallas_call | solution.py:123
  251.2 10.0 %cond_fwd.3 = (bf16[512,384]{1,0:T(8,128)(2,1)}, f32[512,2304]{1,0:T(8,128)}, bf16[4,96,2304]{2,1,0:T(8,128)(2,1)}) custom-call(s32[14]{0:T(128)} %copy-done.8, f32[512,384]{1,0:T(8,128)} %bitcast.91, f32[1,384]{1,0:T(1,128)} %reshape_reshape.22.gain_ref, f32[1,2304]{1,0:T(1,128)} %reshape_reshape.23.bias_ref, bf16[4,1632,384]{2,1,0:T(8,128)(2,1)} %bitcast.115, ...), custom_call_target="tpu_custom_call" | custom-call | flops 6000000000 | bytes 4718592 | tf_op jit(solution)/shard_map/cond_fwd/pallas_call | solution.py:1198
  261.2 92.2 %middle.1 = (bf16[4,128,768]{2,1,0:T(8,128)(2,1)}, bf16[4,128,768]{2,1,0:T(8,128)(2,1)}, bf16[4,128,768]{2,1,0:T(8,128)(2,1)}, bf16[4,128,768]{2,1,0:T(8,128)(2,...) custom-call(s32[14]{0:T(128)} %copy-done.8, ...), custom_call_target="tpu_custom_call" | custom-call | flops 101468602368 | bytes 37748736 | tf_op jit(solution)/shard_map/middle/pallas_call | solution.py:743
  354.9 6.7 cond_back.1
  372.9 43.0 %attn_bwd.2 = (f32[4,512,384]{2,1,0:T(8,128)}, bf16[4,512,384]{2,1,0:T(8,128)(2,1)}, bf16[4,512,384]{2,1,0:T(8,128)(2,1)}, bf16[8,128,512]{2,1,0:T(8,128)(2,1)},...) custom-call(s32[14]{0:T(128)} %copy-done.8, f32[512,1]{1,0:T(8,128)} %copy.89.seg_ref, ...), custom_call_target="tpu_custom_call" | custom-call | flops 52009369600 | bytes 20971520 | tf_op jit(solution)/shard_map/attn_bwd/pallas_call | solution.py:230
  426.3 43.5 %attn_bwd.3 = (f32[4,512,384]{2,1,0:T(8,128)}, bf16[4,512,384]{2,1,0:T(8,128)(2,1)}, bf16[4,512,384]{2,1,0:T(8,128)(2,1)}, bf16[8,128,512]{2,1,0:T(8,128)(2,1)},...) custom-call(s32[14]{0:T(128)} %copy-done.8, f32[512,1]{1,0:T(8,128)} %copy.89.seg_ref, ...), custom_call_target="tpu_custom_call" | custom-call | flops 52009369600 | bytes 20971520 | tf_op jit(solution)/shard_map/attn_bwd/pallas_call | solution.py:230
  484.6 22.5 %back_weight.1 = (f32[1,768]{1,0:T(1,128)}, bf16[4,768,384]{2,1,0:T(8,128)(2,1)}, bf16[4,768,384]{2,1,0:T(8,128)(2,1)}) custom-call(s32[14]{0:T(128)} %copy-done.8, bf16[4,128,768]{2,1,0:T(8,128)(2,1)} %collective-permute-done.refs_0_, bf16[4,128,768]{2,1,0:T(8,128)(2,1)} %collective-permute-done.1.refs_1_, ...), custom_call_target="tpu_custom_call" | custom-call | flops 20535312384 | bytes 32243712 | tf_op jit(solution)/shard_map/back_weight/pallas_call | solution.py:898
  508.6 6.0 collective-permute-done.36.refs_3_
  522.4 5.0 place.2.refs_2_
  529.3 4.5 terms.2
  538.1 31.1 %back_data.1 = (bf16[4,128,768]{2,1,0:T(8,128)(2,1)}, bf16[4,128,768]{2,1,0:T(8,128)(2,1)}, bf16[4,128,768]{2,1,0:T(8,128)(2,1)}, bf16[4,128,768]{2,1,0:T(8,128)...) custom-call(s32[14]{0:T(128)} %copy-done.8, ...), custom_call_target="tpu_custom_call" | custom-call | flops 20535312384 | bytes 39321600 | tf_op jit(solution)/shard_map/back_data/pallas_call | solution.py:947
  586.9 34.7 %pair_bwd.1 = (bf16[128,512,128]{2,1,0:T(8,128)(2,1)}, f32[128,128]{1,0:T(8,128)S(1)}) custom-call(bf16[128,512,128]{2,1,0:T(8,128)(2,1)} %bitcast.113, f32[1,128]{1,0:T(1,128)S(1)} %copy-done.7, bf16[8,256,128]{2,1,0:T(8,128)(2,1)S(1)} %copy-done.1, bf16[8,128,512]{2,1,0:T(8,128)(2,1)S(1)} %broadcast_select_fusion.1.refs_0_, ...), custom_call_target="tpu_custom_call" | custom-call | flops 46137344000 | bytes 50331648 | tf_op jit(solution)/shard_map/pair_bwd/pallas_call | solution.py:372
  630.9 4.0 collective-permute-done.49
  634.9 5.1 collective-permute-done.50
  652.7 11.1 %collective-permute-done.58 = bf16[288,384]{1,0:T(8,128)(2,1)S(1)} collective-permute-done((bf16[288,384]{1,0:T(8,128)(2,1)S(1)}, bf16[288,384]{1,0:T(8,128)(2,1)S(1)}, u32[]{:S(2)}, u32[]{:S(2)}) %collective-permute-start.58) | collective-permute-done | bytes 221216 | tf_op jit(solution)/shard_map/ppermute | solution.py:1236
  663.9 3.0 collective-permute-start.66
  669.3 4.5 place.3
  675.8 4.7 unpack.3
  (388 shorter events, 157.6 us)
Async XLA Ops:
  7.2 41.3 %all-gather.7.cloned.1.call-start = ((), (), s32[]{:S(2)}) async-start(), calls=%async_computation.3 | async-start | bytes 1880064 | tf_op jit(solution)/shard_map/all_gather | solution.py:1374
  14.6 197.3 %all-gather.9.cloned.1.call-start = ((), (), s32[]{:S(2)}) async-start(), calls=%async_computation.4 | async-start | bytes 5326848 | tf_op jit(solution)/shard_map/all_gather | solution.py:1402
  27.2 43.0 %collective-permute-start = (bf16[4,128,768]{2,1,0:T(8,128)(2,1)}, bf16[4,128,768]{2,1,0:T(8,128)(2,1)}, u32[]{:S(2)}, u32[]{:S(2)}) collective-permute-start(bf16[4,128,768]{2,1,0:T(8,128)(2,1)} %get-tuple-element.203.refs_4_), channel_id=1, source_target_pairs={{2,4},{3,5},{4,2},{5,3},{10,12},{11,13},{12,10},{13,11},{18,20},{1... | collective-permute-start | bytes 2359304 | tf_op jit(solution)/shard_map/ppermute | solution.py:1236
  28.8 41.5 %collective-permute-start.1 = (bf16[4,128,768]{2,1,0:T(8,128)(2,1)}, bf16[4,128,768]{2,1,0:T(8,128)(2,1)}, u32[]{:S(2)}, u32[]{:S(2)}) collective-permute-start(bf16[4,128,768]{2,1,0:T(8,128)(2,1)} %get-tuple-element.193), channel_id=1, source_target_pairs={{0,4},{1,5},{2,0},{3,1},{4,6},{5,7},{6,2},{7,3},{8,12},{9,13},{10,... | collective-permute-start | bytes 2359304 | tf_op jit(solution)/shard_map/ppermute | solution.py:1236
  32.2 38.0 %collective-permute-start.2 = (bf16[4,128,768]{2,1,0:T(8,128)(2,1)}, bf16[4,128,768]{2,1,0:T(8,128)(2,1)}, u32[]{:S(2)}, u32[]{:S(2)}) collective-permute-start(bf16[4,128,768]{2,1,0:T(8,128)(2,1)} %get-tuple-element.194), channel_id=1, source_target_pairs={{0,1},{1,0},{2,5},{3,4},{4,3},{5,2},{6,7},{7,6},{8,9},{9,8},{10,13... | collective-permute-start | bytes 2359304 | tf_op jit(solution)/shard_map/ppermute | solution.py:1236
  33.7 39.4 %collective-permute-start.3 = (bf16[4,128,768]{2,1,0:T(8,128)(2,1)}, bf16[4,128,768]{2,1,0:T(8,128)(2,1)}, u32[]{:S(2)}, u32[]{:S(2)}) collective-permute-start(bf16[4,128,768]{2,1,0:T(8,128)(2,1)} %get-tuple-element.195), channel_id=1, source_target_pairs={{0,5},{1,4},{2,1},{3,0},{4,7},{5,6},{6,3},{7,2},{8,13},{9,12},{10,... | collective-permute-start | bytes 2359304 | tf_op jit(solution)/shard_map/ppermute | solution.py:1236
  94.8 376.5 %reduce-scatter.2.cloned.1.call-start = ((), (), s32[]{:S(2)}) async-start(), calls=%async_computation.1 | async-start | bytes 6266880 | tf_op jit(solution)/shard_map/reduce_scatter | solution.py:1452
  119.4 33.6 %collective-permute-start.12 = (bf16[8,128,512]{2,1,0:T(8,128)(2,1)S(1)}, bf16[8,128,512]{2,1,0:T(8,128)(2,1)}, u32[]{:S(2)}, u32[]{:S(2)}) collective-permute-start(bf16[8,128,512]{2,1,0:T(8,128)(2,1)S(1)} %get-tuple-element.220), channel_id=1, source_target_pairs={{0,1},{1,0},{2,5},{3,4},{4,3},{5,2},{6,7},{7,6},{8,9},{9,8},{10,13... | collective-permute-start | bytes 3145736 | tf_op jit(solution)/shard_map/ppermute | solution.py:1236
  125.6 58.3 %collective-permute-start.15 = (bf16[8,128,512]{2,1,0:T(8,128)(2,1)S(1)}, bf16[8,128,512]{2,1,0:T(8,128)(2,1)}, u32[]{:S(2)}, u32[]{:S(2)}) collective-permute-start(bf16[8,128,512]{2,1,0:T(8,128)(2,1)S(1)} %get-tuple-element.225), channel_id=1, source_target_pairs={{2,4},{3,5},{4,2},{5,3},{10,12},{11,13},{12,10},{13,11},{18,20},{1... | collective-permute-start | bytes 3145736 | tf_op jit(solution)/shard_map/ppermute | solution.py:1236
  127.8 84.0 %collective-permute-start.16 = (bf16[8,128,512]{2,1,0:T(8,128)(2,1)S(1)}, bf16[8,128,512]{2,1,0:T(8,128)(2,1)}, u32[]{:S(2)}, u32[]{:S(2)}) collective-permute-start(bf16[8,128,512]{2,1,0:T(8,128)(2,1)S(1)} %get-tuple-element.225), channel_id=1, source_target_pairs={{0,1},{1,0},{2,5},{3,4},{4,3},{5,2},{6,7},{7,6},{8,9},{9,8},{10,13... | collective-permute-start | bytes 3145736 | tf_op jit(solution)/shard_map/ppermute | solution.py:1236
  137.9 47.3 %collective-permute-start.13 = (bf16[8,128,512]{2,1,0:T(8,128)(2,1)S(1)}, bf16[8,128,512]{2,1,0:T(8,128)(2,1)}, u32[]{:S(2)}, u32[]{:S(2)}) collective-permute-start(bf16[8,128,512]{2,1,0:T(8,128)(2,1)S(1)} %broadcast_select_fusion.3.refs_0_), channel_id=1, source_target_pairs={{0,4},{1,5},{2,6},{3,7},{4,0},{5,1},{6,2},{7,3},{8,12},{9,13},{10,... | collective-permute-start | bytes 3145736 | tf_op jit(solution)/shard_map/ppermute | solution.py:1236
  153.1 32.1 %collective-permute-start.14 = (bf16[8,128,512]{2,1,0:T(8,128)(2,1)}, bf16[8,128,512]{2,1,0:T(8,128)(2,1)S(1)}, u32[]{:S(2)}, u32[]{:S(2)}) collective-permute-start(bf16[8,128,512]{2,1,0:T(8,128)(2,1)} %collective-permute-done.12.refs_1_), channel_id=1, source_target_pairs={{0,4},{1,5},{2,6},{3,7},{4,0},{5,1},{6,2},{7,3},{8,12},{9,13},{10,... | collective-permute-start | bytes 3145736 | tf_op jit(solution)/shard_map/ppermute | solution.py:1236
  211.9 39.3 %collective-permute-start.22 = (bf16[4,1632,384]{2,1,0:T(8,128)(2,1)}, bf16[4,1632,384]{2,1,0:T(8,128)(2,1)}, u32[]{:S(2)}, u32[]{:S(2)}) collective-permute-start(bf16[4,1632,384]{2,1,0:T(8,128)(2,1)} %bitcast.114), channel_id=1, source_target_pairs={{0,4},{1,5},{2,6},{3,7},{4,0},{5,1},{6,2},{7,3},{8,12},{9,13},{10,... | collective-permute-start | bytes 15040520 | tf_op jit(solution)/shard_map/ppermute | solution.py:1236
  216.3 44.9 %collective-permute-start.10 = (bf16[4,128,768]{2,1,0:T(8,128)(2,1)S(1)}, bf16[4,128,768]{2,1,0:T(8,128)(2,1)}, u32[]{:S(2)}, u32[]{:S(2)}) collective-permute-start(bf16[4,128,768]{2,1,0:T(8,128)(2,1)S(1)} %copy-done.19), channel_id=1, source_target_pairs={{2,4},{3,5},{4,2},{5,3},{10,12},{11,13},{12,10},{13,11},{18,20},{1... | collective-permute-start | bytes 2359304 | tf_op jit(solution)/shard_map/ppermute | solution.py:1236
  217.8 43.4 %collective-permute-start.19 = (bf16[4,128,768]{2,1,0:T(8,128)(2,1)S(1)}, bf16[4,128,768]{2,1,0:T(8,128)(2,1)}, u32[]{:S(2)}, u32[]{:S(2)}) collective-permute-start(bf16[4,128,768]{2,1,0:T(8,128)(2,1)S(1)} %copy-done.21), channel_id=1, source_target_pairs={{0,5},{1,4},{2,1},{3,0},{4,7},{5,6},{6,3},{7,2},{8,13},{9,12},{10,... | collective-permute-start | bytes 2359304 | tf_op jit(solution)/shard_map/ppermute | solution.py:1236
  361.8 54.1 %collective-permute-start.23 = (bf16[4,128,768]{2,1,0:T(8,128)(2,1)}, bf16[4,128,768]{2,1,0:T(8,128)(2,1)}, u32[]{:S(2)}, u32[]{:S(2)}) collective-permute-start(bf16[4,128,768]{2,1,0:T(8,128)(2,1)} %get-tuple-element.256.refs_4_), channel_id=1, source_target_pairs={{2,4},{3,5},{4,2},{5,3},{10,12},{11,13},{12,10},{13,11},{18,20},{1... | collective-permute-start | bytes 2359304 | tf_op jit(solution)/shard_map/ppermute | solution.py:1236
  363.6 52.4 %collective-permute-start.24 = (bf16[4,128,768]{2,1,0:T(8,128)(2,1)}, bf16[4,128,768]{2,1,0:T(8,128)(2,1)}, u32[]{:S(2)}, u32[]{:S(2)}) collective-permute-start(bf16[4,128,768]{2,1,0:T(8,128)(2,1)} %get-tuple-element.236), channel_id=1, source_target_pairs={{0,2},{1,3},{2,6},{3,7},{4,0},{5,1},{6,4},{7,5},{8,10},{9,11},{10,... | collective-permute-start | bytes 2359304 | tf_op jit(solution)/shard_map/ppermute | solution.py:1236
  366.0 49.9 %collective-permute-start.25 = (bf16[4,128,768]{2,1,0:T(8,128)(2,1)}, bf16[4,128,768]{2,1,0:T(8,128)(2,1)}, u32[]{:S(2)}, u32[]{:S(2)}) collective-permute-start(bf16[4,128,768]{2,1,0:T(8,128)(2,1)} %get-tuple-element.237), channel_id=1, source_target_pairs={{0,1},{1,0},{2,5},{3,4},{4,3},{5,2},{6,7},{7,6},{8,9},{9,8},{10,13... | collective-permute-start | bytes 2359304 | tf_op jit(solution)/shard_map/ppermute | solution.py:1236
  368.1 47.9 %collective-permute-start.26 = (bf16[4,128,768]{2,1,0:T(8,128)(2,1)}, bf16[4,128,768]{2,1,0:T(8,128)(2,1)}, u32[]{:S(2)}, u32[]{:S(2)}) collective-permute-start(bf16[4,128,768]{2,1,0:T(8,128)(2,1)} %get-tuple-element.238), channel_id=1, source_target_pairs={{0,3},{1,2},{2,7},{3,6},{4,1},{5,0},{6,5},{7,4},{8,11},{9,10},{10,... | collective-permute-start | bytes 2359304 | tf_op jit(solution)/shard_map/ppermute | solution.py:1236
  372.8 248.8 %all-gather.11.cloned.1.call-start = ((), (), s32[]{:S(2)}) async-start(), calls=%async_computation.5 | async-start | bytes 1566720 | tf_op jit(solution)/shard_map/all_gather | solution.py:1468
  421.4 49.9 %collective-permute-start.32 = (bf16[8,128,512]{2,1,0:T(8,128)(2,1)}, bf16[8,128,512]{2,1,0:T(8,128)(2,1)}, u32[]{:S(2)}, u32[]{:S(2)}) collective-permute-start(bf16[8,128,512]{2,1,0:T(8,128)(2,1)} %add_convert_fusion.3.refs_5_), channel_id=1, source_target_pairs={{0,1},{1,0},{2,5},{3,4},{4,3},{5,2},{6,7},{7,6},{8,9},{9,8},{10,13... | collective-permute-start | bytes 3145736 | tf_op jit(solution)/shard_map/ppermute | solution.py:1236
  424.6 45.2 %collective-permute-start.30 = (bf16[8,128,512]{2,1,0:T(8,128)(2,1)}, bf16[8,128,512]{2,1,0:T(8,128)(2,1)}, u32[]{:S(2)}, u32[]{:S(2)}) collective-permute-start(bf16[8,128,512]{2,1,0:T(8,128)(2,1)} %add_convert_fusion.4.refs_4_), channel_id=1, source_target_pairs={{2,4},{3,5},{4,2},{5,3},{10,12},{11,13},{12,10},{13,11},{18,20},{1... | collective-permute-start | bytes 3145736 | tf_op jit(solution)/shard_map/ppermute | solution.py:1236
  475.3 33.3 %collective-permute-start.37 = (bf16[408,384]{1,0:T(8,128)(2,1)}, bf16[408,384]{1,0:T(8,128)(2,1)}, u32[]{:S(2)}, u32[]{:S(2)}) collective-permute-start(bf16[408,384]{1,0:T(8,128)(2,1)} %get-tuple-element.440), channel_id=1, source_target_pairs={{0,1},{1,0},{2,3},{3,2},{4,5},{5,4},{6,7},{7,6},{8,9},{9,8},{10,11... | collective-permute-start | bytes 940040 | tf_op jit(solution)/shard_map/ppermute | solution.py:1236
  475.4 33.2 %collective-permute-start.38 = (bf16[408,384]{1,0:T(8,128)(2,1)}, bf16[408,384]{1,0:T(8,128)(2,1)}, u32[]{:S(2)}, u32[]{:S(2)}) collective-permute-start(bf16[408,384]{1,0:T(8,128)(2,1)} %get-tuple-element.439), channel_id=1, source_target_pairs={{0,2},{1,3},{2,0},{3,1},{4,6},{5,7},{6,4},{7,5},{8,10},{9,11},{10,... | collective-permute-start | bytes 940040 | tf_op jit(solution)/shard_map/ppermute | solution.py:1236
  481.2 33.3 %collective-permute-start.36 = (bf16[8,128,512]{2,1,0:T(8,128)(2,1)}, bf16[8,128,512]{2,1,0:T(8,128)(2,1)}, u32[]{:S(2)}, u32[]{:S(2)}) collective-permute-start(bf16[8,128,512]{2,1,0:T(8,128)(2,1)} %add_convert_fusion.1.refs_14_), channel_id=1, source_target_pairs={{0,1},{1,0},{2,5},{3,4},{4,3},{5,2},{6,7},{7,6},{8,9},{9,8},{10,13... | collective-permute-start | bytes 3145736 | tf_op jit(solution)/shard_map/ppermute | solution.py:1236
  522.3 99.3 %all-reduce.3.cloned.1.call-start = ((), (), s32[]{:S(2)}) async-start(), calls=%async_computation.2 | async-start | bytes 1179648 | tf_op jit(solution)/shard_map/psum | solution.py:1487
  534.6 34.6 %collective-permute-start.41 = (bf16[768,384]{1,0:T(8,128)(2,1)}, bf16[768,384]{1,0:T(8,128)(2,1)}, u32[]{:S(2)}, u32[]{:S(2)}) collective-permute-start(bf16[768,384]{1,0:T(8,128)(2,1)} %get-tuple-element.282), channel_id=1, source_target_pairs={{0,1},{1,0},{2,3},{3,2},{4,5},{5,4},{6,7},{7,6},{8,9},{9,8},{10,11... | collective-permute-start | bytes 1769480 | tf_op jit(solution)/shard_map/ppermute | solution.py:1236
  536.6 32.6 %collective-permute-start.42 = (bf16[768,384]{1,0:T(8,128)(2,1)}, bf16[768,384]{1,0:T(8,128)(2,1)}, u32[]{:S(2)}, u32[]{:S(2)}) collective-permute-start(bf16[768,384]{1,0:T(8,128)(2,1)} %get-tuple-element.283), channel_id=1, source_target_pairs={{0,2},{1,3},{2,0},{3,1},{4,6},{5,7},{6,4},{7,5},{8,10},{9,11},{10,... | collective-permute-start | bytes 1769480 | tf_op jit(solution)/shard_map/ppermute | solution.py:1236
  571.6 50.1 %collective-permute-start.45 = (bf16[4,128,768]{2,1,0:T(8,128)(2,1)}, bf16[4,128,768]{2,1,0:T(8,128)(2,1)}, u32[]{:S(2)}, u32[]{:S(2)}) collective-permute-start(bf16[4,128,768]{2,1,0:T(8,128)(2,1)} %get-tuple-element.323.refs_4_), channel_id=1, source_target_pairs={{2,4},{3,5},{4,2},{5,3},{10,12},{11,13},{12,10},{13,11},{18,20},{1... | collective-permute-start | bytes 2359304 | tf_op jit(solution)/shard_map/ppermute | solution.py:1236
  573.2 48.5 %collective-permute-start.46 = (bf16[4,128,768]{2,1,0:T(8,128)(2,1)}, bf16[4,128,768]{2,1,0:T(8,128)(2,1)}, u32[]{:S(2)}, u32[]{:S(2)}) collective-permute-start(bf16[4,128,768]{2,1,0:T(8,128)(2,1)} %get-tuple-element.316), channel_id=1, source_target_pairs={{0,2},{1,3},{2,6},{3,7},{4,0},{5,1},{6,4},{7,5},{8,10},{9,11},{10,... | collective-permute-start | bytes 2359304 | tf_op jit(solution)/shard_map/ppermute | solution.py:1236
  575.6 46.0 %collective-permute-start.47 = (bf16[4,128,768]{2,1,0:T(8,128)(2,1)}, bf16[4,128,768]{2,1,0:T(8,128)(2,1)}, u32[]{:S(2)}, u32[]{:S(2)}) collective-permute-start(bf16[4,128,768]{2,1,0:T(8,128)(2,1)} %get-tuple-element.317), channel_id=1, source_target_pairs={{0,1},{1,0},{2,5},{3,4},{4,3},{5,2},{6,7},{7,6},{8,9},{9,8},{10,13... | collective-permute-start | bytes 2359304 | tf_op jit(solution)/shard_map/ppermute | solution.py:1236
  577.6 44.0 %collective-permute-start.48 = (bf16[4,128,768]{2,1,0:T(8,128)(2,1)}, bf16[4,128,768]{2,1,0:T(8,128)(2,1)}, u32[]{:S(2)}, u32[]{:S(2)}) collective-permute-start(bf16[4,128,768]{2,1,0:T(8,128)(2,1)} %get-tuple-element.318), channel_id=1, source_target_pairs={{0,3},{1,2},{2,7},{3,6},{4,1},{5,0},{6,5},{7,4},{8,11},{9,10},{10,... | collective-permute-start | bytes 2359304 | tf_op jit(solution)/shard_map/ppermute | solution.py:1236
  (111 other events, 1270.2 us)
Sparse Core Ops, SparseCore 0:
  14.7 33.7 all-gather.6
  94.9 116.4 all-gather.8
  373.0 90.9 reduce-scatter.1
  522.5 32.8 all-gather.10
  581.0 39.6 all-reduce.2

commit v4 on v3

--- a/solution.py
+++ b/solution.py
@@ -1308,6 +1308,16 @@
     def over_z(self, x):
         return self.tree(x, self.Z, lambda z, c, f, k: (z ^ k, c, f))
 
+    def z_steps(self):
+        steps, bit = [], 1
+        while bit < self.Z:
+            fn = lambda z, c, f, bit=bit: (z ^ bit, c, f)
+            steps.append(
+                lambda x, fn=fn: (x.astype(f32) + self.send(x, fn).astype(f32)).astype(x.dtype)
+            )
+            bit *= 2
+        return steps + [lambda x: (x, self.core_swap(x))]
+
     def all_steps(self):
         return [
             lambda x: x + self.core_swap(x),
@@ -1323,8 +1333,9 @@
 def lockstep(*lanes):
     values = [v for v, _ in lanes]
     for i in range(max(len(steps) for _, steps in lanes)):
-        values = [steps[i](v) if i < len(steps) else v for v, (_, steps) in zip(values, lanes)]
-        values = tie(*values)
+        on = [n for n, (_, steps) in enumerate(lanes) if i < len(steps)]
+        for n, v in zip(on, tie(*[lanes[n][1][i](values[n]) for n in on])):
+            values[n] = v
     return values
 
 
@@ -1400,7 +1411,7 @@
         packed, mid_got, bias_a, bias_b
     )
     mid_got = lax.all_gather(mid_got, ("fsdp", "z")).reshape(F, net.Z * share, 384)
-    bias_a, bias_b = net.both_cores(net.gather_rows(bias_a)), net.gather_rows(bias_b)
+    bias_a, bias_b = net.gather_rows(bias_a), net.gather_rows(bias_b)
 
     single_first, cond_one, wc1 = cond_fwd(
         ids,
@@ -1417,20 +1428,24 @@
     )
 
     cots = prepare(ids, cotangent, deps=[token])[0]
+    bias_a, q = tie(bias_a, q)
+    bias_a = net.both_cores(bias_a)
     mix_a, lse_a = attn_fwd(ids, seg_col, tag_row, q, k, v, bias_a, 0, deps=cots)
     cots = net.exchange_in(cots)
-    mid_got, mix_a, bias_b, cots[1:3] = tie(mid_got, mix_a, bias_b, cots[1:3])
+    mix_a, bias_b = tie(mix_a, bias_b)
     bias_b = net.both_cores(bias_b)
-    mid_swapped = net.core_swap(mid_got)
     mix_b, lse_b = attn_fwd(ids, seg_col, tag_row, q, k, v, bias_b, 1)
+    mid_got, mix_b, cots = tie(mid_got, mix_b, cots)
+    two_got = mid_got[:, packed_rows(mid_shapes[:3]) :]
+    two_swapped, mid_swapped = net.core_swap(two_got), net.core_swap(mid_got)
     single_second, cond_two, wc2 = cond_fwd(
         ids,
         single_all,
         gs2.reshape(1, -1),
         bc2.reshape(1, -1),
         w_cond2.shape,
-        packed_rows(mid_shapes[:3]),
-        [mid_got, mid_swapped],
+        0,
+        [two_got, two_swapped],
         True,
     )
     outs, d_attn, gate_proj, mid_grad, cond_two_grad, gate_one_grad, keep, give = middle_call(
@@ -1486,6 +1501,8 @@
     wq_parts, keep, give, ags = tie(net.plane_send(wq_parts), keep, give, ags)
     wq_sum = lax.psum(total_of(wq_parts).astype(bf16), "z")
     late_parts = terms(ids, [keep], [net.core_swap(give)])
+    late_parts, ags = tie(late_parts, ags)
+    late_send = net.plane_send(late_parts)
     ags = net.exchange_out(ags)
 
     wc = wt * gz_row
@@ -1494,8 +1511,8 @@
     wc_hi = wc.astype(bf16)
     wc = jnp.concatenate([wc_hi, (wc - wc_hi.astype(f32)).astype(bf16)], axis=1)
     pair_grad, gw = pair_bwd(pair, gz_row, wc, db_a, db_b, deps=late_parts[:1])
-    late_parts, gw, s_one_grad, mid_sum, wq_sum, ags = tie(
-        late_parts, gw, s_one_grad, mid_sum, wq_sum, ags
+    late_send, gw, s_one_grad, mid_sum, wq_sum, ags[1:3] = tie(
+        late_send, gw, s_one_grad, mid_sum, wq_sum, ags[1:3]
     )
 
     s_grad = s_one_grad * gs1 + s_two_grad * gs2
@@ -1508,22 +1525,24 @@
     mid_sum = jnp.concatenate(
         [mid_sum[:, : shares[0]].reshape(-1, 384), mid_sum[:, shares[0] :].reshape(-1, 384)], axis=0
     )
-    late_sum, flat, s_parts, mid_sum, wq_sum = lockstep(
+    (
+        (total_wo, total_wab, total_wout, total_wc2, total_wq),
+        late_sum,
+        flat,
+        s_parts,
+        act_grad,
+    ) = lockstep(
         (
-            late_parts,
+            (mid_sum, wq_sum),
             [
-                lambda x: total_of(net.plane_send(x)).astype(bf16),
-                net.over_z,
-                lambda x: (x, net.core_swap(x)),
+                lambda x: [(y, net.core_swap(y)) for y in x],
+                lambda x: unpack(net.c, [(*x[0], mid_shapes), (*x[1], [w_qkvg.shape])]),
             ],
         ),
+        (total_of(late_send).astype(bf16), net.z_steps()),
         (flat, net.all_steps()),
         (s_parts, [net.chip_sum, net.to_owners]),
-        (mid_sum, [lambda x: (x, net.core_swap(x))]),
-        (wq_sum, [lambda x: (x, net.core_swap(x))]),
-    )
-    total_wo, total_wab, total_wout, total_wc2, total_wq = unpack(
-        net.c, [(*mid_sum, mid_shapes), (*wq_sum, [w_qkvg.shape])]
+        (ags, [lambda x: x, lambda x: place(ids, x)]),
     )
     (total_wc1,) = unpack(net.c, [(*late_sum, [w_cond1.shape])])
     local_n, local_inv = norm_stats(single)
@@ -1545,7 +1564,7 @@
     )
     return (
         block_out[None],
-        place(ids, ags, deps=[gw])[None],
+        act_grad[None],
         single_grad,
         pair_grad[None],
         total_gs1,

time: 702 us -> 691 us (0.984)
  starting transfers between devices: 84.9 us -> 75.7 us
    ppermute x69, starting transfers between devices: 84.7 us -> 75.5 us  [send(): got = lax.ppermute(x, ('z', 'core', 'fsdp'), others)]
    unnamed x141 -> x151, local copies, waits for them, and re-layouts: 22.4 us -> 21.4 us
  transfers between devices with their start and end apart: 74 -> 74, of which waited for: 16 -> 16; matrix products, arithmetic and copies ran while one was open for 6% -> 7% of each run, Pallas kernels for 45% -> 46%
where the time goes in v4:
time: 691 us; the launch traced here: 680 us
  Pallas kernels  409 us (59%)
  waiting for transfers between devices  94.8 us (14%)
  starting transfers between devices  75.7 us (11%)
  local copies, waits for them, and re-layouts  47.6 us (7%)
  other arithmetic  35.2 us (5%)
  between operations  18.1 us (3%)
    pallas_call x1, Pallas kernels, middle_call(): pl.pallas_call(functools.partial(middle_kernel, F, shapes), grid_spec=plt...  91.9 us
    pallas_call x2, Pallas kernels, attn_bwd(): pl.pallas_call(functools.partial(attn_bwd_kernel, F, len(deps), min(T, 51...  86.3 us
    ppermute x69, waiting for transfers between devices, send(): got = lax.ppermute(x, ('z', 'core', 'fsdp'), others)  80 us
    ppermute x69, starting transfers between devices, send(): got = lax.ppermute(x, ('z', 'core', 'fsdp'), others)  75.5 us
    pallas_call x2, Pallas kernels, attn_fwd(): pl.pallas_call(functools.partial(attn_fwd_kernel, F, len(deps), min(T, 25...  51.2 us
    pallas_call x1, Pallas kernels, pair_bwd(): pl.pallas_call(functools.partial(pair_bwd_kernel, P, len(deps), U), grid=...  34.6 us
    pallas_call x1, Pallas kernels, back_data(): pl.pallas_call(functools.partial(back_data_kernel, F, len(deps), shapes,...  31.1 us
    pallas_call x1, Pallas kernels, back_weight(): pl.pallas_call(functools.partial(back_weight_kernel, F, len(deps), [wq_sh...  22.5 us
  transfers between devices with their start and end apart: 74, of which 16 were waited for; matrix products, arithmetic and copies ran while one was open for 7% of the time, Pallas kernels for 46%

profile of v4, /device:TPU:0, one launch (start us, length us, event | category | flops | bytes accessed | tf_op | source)
XLA Modules:
  0.0 680.1 jit_solution(17640297912198758065)
XLA Ops:
  8.8 4.1 concatenate.22
  23.8 3.4 prepare.2
  28.7 3.5 collective-permute-start.1
  33.8 14.7 %all-gather.7.cloned.1.call-done = f32[1088,384]{1,0:T(8,128)} async-done(((f32[136,384]{1,0:T(8,128)}), f32[1088,384]{1,0:T(8,128)}) %all-gather.7.cloned.1.call-update) | async-done | bytes 1671184 | tf_op jit(solution)/shard_map/all_gather | solution.py:1385
  50.2 20.1 %pair_fwd.1 = (bf16[8,128,512]{2,1,0:T(8,128)(2,1)S(1)}, bf16[8,128,512]{2,1,0:T(8,128)(2,1)S(1)}) custom-call(bf16[128,512,128]{2,1,0:T(8,128)(2,1)} %bitcast.115, f32[1,128]{1,0:T(1,128)S(1)} %reshape_reshape.18.gain_ref, bf16[128,1024]{1,0:T(8,128)(2,1)S(1)} %fusion.1.w_ref), custom_call_target="tpu_custom_call" | custom-call | flops 26424115200 | bytes 25165824 | tf_op jit(solution)/shard_map/pair_fwd/pallas_call | solution.py:296
  70.3 2.9 collective-permute-done.3.refs_3_
  77.4 17.0 %collective-permute-done.4.refs_1_.refs_8_.refs_18_ = bf16[1056,384]{1,0:T(8,128)(2,1)} collective-permute-done((bf16[1056,384]{1,0:T(8,128)(2,1)}, bf16[1056,384]{1,0:T(8,128)(2,1)}, u32[]{:S(2)}, u32[]{:S(2)}) %collective-permute-start.4) | collective-permute-done | bytes 811040 | tf_op jit(solution)/shard_map/ppermute | solution.py:1236
  94.4 17.8 %collective-permute-done.5.refs_2_.refs_9_.refs_19_ = bf16[1056,384]{1,0:T(8,128)(2,1)} collective-permute-done((bf16[1056,384]{1,0:T(8,128)(2,1)}, bf16[1056,384]{1,0:T(8,128)(2,1)}, u32[]{:S(2)}, u32[]{:S(2)}) %collective-permute-start.5) | collective-permute-done | bytes 811040 | tf_op jit(solution)/shard_map/ppermute | solution.py:1236
  120.8 8.5 %cond_fwd.2 = (bf16[512,384]{1,0:T(8,128)(2,1)}, f32[512,2304]{1,0:T(8,128)}, bf16[4,96,2304]{2,1,0:T(8,128)(2,1)}) custom-call(s32[14]{0:T(128)} %copy-done.8, f32[512,384]{1,0:T(8,128)} %bitcast.90, f32[1,384]{1,0:T(1,128)} %reshape_reshape.19.gain_ref, f32[1,2304]{1,0:T(1,128)} %reshape_reshape.20.bias_ref, bf16[96,2304]{1,0:T(8,128)(2,1)} %refs_0_.1, ...), custom_call_target="tpu_custom_call" | custom-call | flops 6000000000 | bytes 4718592 | tf_op jit(solution)/shard_map/cond_fwd/pallas_call | solution.py:1198
  129.4 21.9 %qkvg.1 = (bf16[4,512,768]{2,1,0:T(8,128)(2,1)}, bf16[4,512,768]{2,1,0:T(8,128)(2,1)}, bf16[4,512,768]{2,1,0:T(8,128)(2,1)}, f32[4,4,128,768]{3,2,1,0:T(8,128)}, f32[1,128]{1,0:T(1,128)}) custom-call(s32[14]{0:T(128)} %copy-done.8, bf16[4,128,768]{2,1,0:T(8,128)(2,1)} %collective-permute-done.refs_0_, bf16[4,128,768]{2,1,0:T(8,128)(2,1)} %collective-permute-done.1.refs_1_, ...), custom_call_target="tpu_custom_call" | custom-call | flops 22951231488 | bytes 23592960 | tf_op jit(solution)/shard_map/qkvg/pallas_call | solution.py:593
  151.5 4.4 collective-permute-start.12
  163.5 25.7 %attn_fwd.2 = (f32[4,512,384]{2,1,0:T(8,128)}, f32[4,512,128]{2,1,0:T(8,128)}) custom-call(s32[14]{0:T(128)} %copy-done.8, f32[512,1]{1,0:T(8,128)} %copy.90.seg_ref, f32[1,512]{1,0:T(1,128)} %bitcast.111, bf16[4,512,768]{2,1,0:T(8,128)(2,1)} %get-tuple-element.230.q_ref, bf16[4,512,768]{2,1,0:T(8,128)(2,1)} %get-tuple-element.231.k_ref, ...), custom_call_target="tpu_custom_call" | custom-call | flops 31037849600 | bytes 12058624 | tf_op jit(solution)/shard_map/attn_fwd/pallas_call | solution.py:123
  198.3 25.5 %attn_fwd.3 = (f32[4,512,384]{2,1,0:T(8,128)}, f32[4,512,128]{2,1,0:T(8,128)}) custom-call(s32[14]{0:T(128)} %copy-done.8, f32[512,1]{1,0:T(8,128)} %copy.90.seg_ref, f32[1,512]{1,0:T(1,128)} %bitcast.112, bf16[4,512,768]{2,1,0:T(8,128)(2,1)} %get-tuple-element.230.q_ref, bf16[4,512,768]{2,1,0:T(8,128)(2,1)} %get-tuple-element.231.k_ref, ...), custom_call_target="tpu_custom_call" | custom-call | flops 31037849600 | bytes 12058624 | tf_op jit(solution)/shard_map/attn_fwd/pallas_call | solution.py:123
  223.8 4.0 collective-permute-done.19.refs_6_
  227.8 8.4 %collective-permute-done.21.refs_8_ = bf16[4,128,768]{2,1,0:T(8,128)(2,1)} collective-permute-done((bf16[4,128,768]{2,1,0:T(8,128)(2,1)S(1)}, bf16[4,128,768]{2,1,0:T(8,128)(2,1)}, u32[]{:S(2)}, u32[]{:S(2)}) %collective-permute-start.21) | collective-permute-done | bytes 786464 | tf_op jit(solution)/shard_map/ppermute | solution.py:1236
  239.3 6.5 collective-permute-done.22.refs_1_
  246.7 7.4 %cond_fwd.3 = (bf16[512,384]{1,0:T(8,128)(2,1)}, f32[512,2304]{1,0:T(8,128)}, bf16[4,96,2304]{2,1,0:T(8,128)(2,1)}) custom-call(s32[14]{0:T(128)} %copy-done.8, f32[512,384]{1,0:T(8,128)} %bitcast.91, f32[1,384]{1,0:T(1,128)} %reshape_reshape.22.gain_ref, f32[1,2304]{1,0:T(1,128)} %reshape_reshape.23.bias_ref, bf16[4,288,384]{2,1,0:T(8,128)(2,1)} %copy-done.43, ...), custom_call_target="tpu_custom_call" | custom-call | flops 6000000000 | bytes 4718592 | tf_op jit(solution)/shard_map/cond_fwd/pallas_call | solution.py:1198
  254.2 91.9 %middle.1 = (bf16[4,128,768]{2,1,0:T(8,128)(2,1)}, bf16[4,128,768]{2,1,0:T(8,128)(2,1)}, bf16[4,128,768]{2,1,0:T(8,128)(2,1)}, bf16[4,128,768]{2,1,0:T(8,128)(2,...) custom-call(s32[14]{0:T(128)} %copy-done.8, ...), custom_call_target="tpu_custom_call" | custom-call | flops 101468602368 | bytes 37748736 | tf_op jit(solution)/shard_map/middle/pallas_call | solution.py:743
  347.3 6.7 cond_back.1
  364.5 43.0 %attn_bwd.2 = (f32[4,512,384]{2,1,0:T(8,128)}, bf16[4,512,384]{2,1,0:T(8,128)(2,1)}, bf16[4,512,384]{2,1,0:T(8,128)(2,1)}, bf16[8,128,512]{2,1,0:T(8,128)(2,1)},...) custom-call(s32[14]{0:T(128)} %copy-done.8, f32[512,1]{1,0:T(8,128)} %copy.90.seg_ref, ...), custom_call_target="tpu_custom_call" | custom-call | flops 52009369600 | bytes 20971520 | tf_op jit(solution)/shard_map/attn_bwd/pallas_call | solution.py:230
  417.0 43.3 %attn_bwd.3 = (f32[4,512,384]{2,1,0:T(8,128)}, bf16[4,512,384]{2,1,0:T(8,128)(2,1)}, bf16[4,512,384]{2,1,0:T(8,128)(2,1)}, bf16[8,128,512]{2,1,0:T(8,128)(2,1)},...) custom-call(s32[14]{0:T(128)} %copy-done.8, f32[512,1]{1,0:T(8,128)} %copy.90.seg_ref, ...), custom_call_target="tpu_custom_call" | custom-call | flops 52009369600 | bytes 20971520 | tf_op jit(solution)/shard_map/attn_bwd/pallas_call | solution.py:230
  476.6 22.5 %back_weight.1 = (f32[1,768]{1,0:T(1,128)}, bf16[4,768,384]{2,1,0:T(8,128)(2,1)}, bf16[4,768,384]{2,1,0:T(8,128)(2,1)}) custom-call(s32[14]{0:T(128)} %copy-done.8, bf16[4,128,768]{2,1,0:T(8,128)(2,1)} %collective-permute-done.refs_0_, bf16[4,128,768]{2,1,0:T(8,128)(2,1)} %collective-permute-done.1.refs_1_, ...), custom_call_target="tpu_custom_call" | custom-call | flops 20535312384 | bytes 32243712 | tf_op jit(solution)/shard_map/back_weight/pallas_call | solution.py:898
  500.6 4.6 collective-permute-done.37.refs_3_
  514.5 5.0 place.2.refs_2_
  521.6 4.5 terms.2
  530.3 31.1 %back_data.1 = (bf16[4,128,768]{2,1,0:T(8,128)(2,1)}, bf16[4,128,768]{2,1,0:T(8,128)(2,1)}, bf16[4,128,768]{2,1,0:T(8,128)(2,1)}, bf16[4,128,768]{2,1,0:T(8,128)...) custom-call(s32[14]{0:T(128)} %copy-done.8, ...), custom_call_target="tpu_custom_call" | custom-call | flops 20535312384 | bytes 39321600 | tf_op jit(solution)/shard_map/back_data/pallas_call | solution.py:947
  568.4 3.4 terms.3
  577.2 34.6 %pair_bwd.1 = (bf16[128,512,128]{2,1,0:T(8,128)(2,1)}, f32[128,128]{1,0:T(8,128)S(1)}) custom-call(bf16[128,512,128]{2,1,0:T(8,128)(2,1)} %bitcast.116, f32[1,128]{1,0:T(1,128)S(1)} %copy-done.7, bf16[8,256,128]{2,1,0:T(8,128)(2,1)S(1)} %copy-done.1, bf16[8,128,512]{2,1,0:T(8,128)(2,1)S(1)} %broadcast_select_fusion.1.refs_0_, ...), custom_call_target="tpu_custom_call" | custom-call | flops 46137344000 | bytes 50331648 | tf_op jit(solution)/shard_map/pair_bwd/pallas_call | solution.py:372
  629.1 5.1 collective-permute-done.53
  642.6 3.4 unpack.2
  646.0 4.3 place.3
  653.4 3.1 collective-permute-done.64
  (400 shorter events, 159.7 us)
Async XLA Ops:
  7.2 41.3 %all-gather.7.cloned.1.call-start = ((), (), s32[]{:S(2)}) async-start(), calls=%async_computation.3 | async-start | bytes 1880064 | tf_op jit(solution)/shard_map/all_gather | solution.py:1385
  14.6 221.6 %all-gather.9.cloned.1.call-start = ((), (), s32[]{:S(2)}) async-start(), calls=%async_computation.4 | async-start | bytes 5326848 | tf_op jit(solution)/shard_map/all_gather | solution.py:1413
  27.2 43.1 %collective-permute-start = (bf16[4,128,768]{2,1,0:T(8,128)(2,1)}, bf16[4,128,768]{2,1,0:T(8,128)(2,1)}, u32[]{:S(2)}, u32[]{:S(2)}) collective-permute-start(bf16[4,128,768]{2,1,0:T(8,128)(2,1)} %get-tuple-element.216.refs_4_), channel_id=1, source_target_pairs={{2,4},{3,5},{4,2},{5,3},{10,12},{11,13},{12,10},{13,11},{18,20},{1... | collective-permute-start | bytes 2359304 | tf_op jit(solution)/shard_map/ppermute | solution.py:1236
  28.7 41.5 %collective-permute-start.1 = (bf16[4,128,768]{2,1,0:T(8,128)(2,1)}, bf16[4,128,768]{2,1,0:T(8,128)(2,1)}, u32[]{:S(2)}, u32[]{:S(2)}) collective-permute-start(bf16[4,128,768]{2,1,0:T(8,128)(2,1)} %get-tuple-element.206), channel_id=1, source_target_pairs={{0,4},{1,5},{2,0},{3,1},{4,6},{5,7},{6,2},{7,3},{8,12},{9,13},{10,... | collective-permute-start | bytes 2359304 | tf_op jit(solution)/shard_map/ppermute | solution.py:1236
  32.2 38.1 %collective-permute-start.2 = (bf16[4,128,768]{2,1,0:T(8,128)(2,1)}, bf16[4,128,768]{2,1,0:T(8,128)(2,1)}, u32[]{:S(2)}, u32[]{:S(2)}) collective-permute-start(bf16[4,128,768]{2,1,0:T(8,128)(2,1)} %get-tuple-element.207), channel_id=1, source_target_pairs={{0,1},{1,0},{2,5},{3,4},{4,3},{5,2},{6,7},{7,6},{8,9},{9,8},{10,13... | collective-permute-start | bytes 2359304 | tf_op jit(solution)/shard_map/ppermute | solution.py:1236
  33.7 39.4 %collective-permute-start.3 = (bf16[4,128,768]{2,1,0:T(8,128)(2,1)}, bf16[4,128,768]{2,1,0:T(8,128)(2,1)}, u32[]{:S(2)}, u32[]{:S(2)}) collective-permute-start(bf16[4,128,768]{2,1,0:T(8,128)(2,1)} %get-tuple-element.208), channel_id=1, source_target_pairs={{0,5},{1,4},{2,1},{3,0},{4,7},{5,6},{6,3},{7,2},{8,13},{9,12},{10,... | collective-permute-start | bytes 2359304 | tf_op jit(solution)/shard_map/ppermute | solution.py:1236
  74.6 37.5 %collective-permute-start.5 = (bf16[1056,384]{1,0:T(8,128)(2,1)}, bf16[1056,384]{1,0:T(8,128)(2,1)}, u32[]{:S(2)}, u32[]{:S(2)}) collective-permute-start(bf16[1056,384]{1,0:T(8,128)(2,1)} %get-tuple-element.217), channel_id=1, source_target_pairs={{0,2},{1,3},{2,0},{3,1},{4,6},{5,7},{6,4},{7,5},{8,10},{9,11},{10,... | collective-permute-start | bytes 2433032 | tf_op jit(solution)/shard_map/ppermute | solution.py:1236
  74.6 37.5 %collective-permute-start.6 = (bf16[1056,384]{1,0:T(8,128)(2,1)}, bf16[1056,384]{1,0:T(8,128)(2,1)}, u32[]{:S(2)}, u32[]{:S(2)}) collective-permute-start(bf16[1056,384]{1,0:T(8,128)(2,1)} %get-tuple-element.217), channel_id=1, source_target_pairs={{0,3},{1,2},{2,1},{3,0},{4,7},{5,6},{6,5},{7,4},{8,11},{9,10},{10,... | collective-permute-start | bytes 2433032 | tf_op jit(solution)/shard_map/ppermute | solution.py:1236
  116.9 34.4 %collective-permute-start.7 = (bf16[8,128,512]{2,1,0:T(8,128)(2,1)S(1)}, bf16[8,128,512]{2,1,0:T(8,128)(2,1)}, u32[]{:S(2)}, u32[]{:S(2)}) collective-permute-start(bf16[8,128,512]{2,1,0:T(8,128)(2,1)S(1)} %get-tuple-element.224), channel_id=1, source_target_pairs={{2,4},{3,5},{4,2},{5,3},{10,12},{11,13},{12,10},{13,11},{18,20},{1... | collective-permute-start | bytes 3145736 | tf_op jit(solution)/shard_map/ppermute | solution.py:1236
  119.1 342.6 %reduce-scatter.2.cloned.1.call-start = ((), (), s32[]{:S(2)}) async-start(), calls=%async_computation.1 | async-start | bytes 6266880 | tf_op jit(solution)/shard_map/reduce_scatter | solution.py:1467
  119.2 42.3 %collective-permute-start.14 = (bf16[8,128,512]{2,1,0:T(8,128)(2,1)S(1)}, bf16[8,128,512]{2,1,0:T(8,128)(2,1)}, u32[]{:S(2)}, u32[]{:S(2)}) collective-permute-start(bf16[8,128,512]{2,1,0:T(8,128)(2,1)S(1)} %get-tuple-element.241), channel_id=1, source_target_pairs={{2,4},{3,5},{4,2},{5,3},{10,12},{11,13},{12,10},{13,11},{18,20},{1... | collective-permute-start | bytes 3145736 | tf_op jit(solution)/shard_map/ppermute | solution.py:1236
  157.4 33.8 %collective-permute-start.15 = (bf16[8,128,512]{2,1,0:T(8,128)(2,1)S(1)}, bf16[8,128,512]{2,1,0:T(8,128)(2,1)}, u32[]{:S(2)}, u32[]{:S(2)}) collective-permute-start(bf16[8,128,512]{2,1,0:T(8,128)(2,1)S(1)} %get-tuple-element.241), channel_id=1, source_target_pairs={{0,1},{1,0},{2,5},{3,4},{4,3},{5,2},{6,7},{7,6},{8,9},{9,8},{10,13... | collective-permute-start | bytes 3145736 | tf_op jit(solution)/shard_map/ppermute | solution.py:1236
  194.3 33.5 %collective-permute-start.19 = (bf16[4,128,768]{2,1,0:T(8,128)(2,1)}, bf16[4,128,768]{2,1,0:T(8,128)(2,1)}, u32[]{:S(2)}, u32[]{:S(2)}) collective-permute-start(bf16[4,128,768]{2,1,0:T(8,128)(2,1)} %copy-done.23), channel_id=1, source_target_pairs={{0,4},{1,5},{2,0},{3,1},{4,6},{5,7},{6,2},{7,3},{8,12},{9,13},{10,... | collective-permute-start | bytes 2359304 | tf_op jit(solution)/shard_map/ppermute | solution.py:1236
  197.3 38.9 %collective-permute-start.21 = (bf16[4,128,768]{2,1,0:T(8,128)(2,1)S(1)}, bf16[4,128,768]{2,1,0:T(8,128)(2,1)}, u32[]{:S(2)}, u32[]{:S(2)}) collective-permute-start(bf16[4,128,768]{2,1,0:T(8,128)(2,1)S(1)} %copy-done.20), channel_id=1, source_target_pairs={{0,5},{1,4},{2,1},{3,0},{4,7},{5,6},{6,3},{7,2},{8,13},{9,12},{10,... | collective-permute-start | bytes 2359304 | tf_op jit(solution)/shard_map/ppermute | solution.py:1236
  354.5 53.0 %collective-permute-start.24 = (bf16[4,128,768]{2,1,0:T(8,128)(2,1)}, bf16[4,128,768]{2,1,0:T(8,128)(2,1)}, u32[]{:S(2)}, u32[]{:S(2)}) collective-permute-start(bf16[4,128,768]{2,1,0:T(8,128)(2,1)} %get-tuple-element.276.refs_4_), channel_id=1, source_target_pairs={{2,4},{3,5},{4,2},{5,3},{10,12},{11,13},{12,10},{13,11},{18,20},{1... | collective-permute-start | bytes 2359304 | tf_op jit(solution)/shard_map/ppermute | solution.py:1236
  356.2 51.3 %collective-permute-start.25 = (bf16[4,128,768]{2,1,0:T(8,128)(2,1)}, bf16[4,128,768]{2,1,0:T(8,128)(2,1)}, u32[]{:S(2)}, u32[]{:S(2)}) collective-permute-start(bf16[4,128,768]{2,1,0:T(8,128)(2,1)} %get-tuple-element.256), channel_id=1, source_target_pairs={{0,2},{1,3},{2,6},{3,7},{4,0},{5,1},{6,4},{7,5},{8,10},{9,11},{10,... | collective-permute-start | bytes 2359304 | tf_op jit(solution)/shard_map/ppermute | solution.py:1236
  358.4 49.1 %collective-permute-start.26 = (bf16[4,128,768]{2,1,0:T(8,128)(2,1)}, bf16[4,128,768]{2,1,0:T(8,128)(2,1)}, u32[]{:S(2)}, u32[]{:S(2)}) collective-permute-start(bf16[4,128,768]{2,1,0:T(8,128)(2,1)} %get-tuple-element.257), channel_id=1, source_target_pairs={{0,1},{1,0},{2,5},{3,4},{4,3},{5,2},{6,7},{7,6},{8,9},{9,8},{10,13... | collective-permute-start | bytes 2359304 | tf_op jit(solution)/shard_map/ppermute | solution.py:1236
  359.0 48.5 %collective-permute-start.27 = (bf16[4,128,768]{2,1,0:T(8,128)(2,1)}, bf16[4,128,768]{2,1,0:T(8,128)(2,1)}, u32[]{:S(2)}, u32[]{:S(2)}) collective-permute-start(bf16[4,128,768]{2,1,0:T(8,128)(2,1)} %get-tuple-element.258), channel_id=1, source_target_pairs={{0,3},{1,2},{2,7},{3,6},{4,1},{5,0},{6,5},{7,4},{8,11},{9,10},{10,... | collective-permute-start | bytes 2359304 | tf_op jit(solution)/shard_map/ppermute | solution.py:1236
  364.4 251.2 %all-gather.11.cloned.1.call-start = ((), (), s32[]{:S(2)}) async-start(), calls=%async_computation.5 | async-start | bytes 1566720 | tf_op jit(solution)/shard_map/all_gather | solution.py:1483
  413.4 48.3 %collective-permute-start.33 = (bf16[8,128,512]{2,1,0:T(8,128)(2,1)}, bf16[8,128,512]{2,1,0:T(8,128)(2,1)}, u32[]{:S(2)}, u32[]{:S(2)}) collective-permute-start(bf16[8,128,512]{2,1,0:T(8,128)(2,1)} %add_convert_fusion.3.refs_5_), channel_id=1, source_target_pairs={{0,1},{1,0},{2,5},{3,4},{4,3},{5,2},{6,7},{7,6},{8,9},{9,8},{10,13... | collective-permute-start | bytes 3145736 | tf_op jit(solution)/shard_map/ppermute | solution.py:1236
  415.3 45.0 %collective-permute-start.31 = (bf16[8,128,512]{2,1,0:T(8,128)(2,1)}, bf16[8,128,512]{2,1,0:T(8,128)(2,1)}, u32[]{:S(2)}, u32[]{:S(2)}) collective-permute-start(bf16[8,128,512]{2,1,0:T(8,128)(2,1)} %add_convert_fusion.4.refs_4_), channel_id=1, source_target_pairs={{2,4},{3,5},{4,2},{5,3},{10,12},{11,13},{12,10},{13,11},{18,20},{1... | collective-permute-start | bytes 3145736 | tf_op jit(solution)/shard_map/ppermute | solution.py:1236
  465.9 34.6 %collective-permute-start.38 = (bf16[408,384]{1,0:T(8,128)(2,1)}, bf16[408,384]{1,0:T(8,128)(2,1)}, u32[]{:S(2)}, u32[]{:S(2)}) collective-permute-start(bf16[408,384]{1,0:T(8,128)(2,1)} %get-tuple-element.466), channel_id=1, source_target_pairs={{0,1},{1,0},{2,3},{3,2},{4,5},{5,4},{6,7},{7,6},{8,9},{9,8},{10,11... | collective-permute-start | bytes 940040 | tf_op jit(solution)/shard_map/ppermute | solution.py:1236
  467.4 33.2 %collective-permute-start.39 = (bf16[408,384]{1,0:T(8,128)(2,1)}, bf16[408,384]{1,0:T(8,128)(2,1)}, u32[]{:S(2)}, u32[]{:S(2)}) collective-permute-start(bf16[408,384]{1,0:T(8,128)(2,1)} %get-tuple-element.465), channel_id=1, source_target_pairs={{0,2},{1,3},{2,0},{3,1},{4,6},{5,7},{6,4},{7,5},{8,10},{9,11},{10,... | collective-permute-start | bytes 940040 | tf_op jit(solution)/shard_map/ppermute | solution.py:1236
  471.9 33.3 %collective-permute-start.37 = (bf16[8,128,512]{2,1,0:T(8,128)(2,1)}, bf16[8,128,512]{2,1,0:T(8,128)(2,1)}, u32[]{:S(2)}, u32[]{:S(2)}) collective-permute-start(bf16[8,128,512]{2,1,0:T(8,128)(2,1)} %add_convert_fusion.1.refs_14_), channel_id=1, source_target_pairs={{0,1},{1,0},{2,5},{3,4},{4,3},{5,2},{6,7},{7,6},{8,9},{9,8},{10,13... | collective-permute-start | bytes 3145736 | tf_op jit(solution)/shard_map/ppermute | solution.py:1236
  514.5 101.1 %all-reduce.3.cloned.1.call-start = ((), (), s32[]{:S(2)}) async-start(), calls=%async_computation.2 | async-start | bytes 1179648 | tf_op jit(solution)/shard_map/psum | solution.py:1502
  526.8 34.6 %collective-permute-start.42 = (bf16[768,384]{1,0:T(8,128)(2,1)}, bf16[768,384]{1,0:T(8,128)(2,1)}, u32[]{:S(2)}, u32[]{:S(2)}) collective-permute-start(bf16[768,384]{1,0:T(8,128)(2,1)} %get-tuple-element.302), channel_id=1, source_target_pairs={{0,1},{1,0},{2,3},{3,2},{4,5},{5,4},{6,7},{7,6},{8,9},{9,8},{10,11... | collective-permute-start | bytes 1769480 | tf_op jit(solution)/shard_map/ppermute | solution.py:1236
  527.4 34.1 %collective-permute-start.43 = (bf16[768,384]{1,0:T(8,128)(2,1)}, bf16[768,384]{1,0:T(8,128)(2,1)}, u32[]{:S(2)}, u32[]{:S(2)}) collective-permute-start(bf16[768,384]{1,0:T(8,128)(2,1)} %get-tuple-element.303), channel_id=1, source_target_pairs={{0,2},{1,3},{2,0},{3,1},{4,6},{5,7},{6,4},{7,5},{8,10},{9,11},{10,... | collective-permute-start | bytes 1769480 | tf_op jit(solution)/shard_map/ppermute | solution.py:1236
  571.8 43.8 %collective-permute-start.49 = (bf16[4,128,768]{2,1,0:T(8,128)(2,1)}, bf16[4,128,768]{2,1,0:T(8,128)(2,1)}, u32[]{:S(2)}, u32[]{:S(2)}) collective-permute-start(bf16[4,128,768]{2,1,0:T(8,128)(2,1)} %get-tuple-element.343), channel_id=1, source_target_pairs={{0,2},{1,3},{2,6},{3,7},{4,0},{5,1},{6,4},{7,5},{8,10},{9,11},{10,... | collective-permute-start | bytes 2359304 | tf_op jit(solution)/shard_map/ppermute | solution.py:1236
  572.4 43.2 %collective-permute-start.50 = (bf16[4,128,768]{2,1,0:T(8,128)(2,1)}, bf16[4,128,768]{2,1,0:T(8,128)(2,1)}, u32[]{:S(2)}, u32[]{:S(2)}) collective-permute-start(bf16[4,128,768]{2,1,0:T(8,128)(2,1)} %get-tuple-element.344), channel_id=1, source_target_pairs={{0,1},{1,0},{2,5},{3,4},{4,3},{5,2},{6,7},{7,6},{8,9},{9,8},{10,13... | collective-permute-start | bytes 2359304 | tf_op jit(solution)/shard_map/ppermute | solution.py:1236
  573.7 38.1 %collective-permute-start.46 = (bf16[288,384]{1,0:T(8,128)(2,1)S(1)}, bf16[288,384]{1,0:T(8,128)(2,1)S(1)}, u32[]{:S(2)}, u32[]{:S(2)}) collective-permute-start(bf16[288,384]{1,0:T(8,128)(2,1)S(1)} %get-tuple-element.326), channel_id=1, source_target_pairs={{0,1},{1,0},{2,3},{3,2},{4,5},{5,4},{6,7},{7,6},{8,9},{9,8},{10,11... | collective-permute-start | bytes 663560 | tf_op jit(solution)/shard_map/ppermute | solution.py:1236
  574.4 38.1 %collective-permute-start.47 = (bf16[288,384]{1,0:T(8,128)(2,1)S(1)}, bf16[288,384]{1,0:T(8,128)(2,1)S(1)}, u32[]{:S(2)}, u32[]{:S(2)}) collective-permute-start(bf16[288,384]{1,0:T(8,128)(2,1)S(1)} %get-tuple-element.327), channel_id=1, source_target_pairs={{0,2},{1,3},{2,0},{3,1},{4,6},{5,7},{6,4},{7,5},{8,10},{9,11},{10,... | collective-permute-start | bytes 663560 | tf_op jit(solution)/shard_map/ppermute | solution.py:1236
  575.4 40.2 %collective-permute-start.48 = (bf16[288,384]{1,0:T(8,128)(2,1)}, bf16[288,384]{1,0:T(8,128)(2,1)}, u32[]{:S(2)}, u32[]{:S(2)}) collective-permute-start(bf16[288,384]{1,0:T(8,128)(2,1)} %get-tuple-element.328), channel_id=1, source_target_pairs={{0,3},{1,2},{2,1},{3,0},{4,7},{5,6},{6,5},{7,4},{8,11},{9,10},{10,... | collective-permute-start | bytes 663560 | tf_op jit(solution)/shard_map/ppermute | solution.py:1236
  (116 other events, 1336.8 us)
Sparse Core Ops, SparseCore 0:
  14.7 33.7 all-gather.6
  119.3 97.5 all-gather.8
  364.5 89.7 reduce-scatter.1
  514.6 31.7 all-gather.10
  567.3 39.2 all-reduce.2
